TPU v7x, 32 devices: a whole 2x2x4 slice. The times are simulated.
32 devices in a mesh: replica: 2 (over x), shard: 4 (over y, core), seq: 4 (over z).
Axes of the slice: x: 2, y: 2, z: 4, core: 2. Of those that a mesh axis runs over, the one named last changes fastest.
Arguments:
- states: float32 [6240, 1536], P(('replica', 'shard', 'seq')), may hold values from -6 to 6
- text_emb: bfloat16 [4096, 1536], P(('replica', 'shard', 'seq')), may hold values from -6 to 6
- grid_pos: int32 [3, 6240], P(None, ('replica', 'shard', 'seq')), may hold values from 0 to 63
- time_mod: float32 [8, 6, 1536], P(('replica', 'shard')), may hold values from -4 to 4
- w_qkv: bfloat16 [1536, 3, 1536], P(('shard', 'seq')), may hold values from -0.15625 to 0.15625
- w_out: bfloat16 [1536, 1536], P(('shard', 'seq')), may hold values from -2.5 to 2.5
- w_cross: bfloat16 [1536, 3, 1536], P(('shard', 'seq')), may hold values from -0.15625 to 0.15625
- w_crossout: bfloat16 [1536, 1536], P(('shard', 'seq')), may hold values from -2.5 to 2.5
- w_up: bfloat16 [1536, 8960], P(('shard', 'seq')), may hold values from -0.15625 to 0.15625
- w_down: bfloat16 [8960, 1536], P(('shard', 'seq')), may hold values from -0.0625 to 0.0625
- attn_bias: float32 [8, 1536], replicated, may hold values from -2 to 2
- qk_gain: float32 [4, 1536], replicated, may hold values from 0.5 to 1.5
- norm_gain: float32 [1536], replicated, may hold values from 0.5 to 1.5
- norm_bias: float32 [1536], replicated, may hold values from -2 to 2
- up_bias: float32 [8960], replicated, may hold values from -2 to 2
- down_bias: float32 [1536], replicated, may hold values from -2 to 2
- modulation: float32 [6, 1536], replicated, may hold values from -4 to 4
- out_grad: float32 [6240, 1536], P(('replica', 'shard', 'seq')), may hold values from -6 to 6
Outputs:
- block_out: float32 [6240, 1536], P(('replica', 'shard', 'seq'))
- states_grad: float32 [6240, 1536], P(('replica', 'shard', 'seq'))
- text_grad: float32 [4096, 1536], P(('replica', 'shard', 'seq'))
- time_grad: float32 [8, 6, 1536], P(('replica', 'shard'))
- qkv_grad: float32 [1536, 3, 1536], P(('shard', 'seq'))
- outproj_grad: float32 [1536, 1536], P(('shard', 'seq'))
- crossqkv_grad: float32 [1536, 3, 1536], P(('shard', 'seq'))
- crossout_grad: float32 [1536, 1536], P(('shard', 'seq'))
- up_grad: float32 [1536, 8960], P(('shard', 'seq'))
- down_grad: float32 [8960, 1536], P(('shard', 'seq'))
- bias_grad: float32 [8, 1536], replicated
- gain_grad: float32 [4, 1536], replicated
- lngain_grad: float32 [1536], replicated
- lnbias_grad: float32 [1536], replicated
- upbias_grad: float32 [8960], replicated
- downbias_grad: float32 [1536], replicated
- mod_grad: float32 [6, 1536], replicated
All inputs are finite; a program needn't handle non-finite values.
Results may differ from a plain program's by a relative error of at most 0.02.
Values may be sent and summed in bfloat16 or wider, within the bound.
A program may use at most 448 MiB of HBM per device.

v0:
```python
from functools import partial
import math

import jax
import jax.numpy as jnp
import numpy as np
from jax import lax
from jax.sharding import PartitionSpec as P

HEADS = 12
HD = 128
TEXT = 512
LEN = 780
CLIPS = 1


EPS = 1e-06


def rope_tables(grid_pos):
    pair_count = HD // 2
    third_part = pair_count // 3
    first_part = pair_count - 2 * third_part
    pair_index = np.arange(pair_count)
    part_of = np.where(
        pair_index < first_part, 0, np.where(pair_index < first_part + third_part, 1, 2)
    )
    offset = np.where(
        part_of == 0,
        pair_index,
        np.where(part_of == 1, pair_index - first_part, pair_index - first_part - third_part),
    )
    part_width = np.where(part_of == 0, first_part, third_part)
    frequency = 10000.0 ** (-offset / part_width)
    positions = grid_pos.astype(jnp.float32)
    angles = positions[0][:, None] * jnp.asarray(frequency * (part_of == 0), jnp.float32)[None, :]
    angles = (
        angles
        + positions[1][:, None] * jnp.asarray(frequency * (part_of == 1), jnp.float32)[None, :]
    )
    angles = (
        angles
        + positions[2][:, None] * jnp.asarray(frequency * (part_of == 2), jnp.float32)[None, :]
    )
    return (jnp.cos(angles), jnp.sin(angles))


def layer_norm(values):
    center = values - jnp.mean(values, -1, keepdims=True)
    inverse = lax.rsqrt(jnp.mean(center * center, -1, keepdims=True) + EPS)
    return (center * inverse, inverse)


def norm_backward(normed, inverse, grad_in):
    return inverse * (
        grad_in
        - jnp.mean(grad_in, -1, keepdims=True)
        - normed * jnp.mean(grad_in * normed, -1, keepdims=True)
    )


def rms_norm(values, gain):
    return values * lax.rsqrt(jnp.mean(values * values, -1, keepdims=True) + EPS) * gain


def rotate(values, cosine_tab, sine_tab):
    row_count = values.shape[0]
    paired = values.reshape(row_count, HEADS, HD // 2, 2)
    even_part = paired[..., 0]
    odd_part = paired[..., 1]
    cosine = cosine_tab[:, None, :]
    sine_val = sine_tab[:, None, :]
    turned = jnp.stack(
        [even_part * cosine - odd_part * sine_val, even_part * sine_val + odd_part * cosine], -1
    )
    return turned.reshape(row_count, HEADS * HD)


def head_scores(q_heads, k_heads, same_clip, scale_val):
    scores = (
        jnp.einsum("qhd,khd->hqk", q_heads, k_heads, preferred_element_type=jnp.float32) * scale_val
    )
    if same_clip is not None:
        scores = jnp.where(same_clip[None], scores, -1e30)
    return scores


def attend_forward(q_heads, k_heads, v_heads, same_clip, scale_val):
    scores = head_scores(q_heads, k_heads, same_clip, scale_val)
    row_max = jnp.max(scores, -1, keepdims=True)
    exp_vals = jnp.exp(scores - row_max)
    row_total = jnp.sum(exp_vals, -1, keepdims=True)
    attn_probs = exp_vals / row_total
    mixed = jnp.einsum(
        "hqk,khd->qhd", attn_probs.astype(jnp.bfloat16), v_heads, preferred_element_type=jnp.float32
    )
    return (mixed.astype(jnp.bfloat16), (row_max + jnp.log(row_total))[..., 0])


def attend_backward(q_heads, k_heads, v_heads, grad_mix, log_total, same_clip, scale_val):
    scores = head_scores(q_heads, k_heads, same_clip, scale_val)
    attn_probs = jnp.exp(scores - log_total[..., None])
    grad_probs = jnp.einsum("qhd,khd->hqk", grad_mix, v_heads, preferred_element_type=jnp.float32)
    row_delta = jnp.sum(attn_probs * grad_probs, -1, keepdims=True)
    grad_scores = (attn_probs * (grad_probs - row_delta)).astype(jnp.bfloat16)
    grad_query = (
        jnp.einsum("hqk,khd->qhd", grad_scores, k_heads, preferred_element_type=jnp.float32)
        * scale_val
    )
    grad_key = (
        jnp.einsum("hqk,qhd->khd", grad_scores, q_heads, preferred_element_type=jnp.float32)
        * scale_val
    )
    grad_value = jnp.einsum(
        "hqk,qhd->khd",
        attn_probs.astype(jnp.bfloat16),
        grad_mix,
        preferred_element_type=jnp.float32,
    )
    return (grad_query, grad_key, grad_value)


def fetch_pair(first_w, second_w):
    return (
        lax.all_gather(first_w, ("shard", "seq"), axis=0, tiled=True),
        lax.all_gather(second_w, ("shard", "seq"), axis=0, tiled=True),
    )


def refetch_pair(first_w, second_w):
    return (
        lax.all_gather(first_w, ("shard", "seq"), axis=0, tiled=True),
        lax.all_gather(second_w, ("shard", "seq"), axis=0, tiled=True),
    )


def rows_product(left_rows, right_rows, row_start, row_span):
    sliced = lax.dynamic_slice_in_dim(left_rows, row_start, row_span, 1)
    return lax.dot_general(
        sliced, right_rows, (((0,), (0,)), ((), ())), preferred_element_type=jnp.float32
    )


def scattered_term(term_fn, shard_rows):
    return lax.psum_scatter(
        term_fn(jnp.int32(0), shard_rows * lax.axis_size(("shard", "seq"))).astype(jnp.bfloat16),
        ("shard", "seq"),
        scatter_dimension=0,
        tiled=True,
    ).astype(jnp.float32)


def over_replicas(shard_sum):
    return lax.psum(shard_sum.astype(jnp.bfloat16), "replica").astype(jnp.float32)


def weight_rows(left_rows, right_rows, shard_rows):
    shard_sum = scattered_term(
        lambda row_start, row_span: rows_product(left_rows, right_rows, row_start, row_span),
        shard_rows,
    )
    return over_replicas(shard_sum)


def times_transpose(left_rows, weight_mat):
    return lax.dot_general(
        left_rows, weight_mat, (((1,), (1,)), ((), ())), preferred_element_type=jnp.float32
    )


def on_device(
    states,
    text_emb,
    grid_pos,
    time_mod,
    w_qkv,
    w_out,
    w_cross,
    w_crossout,
    w_up,
    w_down,
    attn_bias,
    qk_gain,
    norm_gain,
    norm_bias,
    up_bias,
    down_bias,
    modulation,
    out_grad,
):
    row_count = states.shape[0]
    model_dim = states.shape[1]
    scale_val = 1.0 / math.sqrt(HD)
    seq_index = lax.axis_index("seq")
    token_ids = seq_index * row_count + jnp.arange(row_count, dtype=jnp.int32)
    clip_hot = (token_ids[:, None] // LEN == jnp.arange(CLIPS, dtype=jnp.int32)[None, :]).astype(
        jnp.float32
    )
    mod_sum = modulation[None] + time_mod
    token_mod = jnp.sum(clip_hot[:, :, None, None] * mod_sum[None], 1)
    cosine_tab, sine_tab = rope_tables(grid_pos)
    head_shape = (row_count, HEADS, HD)

    def prepare_pair(query_in, key_in, gain_query, gain_key):
        return (
            rotate(rms_norm(query_in, gain_query), cosine_tab, sine_tab),
            rotate(rms_norm(key_in, gain_key), cosine_tab, sine_tab),
        )

    full_qkv, full_out = fetch_pair(w_qkv, w_out)
    self_normed, self_inverse = layer_norm(states)
    self_in = (self_normed * (1.0 + token_mod[:, 1]) + token_mod[:, 0]).astype(jnp.bfloat16)
    project = (
        jnp.einsum("td,dkf->tkf", self_in, full_qkv, preferred_element_type=jnp.float32)
        + attn_bias[:3][None]
    )
    query_pre = project[:, 0]
    key_pre = project[:, 1]
    value_rows = project[:, 2].astype(jnp.bfloat16)
    (queries, key_rows), prep_pull = jax.vjp(
        prepare_pair, query_pre, key_pre, qk_gain[0], qk_gain[1]
    )
    q_heads, k_heads, v_heads = (
        lax.all_to_all(
            queries.astype(jnp.bfloat16).reshape(head_shape),
            "seq",
            split_axis=1,
            concat_axis=0,
            tiled=True,
        ),
        lax.all_to_all(
            key_rows.astype(jnp.bfloat16).reshape(head_shape),
            "seq",
            split_axis=1,
            concat_axis=0,
            tiled=True,
        ),
        lax.all_to_all(
            value_rows.reshape(head_shape), "seq", split_axis=1, concat_axis=0, tiled=True
        ),
    )
    local_heads = q_heads.shape[1]
    clip_shape = (CLIPS, LEN, local_heads, HD)
    clip_q = q_heads.reshape(clip_shape)
    clip_k = k_heads.reshape(clip_shape)
    clip_v = v_heads.reshape(clip_shape)

    def self_clip(clip_items):
        return attend_forward(clip_items[0], clip_items[1], clip_items[2], None, scale_val)

    mixed_heads, self_lse = lax.map(self_clip, (clip_q, clip_k, clip_v))
    mixed_tok = lax.all_to_all(
        mixed_heads.reshape(CLIPS * LEN, local_heads, HD),
        "seq",
        split_axis=0,
        concat_axis=1,
        tiled=True,
    ).reshape(row_count, model_dim)
    branch = jnp.dot(mixed_tok, full_out, preferred_element_type=jnp.float32) + attn_bias[3]
    after_self = states + branch * token_mod[:, 2]
    full_cross, full_crossout = fetch_pair(w_cross, w_crossout)
    cross_normed, cross_inverse = layer_norm(after_self)
    cross_in = (cross_normed * norm_gain + norm_bias).astype(jnp.bfloat16)
    cq_pre = jnp.dot(cross_in, full_cross[:, 0], preferred_element_type=jnp.float32) + attn_bias[4]
    text_proj = (
        jnp.einsum("td,dkf->tkf", text_emb, full_cross[:, 1:], preferred_element_type=jnp.float32)
        + attn_bias[5:7][None]
    )
    ck_pre = text_proj[:, 0]
    cross_qf, cq_pull = jax.vjp(rms_norm, cq_pre, qk_gain[2])
    cross_kf, ck_pull = jax.vjp(rms_norm, ck_pre, qk_gain[3])
    cross_q = cross_qf.astype(jnp.bfloat16).reshape(head_shape)
    cross_k = cross_kf.astype(jnp.bfloat16)
    cross_v = text_proj[:, 1].astype(jnp.bfloat16)
    all_keys, all_values = (
        lax.all_gather(cross_k, "seq", axis=0, tiled=True),
        lax.all_gather(cross_v, "seq", axis=0, tiled=True),
    )
    text_total = all_keys.shape[0]
    all_keys = all_keys.reshape(text_total, HEADS, HD)
    all_values = all_values.reshape(text_total, HEADS, HD)
    text_clip = jnp.arange(text_total, dtype=jnp.int32) // TEXT
    same_clip = token_ids[:, None] // LEN == text_clip[None, :]
    cross_mix, cross_lse = attend_forward(cross_q, all_keys, all_values, same_clip, scale_val)
    cross_mix = cross_mix.reshape(row_count, model_dim)
    cross_out = jnp.dot(cross_mix, full_crossout, preferred_element_type=jnp.float32) + attn_bias[7]
    after_cross = after_self + cross_out
    full_up, full_down = fetch_pair(w_up, w_down)
    ffn_normed, ffn_inverse = layer_norm(after_cross)
    ffn_in = (ffn_normed * (1.0 + token_mod[:, 4]) + token_mod[:, 3]).astype(jnp.bfloat16)
    hidden_pre = jnp.dot(ffn_in, full_up, preferred_element_type=jnp.float32) + up_bias
    hidden, gelu_pull = jax.vjp(partial(jax.nn.gelu, approximate=True), hidden_pre)
    hidden_low = hidden.astype(jnp.bfloat16)
    ffn_out = jnp.dot(hidden_low, full_down, preferred_element_type=jnp.float32) + down_bias
    block_out = after_cross + ffn_out * token_mod[:, 5]
    back_up, back_down = refetch_pair(w_up, w_down)
    grad_gate2 = out_grad * ffn_out
    d_ffnout = (out_grad * token_mod[:, 5]).astype(jnp.bfloat16)
    d_hidden = times_transpose(d_ffnout, back_down)
    (d_hpre,) = gelu_pull(d_hidden)
    d_hpre_low = d_hpre.astype(jnp.bfloat16)
    d_ffnin = times_transpose(d_hpre_low, back_up)
    grad_scale2 = d_ffnin * ffn_normed
    d_cross = out_grad + norm_backward(ffn_normed, ffn_inverse, d_ffnin * (1.0 + token_mod[:, 4]))
    up_shard = weight_rows(ffn_in, d_hpre_low, w_up.shape[0])
    down_shard = weight_rows(hidden_low, d_ffnout, w_down.shape[0])
    back_cross, back_crossout = refetch_pair(w_cross, w_crossout)
    d_crossout = d_cross.astype(jnp.bfloat16)
    d_cmix = times_transpose(d_crossout, back_crossout).astype(jnp.bfloat16)
    grad_cq, grad_ck_all, grad_cv_all = attend_backward(
        cross_q, all_keys, all_values, d_cmix.reshape(head_shape), cross_lse, same_clip, scale_val
    )
    grad_ck, grad_cv = (
        lax.psum_scatter(
            grad_ck_all.astype(jnp.bfloat16), "seq", scatter_dimension=0, tiled=True
        ).astype(jnp.float32),
        lax.psum_scatter(
            grad_cv_all.astype(jnp.bfloat16), "seq", scatter_dimension=0, tiled=True
        ).astype(jnp.float32),
    )
    text_rows = grad_ck.shape[0]
    d_cv = grad_cv.reshape(text_rows, model_dim).astype(jnp.bfloat16)
    d_ck_full, ck_gain = ck_pull(grad_ck.reshape(text_rows, model_dim))
    d_ck = d_ck_full.astype(jnp.bfloat16)
    d_cq_full, cq_gain = cq_pull(grad_cq.reshape(row_count, model_dim))
    d_cq = d_cq_full.astype(jnp.bfloat16)
    text_grad = times_transpose(d_ck, back_cross[:, 1]) + times_transpose(d_cv, back_cross[:, 2])
    d_crossin = times_transpose(d_cq, back_cross[:, 0])
    lngain_local = jnp.sum(d_crossin * cross_normed, 0)
    lnbias_local = jnp.sum(d_crossin, 0)
    d_self = d_cross + norm_backward(cross_normed, cross_inverse, d_crossin * norm_gain)

    def cross_term(row_start, row_span):
        return jnp.stack(
            [
                rows_product(cross_in, d_cq, row_start, row_span),
                rows_product(text_emb, d_ck, row_start, row_span),
                rows_product(text_emb, d_cv, row_start, row_span),
            ],
            1,
        )

    cross_rows = w_cross.shape[0]
    cross_sum = scattered_term(cross_term, cross_rows)
    cross_shard = over_replicas(cross_sum)
    crossout_shard = weight_rows(cross_mix, d_crossout, w_crossout.shape[0])
    back_qkv, back_out = refetch_pair(w_qkv, w_out)
    grad_gate1 = d_self * branch
    d_branch = (d_self * token_mod[:, 2]).astype(jnp.bfloat16)
    d_mix = times_transpose(d_branch, back_out).astype(jnp.bfloat16).reshape(head_shape)
    d_mix_heads = lax.all_to_all(d_mix, "seq", split_axis=1, concat_axis=0, tiled=True)

    def self_back(clip_items):
        grad_query, grad_key, grad_value = attend_backward(
            clip_items[0],
            clip_items[1],
            clip_items[2],
            clip_items[3],
            clip_items[4],
            None,
            scale_val,
        )
        return (
            grad_query.astype(jnp.bfloat16),
            grad_key.astype(jnp.bfloat16),
            grad_value.astype(jnp.bfloat16),
        )

    dq_heads, dk_heads, dv_heads = lax.map(
        self_back, (clip_q, clip_k, clip_v, d_mix_heads.reshape(clip_shape), self_lse)
    )
    flat_shape = (CLIPS * LEN, local_heads, HD)
    dq_tok, dk_tok, dv_tok = (
        lax.all_to_all(
            dq_heads.reshape(flat_shape), "seq", split_axis=0, concat_axis=1, tiled=True
        ),
        lax.all_to_all(
            dk_heads.reshape(flat_shape), "seq", split_axis=0, concat_axis=1, tiled=True
        ),
        lax.all_to_all(
            dv_heads.reshape(flat_shape), "seq", split_axis=0, concat_axis=1, tiled=True
        ),
    )
    dq_pre, dk_pre, query_gain, key_gain = prep_pull(
        (
            dq_tok.reshape(row_count, model_dim).astype(jnp.float32),
            dk_tok.reshape(row_count, model_dim).astype(jnp.float32),
        )
    )
    d_values = dv_tok.reshape(row_count, model_dim)
    d_qkv = jnp.stack([dq_pre.astype(jnp.bfloat16), dk_pre.astype(jnp.bfloat16), d_values], 1)
    d_selfin = jnp.einsum("tkf,dkf->td", d_qkv, back_qkv, preferred_element_type=jnp.float32)
    grad_scale1 = d_selfin * self_normed
    states_grad = d_self + norm_backward(
        self_normed, self_inverse, d_selfin * (1.0 + token_mod[:, 1])
    )
    qkv_shard = weight_rows(self_in, d_qkv, w_qkv.shape[0])
    outproj_shard = weight_rows(mixed_tok, d_branch, w_out.shape[0])
    token_modgrad = jnp.stack(
        [d_selfin, grad_scale1, grad_gate1, d_ffnin, grad_scale2, grad_gate2], 1
    )
    clip_part = jnp.sum(clip_hot[:, :, None, None] * token_modgrad[:, None], 0)
    time_grad = lax.psum(clip_part.astype(jnp.bfloat16), "seq").astype(jnp.float32)
    mod_local = jnp.sum(token_modgrad, 0)
    bias_local = jnp.stack(
        [
            jnp.sum(d_qkv[:, 0].astype(jnp.float32), 0),
            jnp.sum(d_qkv[:, 1].astype(jnp.float32), 0),
            jnp.sum(d_values.astype(jnp.float32), 0),
            jnp.sum(d_branch.astype(jnp.float32), 0),
            jnp.sum(d_cq.astype(jnp.float32), 0),
            jnp.sum(d_ck.astype(jnp.float32), 0),
            jnp.sum(d_cv.astype(jnp.float32), 0),
            jnp.sum(d_crossout.astype(jnp.float32), 0),
        ],
        0,
    )
    gain_local = jnp.stack([query_gain, key_gain, cq_gain, ck_gain], 0)
    upbias_local = jnp.sum(d_hpre_low.astype(jnp.float32), 0)
    downbias_local = jnp.sum(d_ffnout.astype(jnp.float32), 0)
    bias_grad, gain_grad, lngain_grad, lnbias_grad, upbias_grad, downbias_grad, mod_grad = lax.psum(
        (
            bias_local,
            gain_local,
            lngain_local,
            lnbias_local,
            upbias_local,
            downbias_local,
            mod_local,
        ),
        ("replica", "shard", "seq"),
    )
    return (
        block_out,
        states_grad,
        text_grad,
        time_grad,
        qkv_shard,
        outproj_shard,
        cross_shard,
        crossout_shard,
        up_shard,
        down_shard,
        bias_grad,
        gain_grad,
        lngain_grad,
        lnbias_grad,
        upbias_grad,
        downbias_grad,
        mod_grad,
    )


def solution(mesh):
    placed = (
        P(("replica", "shard", "seq"), None),
        P(("replica", "shard", "seq"), None),
        P(None, ("replica", "shard", "seq")),
        P(("replica", "shard"), None, None),
        P(("shard", "seq"), None, None),
        P(("shard", "seq"), None),
        P(("shard", "seq"), None, None),
        P(("shard", "seq"), None),
        P(("shard", "seq"), None),
        P(("shard", "seq"), None),
        P(),
        P(),
        P(),
        P(),
        P(),
        P(),
        P(),
        P(("replica", "shard", "seq"), None),
    )
    return jax.shard_map(
        on_device,
        mesh=mesh,
        in_specs=placed,
        out_specs=(
            P(("replica", "shard", "seq"), None),
            P(("replica", "shard", "seq"), None),
            P(("replica", "shard", "seq"), None),
            P(("replica", "shard"), None, None),
            P(("shard", "seq"), None, None),
            P(("shard", "seq"), None),
            P(("shard", "seq"), None, None),
            P(("shard", "seq"), None),
            P(("shard", "seq"), None),
            P(("shard", "seq"), None),
            P(),
            P(),
            P(),
            P(),
            P(),
            P(),
            P(),
        ),
        check_vma=False,
    )
```

profile of v0, /device:TPU:0, one launch (start us, length us, event | category | flops | bytes accessed | tf_op | source)
XLA Modules:
  0.0 2205.3 jit_solution(17645621579745134475)
XLA Ops:
  10.2 113.1 %all-gather.14.cloned.1.call-done = bf16[1536,3,1536]{2,0,1:T(8,128)(2,1)} async-done(((bf16[96,3,1536]{2,0,1:T(8,128)(2,1)}), bf16[1536,3,1536]{2,0,1:T(8,128)(2,1)}) %all-gather.14.cloned.1.call-update) | async-done | bytes 14155792 | tf_op jit(solution)/shard_map/all_gather | solution.py:125
  123.3 5.1 fusion.25
  140.8 93.2 %all-gather.10.cloned.1.call-done = bf16[1536,3,1536]{2,0,1:T(8,128)(2,1)} async-done(((bf16[96,3,1536]{2,0,1:T(8,128)(2,1)}), bf16[1536,3,1536]{2,0,1:T(8,128)(2,1)}) %all-gather.10.cloned.1.call-update) | async-done | bytes 14155792 | tf_op jit(solution)/shard_map/all_gather | solution.py:125
  234.0 6.8 convolution_add_fusion.1
  258.4 4.1 subtract_convert_fusion
  270.6 4.6 all-to-all-start.2
  281.3 17.4 all-to-all-done.2
  306.9 26.1 %all-to-all-done.1 = bf16[195,12,128]{2,0,1:T(8,128)(2,1)S(1)} async-done(((bf16[195,12,128]{2,0,1:T(8,128)(2,1)}), bf16[195,12,128]{2,0,1:T(8,128)(2,1)S(1)}, u32[]{:S(2)}, u32[]{:S(2)}) %all-to-all-start.1) | async-done | bytes 599072 | tf_op jit(solution)/shard_map/all_to_all | solution.py:224
  333.0 4.2 all-to-all-start
  342.6 14.5 all-to-all-done
  372.1 36.9 %all-to-all-done.3 = bf16[780,3,128]{2,1,0:T(4,128)(2,1)S(1)} async-done(((bf16[780,3,128]{2,1,0:T(4,128)(2,1)}), bf16[780,3,128]{2,1,0:T(4,128)(2,1)S(1)}, u32[]{:S(2)}, u32[]{:S(2)}) %all-to-all-start.3) | async-done | bytes 599072 | tf_op jit(solution)/shard_map/all_to_all | solution.py:252
  410.1 5.1 fusion.110
  434.1 29.4 %all-gather.18.cloned.1.call-done = bf16[1536,1536]{1,0:T(8,128)(2,1)} async-done(((bf16[96,1536]{1,0:T(8,128)(2,1)}), bf16[1536,1536]{1,0:T(8,128)(2,1)}) %all-gather.18.cloned.1.call-update) | async-done | bytes 4718608 | tf_op jit(solution)/shard_map/all_gather | solution.py:126
  472.3 138.9 %all-gather.22.cloned.1.call-done = bf16[8960,1536]{1,0:T(8,128)(2,1)} async-done(((bf16[560,1536]{1,0:T(8,128)(2,1)}), bf16[8960,1536]{1,0:T(8,128)(2,1)}) %all-gather.22.cloned.1.call-update) | async-done | bytes 27525136 | tf_op jit(solution)/shard_map/all_gather | solution.py:126
  611.2 17.0 fusion.115
  628.1 132.2 %all-gather.20.cloned.1.call-done = bf16[1536,8960]{1,0:T(8,128)(2,1)} async-done(((bf16[96,8960]{1,0:T(8,128)(2,1)}), bf16[1536,8960]{1,0:T(8,128)(2,1)}) %all-gather.20.cloned.1.call-update) | async-done | bytes 27525136 | tf_op jit(solution)/shard_map/all_gather | solution.py:125
  760.3 19.4 convert_reduce_fusion
  779.7 15.0 fusion.105
  794.7 21.4 convert_reduce_fusion.4
  816.1 5.3 convolution_convert_fusion.9
  823.7 4.5 multiply_reduce_fusion.3
  850.9 4.9 multiply_reduce_fusion.6
  862.9 4.6 all-to-all-start.4
  871.4 24.1 %all-to-all-done.4 = bf16[195,12,128]{2,0,1:T(8,128)(2,1)S(1)} async-done(((bf16[195,12,128]{2,0,1:T(8,128)(2,1)}), bf16[195,12,128]{2,0,1:T(8,128)(2,1)S(1)}, u32[]{:S(2)}, u32[]{:S(2)}) %all-to-all-start.4) | async-done | bytes 599072 | tf_op jit(solution)/shard_map/all_to_all | solution.py:351
  897.6 5.7 multiply_reduce_fusion
  909.1 4.2 all-to-all-start.6
  918.5 9.7 all-to-all-done.6
  928.2 4.2 all-to-all-start.5
  932.4 4.8 fusion.51
  946.9 17.4 all-to-all-done.5
  964.4 4.2 all-to-all-start.7
  977.3 6.4 multiply_add_fusion.8
  1025.3 7.2 convolution_convert_fusion.2
  1044.6 6.3 pad_maximum_fusion
  1052.0 15.2 convolution_convert_fusion.1
  1068.3 16.1 convolution_convert_fusion
  1089.4 13.3 fusion.106
  1112.2 5.4 reduce_sum.457
  1117.6 6.9 multiply_reduce_fusion.4
  1125.8 6.6 multiply_reduce_fusion.5
  1136.2 87.5 %reduce-scatter.13.cloned.1.call-done = bf16[96,3,1536]{2,0,1:T(8,128)(2,1)} async-done(((bf16[1536,3,1536]{2,0,1:T(8,128)(2,1)}), bf16[96,3,1536]{2,0,1:T(8,128)(2,1)}) %reduce-scatter.13.cloned.1.call-update) | async-done | bytes 884752 | tf_op jit(solution)/shard_map/reduce_scatter | solution.py:145
  1223.7 149.0 %reduce-scatter.17.cloned.1.call-done = bf16[96,3,1536]{2,0,1:T(8,128)(2,1)} async-done(((bf16[1536,3,1536]{2,0,1:T(8,128)(2,1)}), bf16[96,3,1536]{2,0,1:T(8,128)(2,1)}) %reduce-scatter.17.cloned.1.call-update) | async-done | bytes 884752 | tf_op jit(solution)/shard_map/reduce_scatter | solution.py:145
  1372.7 267.9 %reduce-scatter.21.cloned.1.call-done = bf16[96,8960]{1,0:T(8,128)(2,1)} async-done(((bf16[1536,8960]{1,0:T(8,128)(2,1)}), bf16[96,8960]{1,0:T(8,128)(2,1)}) %reduce-scatter.21.cloned.1.call-update) | async-done | bytes 1720336 | tf_op jit(solution)/shard_map/reduce_scatter | solution.py:145
  1640.6 267.8 %reduce-scatter.23.cloned.1.call-done = bf16[560,1536]{1,0:T(8,128)(2,1)} async-done(((bf16[8960,1536]{1,0:T(8,128)(2,1)}), bf16[560,1536]{1,0:T(8,128)(2,1)}) %reduce-scatter.23.cloned.1.call-update) | async-done | bytes 1720336 | tf_op jit(solution)/shard_map/reduce_scatter | solution.py:145
  1916.6 17.2 psum.98
  1944.8 4.9 fusion.30
  1949.7 103.4 %all-reduce.11.cloned.1.call-done = (bf16[96,3,1536]{2,0,1:T(8,128)(2,1)}, bf16[96,1536]{1,0:T(8,128)(2,1)}, bf16[96,3,1536]{2,0,1:T(8,128)(2,1)}, bf16[96,1536]...) async-done(((bf16[96,3,1536]{2,0,1:T(8,128)(2,1)}, bf16[96,1536]{1,0:T(8,128)(2,1)}, bf16[96,3,1536]{2,0,1:T(8,128)(2,1)}, ...) | async-done | bytes 5799952 | tf_op jit(solution)/shard_map/psum | solution.py:154
  2063.5 125.0 %all-reduce.9.cloned.1.call-done = (f32[8,1536]{1,0:T(8,128)}, f32[4,1536]{1,0:T(4,128)}, f32[1536]{0:T(1024)}, f32[1536]{0:T(1024)}, f32[8960]{0:T(1024)}, /*index=5*/f32[1536]{0:T(1024)}, f32[6,1536]{1,0:T(8,128)}) async-done(((f32[8,1536]{1,0:T(8,128)}, f32[4,1536]{1,0:T(4,128)}, f32[1536]{0:T(1024)}, f32[1536]{0:T(1024)}, f32[8960]{0:T(1024)}, /*index=5*/f32[1536]{0:T(1024)}, f32[6,1536]{1,0:T(8,128)}), ...) | async-done | bytes 164880 | tf_op jit(solution)/shard_map/psum | solution.py:421
  (532 shorter events, 284.5 us)
Async XLA Ops:
  7.2 116.1 %copy-start = (bf16[128,1536]{1,0:T(8,128)(2,1)S(1)}, bf16[128,1536]{1,0:T(8,128)(2,1)}, u32[]{:S(2)}) copy-start(bf16[128,1536]{1,0:T(8,128)(2,1)} %param.22) | copy-start | bytes 1179652
  7.2 116.0 %all-gather.14.cloned.1.call-start = ((), (), s32[]{:S(2)}) async-start(), calls=%async_computation.18 | async-start | bytes 15040512 | tf_op jit(solution)/shard_map/all_gather | solution.py:125
  8.0 226.0 %all-gather.10.cloned.1.call-start = ((), (), s32[]{:S(2)}) async-start(), calls=%async_computation.16 | async-start | bytes 15040512 | tf_op jit(solution)/shard_map/all_gather | solution.py:125
  8.7 401.4 %all-gather.12.cloned.1.call-start = ((), (), s32[]{:S(2)}) async-start(), calls=%async_computation.17 | async-start | bytes 5013504 | tf_op jit(solution)/shard_map/all_gather | solution.py:126
  9.4 411.8 %all-gather.16.cloned.1.call-start = ((), (), s32[]{:S(2)}) async-start(), calls=%async_computation.19 | async-start | bytes 1966080 | tf_op jit(solution)/shard_map/all_gather | solution.py:276
  10.2 118.4 %copy-start.78 = (f32[1536]{0:T(1024)}, f32[1536]{0:T(1024)S(1)}, u32[]{:S(2)}) copy-start(f32[1536]{0:T(1024)S(1)} %get-tuple-element.86) | copy-start | bytes 18436
  10.2 122.5 %copy-start.87 = (f32[1536]{0:T(1024)}, f32[1536]{0:T(1024)S(1)}, u32[]{:S(2)}) copy-start(f32[1536]{0:T(1024)S(1)} %get-tuple-element.85) | copy-start | bytes 18436
  10.2 123.7 %copy-start.85 = (f32[1536]{0:T(1024)}, f32[1536]{0:T(1024)S(1)}, u32[]{:S(2)}) copy-start(f32[1536]{0:T(1024)S(1)} %get-tuple-element.84) | copy-start | bytes 18436
  129.7 294.5 %all-gather.24.cloned.1.call-start = ((), (), s32[]{:S(2)}) async-start(), calls=%async_computation.29 | async-start | bytes 1966080 | tf_op jit(solution)/shard_map/all_gather | solution.py:277
  130.6 332.9 %all-gather.18.cloned.1.call-start = ((), (), s32[]{:S(2)}) async-start(), calls=%async_computation.20 | async-start | bytes 5013504 | tf_op jit(solution)/shard_map/all_gather | solution.py:126
  131.2 480.0 %all-gather.22.cloned.1.call-start = ((), (), s32[]{:S(2)}) async-start(), calls=%async_computation.22 | async-start | bytes 29245440 | tf_op jit(solution)/shard_map/all_gather | solution.py:126
  132.0 628.4 %all-gather.20.cloned.1.call-start = ((), (), s32[]{:S(2)}) async-start(), calls=%async_computation.21 | async-start | bytes 29245440 | tf_op jit(solution)/shard_map/all_gather | solution.py:125
  136.4 122.0 %copy-start.73 = (f32[195,64]{0,1:T(8,128)}, f32[195,64]{0,1:T(8,128)S(1)}, u32[]{:S(2)}) copy-start(f32[195,64]{0,1:T(8,128)S(1)} %get-tuple-element.136) | copy-start | bytes 149764
  140.4 93.5 %slice-start.9 = ((f32[8,1536]{1,0:T(8,128)}), f32[3,1536]{1,0:T(4,128)S(1)}, s32[]{:S(2)}) async-start(f32[8,1536]{1,0:T(8,128)} %param.31), calls=%async_computation.43 | async-start | bytes 49152 | tf_op jit(solution)/shard_map/slice | solution.py:215
  140.8 100.0 %copy-start.37 = (bf16[195,1536,1]{1,0,2:T(8,128)(2,1)}, bf16[195,1536,1]{1,0,2:T(8,128)(2,1)S(1)}, u32[]{:S(2)}) copy-start(bf16[195,1536,1]{1,0,2:T(8,128)(2,1)S(1)} %fusion.77) | copy-start | bytes 1797124
  246.9 8.5 copy-start.26
  270.6 28.1 %all-to-all-start.2 = ((bf16[195,12,128]{2,0,1:T(8,128)(2,1)}), bf16[195,12,128]{2,0,1:T(8,128)(2,1)}, u32[]{:S(2)}, u32[]{:S(2)}) async-start(bf16[195,12,128]{2,0,1:T(8,128)(2,1)} %copy.150), calls=%async_computation.2 | async-start | bytes 1228800 | tf_op jit(solution)/shard_map/all_to_all | solution.py:231
  298.7 34.3 %all-to-all-start.1 = ((bf16[195,12,128]{2,0,1:T(8,128)(2,1)}), bf16[195,12,128]{2,0,1:T(8,128)(2,1)S(1)}, u32[]{:S(2)}, u32[]{:S(2)}) async-start(bf16[195,12,128]{2,0,1:T(8,128)(2,1)} %copy.147), calls=%async_computation.1 | async-start | bytes 1228800 | tf_op jit(solution)/shard_map/all_to_all | solution.py:224
  333.0 24.0 %all-to-all-start = ((bf16[195,12,128]{2,0,1:T(8,128)(2,1)}), bf16[195,12,128]{2,0,1:T(8,128)(2,1)}, u32[]{:S(2)}, u32[]{:S(2)}) async-start(bf16[195,12,128]{2,0,1:T(8,128)(2,1)} %copy.144), calls=%async_computation | async-start | bytes 1228800 | tf_op jit(solution)/shard_map/all_to_all | solution.py:238
  340.4 18.8 copy-start.44
  342.6 18.1 copy-start.46
  367.5 41.5 %all-to-all-start.3 = ((bf16[780,3,128]{2,1,0:T(4,128)(2,1)}), bf16[780,3,128]{2,1,0:T(4,128)(2,1)S(1)}, u32[]{:S(2)}, u32[]{:S(2)}) async-start(bf16[780,3,128]{2,1,0:T(4,128)(2,1)} %copy.153), calls=%async_computation.3 | async-start | bytes 1597440 | tf_op jit(solution)/shard_map/all_to_all | solution.py:252
  371.0 666.7 %reduce-scatter.25.cloned.1.call-start = ((), (), s32[]{:S(2)}) async-start(), calls=%async_computation.30 | async-start | bytes 1966080
  415.3 48.2 %copy-start.21 = (f32[195,1536]{1,0:T(8,128)}, f32[195,1536]{1,0:T(8,128)S(1)}, u32[]{:S(2)}) copy-start(f32[195,1536]{1,0:T(8,128)S(1)} %get-tuple-element.116) | copy-start | bytes 3594244
  467.0 327.7 %copy-start.9 = (f32[195,1536]{1,0:T(8,128)}, f32[195,1536]{1,0:T(8,128)S(1)}, u32[]{:S(2)}) copy-start(f32[195,1536]{1,0:T(8,128)S(1)} %get-tuple-element.149) | copy-start | bytes 3594244
  472.3 155.9 %copy-start.59 = (bf16[195,1536]{1,0:T(8,128)(2,1)}, bf16[195,1536]{1,0:T(8,128)(2,1)S(1)}, u32[]{:S(2)}) copy-start(bf16[195,1536]{1,0:T(8,128)(2,1)S(1)} %get-tuple-element.101) | copy-start | bytes 1797124
  472.3 288.0 %copy-start.61 = (bf16[195,1536]{1,0:T(8,128)(2,1)}, bf16[195,1536]{1,0:T(8,128)(2,1)S(1)}, u32[]{:S(2)}) copy-start(bf16[195,1536]{1,0:T(8,128)(2,1)S(1)} %get-tuple-element.118) | copy-start | bytes 1797124
  760.3 19.4 copy-start.94
  760.3 19.4 copy-start.100
  779.7 15.0 copy-start.133
  794.7 21.4 copy-start.16
  832.4 208.1 %reduce-scatter.27.cloned.1.call-start = ((), (), s32[]{:S(2)}) async-start(), calls=%async_computation.31 | async-start | bytes 1966080 | tf_op jit(solution)/shard_map/convert_element_type | solution.py:322
  838.7 297.5 %reduce-scatter.19.cloned.1.call-start = ((), (), s32[]{:S(2)}) async-start(), calls=%async_computation.26 | async-start | bytes 5013504 | tf_op jit(solution)/shard_map/reduce_scatter | solution.py:145
  845.3 12.4 slice-start.7
  857.7 247.5 %copy-start.19 = (f32[195,1536]{1,0:T(8,128)}, f32[195,1536]{1,0:T(8,128)S(1)}, u32[]{:S(2)}) copy-start(f32[195,1536]{1,0:T(8,128)S(1)} %get-tuple-element.112) | copy-start | bytes 3594244
  862.9 32.6 %all-to-all-start.4 = ((bf16[195,12,128]{2,0,1:T(8,128)(2,1)}), bf16[195,12,128]{2,0,1:T(8,128)(2,1)S(1)}, u32[]{:S(2)}, u32[]{:S(2)}) async-start(bf16[195,12,128]{2,0,1:T(8,128)(2,1)} %copy.166), calls=%async_computation.4 | async-start | bytes 1228800 | tf_op jit(solution)/shard_map/all_to_all | solution.py:351
  867.5 268.7 %reduce-scatter.15.cloned.1.call-start = ((), (), s32[]{:S(2)}) async-start(), calls=%async_computation.24 | async-start | bytes 5013504 | tf_op jit(solution)/shard_map/reduce_scatter | solution.py:145
  909.1 19.1 all-to-all-start.6
  928.2 36.1 %all-to-all-start.5 = ((bf16[780,3,128]{2,1,0:T(4,128)(2,1)}), bf16[780,3,128]{2,1,0:T(4,128)(2,1)}, u32[]{:S(2)}, u32[]{:S(2)}) async-start(bf16[780,3,128]{2,1,0:T(4,128)(2,1)} %copy.169), calls=%async_computation.5 | async-start | bytes 1597440 | tf_op jit(solution)/shard_map/all_to_all | solution.py:374
  964.4 50.5 %all-to-all-start.7 = ((bf16[780,3,128]{2,1,0:T(4,128)(2,1)}), bf16[780,3,128]{2,1,0:T(4,128)(2,1)}, u32[]{:S(2)}, u32[]{:S(2)}) async-start(bf16[780,3,128]{2,1,0:T(4,128)(2,1)} %copy.179), calls=%async_computation.7 | async-start | bytes 1597440 | tf_op jit(solution)/shard_map/all_to_all | solution.py:380
  968.5 255.2 %reduce-scatter.13.cloned.1.call-start = ((), (), s32[]{:S(2)}) async-start(), calls=%async_computation.23 | async-start | bytes 15040512 | tf_op jit(solution)/shard_map/reduce_scatter | solution.py:145
  983.7 10.1 copy-start.41
  1032.5 340.2 %reduce-scatter.17.cloned.1.call-start = ((), (), s32[]{:S(2)}) async-start(), calls=%async_computation.25 | async-start | bytes 15040512 | tf_op jit(solution)/shard_map/reduce_scatter | solution.py:145
  1051.0 589.6 %reduce-scatter.21.cloned.1.call-start = ((), (), s32[]{:S(2)}) async-start(), calls=%async_computation.27 | async-start | bytes 29245440 | tf_op jit(solution)/shard_map/reduce_scatter | solution.py:145
  1067.2 841.2 %reduce-scatter.23.cloned.1.call-start = ((), (), s32[]{:S(2)}) async-start(), calls=%async_computation.28 | async-start | bytes 29245440 | tf_op jit(solution)/shard_map/reduce_scatter | solution.py:145
  1084.5 968.6 %all-reduce.11.cloned.1.call-start = ((), (), s32[]{:S(2)}) async-start(), calls=%async_computation.33 | async-start | bytes 11599872 | tf_op jit(solution)/shard_map/psum | solution.py:154
  1908.5 280.0 %all-reduce.9.cloned.1.call-start = ((), (), s32[]{:S(2)}) async-start(), calls=%async_computation.32 | async-start | bytes 368640 | tf_op jit(solution)/shard_map/psum | solution.py:421
  1915.6 19.0 copy-start.13
  (124 other events, 331.7 us)
Sparse Core Ops, SparseCore 0:
  10.4 112.8 all-gather.13
  125.6 108.2 all-gather.9
  236.3 58.7 all-gather.11
  297.1 58.2 all-gather.15
  356.7 52.7 all-gather.23
  411.7 51.7 all-gather.17
  465.0 146.1 all-gather.21
  612.7 147.5 all-gather.19
  832.5 35.4 reduce-scatter.24
  870.1 37.9 reduce-scatter.26
  912.0 84.1 reduce-scatter.18
  999.9 74.5 reduce-scatter.14
  1078.7 145.0 reduce-scatter.12
  1227.7 144.9 reduce-scatter.16
  1376.7 263.8 reduce-scatter.20
  1644.6 263.8 reduce-scatter.22
  1911.3 141.7 all-reduce.10
  2060.5 127.9 all-reduce.8
where the time goes:
time: 2210 us
  waiting for transfers between devices  1660 us (75%)
  matrix products  220 us (10%)
  local copies, waits for them, and re-layouts  156 us (7%)
  other arithmetic  103 us (5%)
  starting transfers between devices  34.6 us (2%)
    reduce_scatter x6, waiting for transfers between devices, scattered_term(): lax.psum_scatter(term_fn(jnp.int32(0), shard_rows * lax.axis_size(('shard...  772 us
    all_gather x3, waiting for transfers between devices, fetch_pair(): lax.all_gather(first_w, ('shard', 'seq'), axis=0, tiled=True)  338 us
    all_gather x3, waiting for transfers between devices, fetch_pair(): lax.all_gather(second_w, ('shard', 'seq'), axis=0, tiled=True)  168 us
    psum x1, waiting for transfers between devices, on_device(): lax.psum((bias_local, gain_local, lngain_local, lnbias_local, upbias_loca...  125 us
    psum x1, waiting for transfers between devices, over_replicas(): lax.psum(shard_sum.astype(jnp.bfloat16), 'replica').astype(jnp.float32)  103 us
    dot_general x8, matrix products, rows_product(): lax.dot_general(sliced, right_rows, (((0,), (0,)), ((), ())), preferred_e...  53.5 us
    dot_general x7, matrix products, times_transpose(): lax.dot_general(left_rows, weight_mat, (((1,), (1,)), ((), ())), preferre...  52.6 us
    unnamed x309, local copies, waits for them, and re-layouts  50 us
  transfers between devices with their start and end apart: 26, of which 18 were waited for; matrix products, arithmetic and copies ran while one was open for 17% of the time, Pallas kernels for 0%

commit v1 on v0

v1 whole, which is shorter than its diff:
```python
import math

import jax
import jax.numpy as jnp
import numpy as np
from jax import lax
from jax.sharding import Mesh, PartitionSpec as P

HD = 128
EPS = 1e-06
F32 = jnp.float32
BF16 = jnp.bfloat16
SCALE = 1.0 / math.sqrt(HD)
SWAP = [(0, 1), (1, 0)]


def rope_tables(grid_pos):
    pairs = HD // 2
    width = pairs // 3
    first = pairs - 2 * width
    index = np.arange(pairs)
    part = np.where(index < first, 0, np.where(index < first + width, 1, 2))
    offset = np.where(part == 0, index, np.where(part == 1, index - first, index - first - width))
    frequency = 10000.0 ** (-offset / np.where(part == 0, first, width))
    position = grid_pos.astype(F32)
    angles = 0.0
    for axis in range(3):
        lane = np.repeat(frequency * (part == axis), 2)
        angles = angles + position[axis][:, None] * jnp.asarray(lane, F32)[None, :]
    sign = np.where(np.arange(HD) % 2 == 0, -1.0, 1.0)
    return jnp.cos(angles), jnp.sin(angles) * jnp.asarray(sign, F32)[None, :]


def partner(values):
    even = (jnp.arange(values.shape[-1]) % 2) == 0
    return jnp.where(even, jnp.roll(values, -1, -1), jnp.roll(values, 1, -1))


def turn(values, cosine, sine):
    heads = values.shape[-1] // HD
    wide = (1,) * (values.ndim - 1) + (heads,)
    return values * jnp.tile(cosine, wide) + partner(values) * jnp.tile(sine, wide)


def layer_norm(values):
    center = values - jnp.mean(values, -1, keepdims=True)
    inverse = lax.rsqrt(jnp.mean(center * center, -1, keepdims=True) + EPS)
    return center * inverse, inverse


def norm_backward(normed, inverse, grad_in):
    return inverse * (
        grad_in
        - jnp.mean(grad_in, -1, keepdims=True)
        - normed * jnp.mean(grad_in * normed, -1, keepdims=True)
    )


def mm(a, b):
    return lax.dot_general(a, b, (((a.ndim - 1,), (0,)), ((), ())), preferred_element_type=F32)


def mm_t(a, b):
    return lax.dot_general(a, b, (((a.ndim - 1,), (1,)), ((), ())), preferred_element_type=F32)


def outer(a, b):
    lead = tuple(range(a.ndim - 1))
    return lax.dot_general(a, b, ((lead, lead), ((), ())), preferred_element_type=F32)


def on_device(
    states, text_emb, grid_pos, time_mod, w_qkv, w_out, w_cross, w_crossout, w_up, w_down,
    attn_bias, qk_gain, norm_gain, norm_bias, up_bias, down_bias, modulation, out_grad,
):
    x, y, core = lax.axis_index("x"), lax.axis_index("y"), lax.axis_index("core")
    seqs = lax.axis_size("z")
    reps = lax.axis_size("rep")
    dim = states.shape[1]
    block = y * 2 + x

    def from_y(a):
        return lax.ppermute(a, "y", SWAP)

    def from_x(a):
        return lax.ppermute(a, "x", SWAP)

    def from_xy(a):
        return lax.ppermute(a, ("x", "y"), [(i, 3 - i) for i in range(4)])

    def from_core(a):
        return lax.ppermute(a, "core", SWAP)

    def gather4(a):
        far, xs, ys = from_xy(a), from_x(a), from_y(a)
        return jnp.stack([a, ys, xs, far])

    def reduce4(term):
        far = from_xy(term(3).astype(BF16))
        xs = from_x(term(2).astype(BF16))
        ys = from_y(term(1).astype(BF16))
        return term(0) + ys.astype(F32) + xs.astype(F32) + far.astype(F32)

    def sum4(stat):
        far, xs, ys = from_xy(stat), from_x(stat), from_y(stat)
        return (
            stat
            + jnp.stack([ys[1], ys[0], ys[3], ys[2]])
            + jnp.stack([xs[2], xs[3], xs[0], xs[1]])
            + jnp.stack([far[3], far[2], far[1], far[0]])
        )

    def reorder(a):
        a = jnp.where(x == 1, jnp.stack([a[2], a[3], a[0], a[1]]), a)
        return jnp.where(y == 1, jnp.stack([a[1], a[0], a[3], a[2]]), a)

    def heads_swap(a):
        return lax.all_to_all(a, "z", split_axis=0, concat_axis=0, tiled=True)

    def pick(v, blocks=4):
        return lax.dynamic_index_in_dim(
            v.reshape(v.shape[:-1] + (blocks, v.shape[-1] // blocks)), block, v.ndim - 1, False
        )

    def spread(v):
        hot = (jnp.arange(4) == block).astype(F32)
        full = v[..., None, :] * hot[:, None]
        return full.reshape(v.shape[:-1] + (4 * v.shape[-1],))

    def column_block(w):
        rows, groups, width = w.shape[0], w.shape[1], w.shape[2] // 4
        mine = lax.dynamic_index_in_dim(w.reshape(rows, groups, 2, 2, width), x, 3, False)
        keep = lax.dynamic_index_in_dim(mine, y, 2, False).reshape(rows, groups * width)
        send = lax.dynamic_index_in_dim(mine, 1 - y, 2, False).reshape(rows, groups * width)
        recv = from_y(send)
        both = jnp.where(y == 0, jnp.stack([keep, recv]), jnp.stack([recv, keep]))
        full = lax.all_gather(both, ("core", "z"), axis=1, tiled=True)
        return full.reshape(-1, groups * width)

    def row_block(w):
        rows, half = w.shape[0], w.shape[1] // 2
        keep = lax.dynamic_slice_in_dim(w, core * half, half, 1)
        recv = from_core(lax.dynamic_slice_in_dim(w, (1 - core) * half, half, 1))
        mine = jnp.where(core == x, keep, recv)
        full = lax.all_gather(mine, ("core", "z"), axis=0, tiled=True)
        return full.reshape(2, seqs * rows, half).transpose(1, 0, 2).reshape(seqs * rows, 2 * half)

    def over_reps(a):
        return lax.psum(a, "rep") if reps > 1 else a

    def column_grad(g, groups):
        width = g.shape[1] // groups
        g = g.astype(BF16).reshape(2, 2, seqs, -1, groups * width)
        keep = lax.dynamic_index_in_dim(g, core, 1, False)
        recv = from_core(lax.dynamic_index_in_dim(g, 1 - core, 1, False))
        both = (keep.astype(F32) + recv.astype(F32)).astype(BF16)
        both = both.transpose(1, 0, 2, 3).reshape(-1, groups * width)
        part = lax.psum_scatter(both, "z", scatter_dimension=0, tiled=True)
        part = over_reps(part).reshape(2, -1, groups * width)
        keep = lax.dynamic_index_in_dim(part, y, 0, False)
        recv = from_y(lax.dynamic_index_in_dim(part, 1 - y, 0, False))
        ours = jnp.where(y == 0, jnp.stack([keep, recv]), jnp.stack([recv, keep]))
        theirs = from_x(ours)
        rows = ours.shape[1]
        ours = ours.reshape(2, rows, groups, width)
        theirs = theirs.reshape(2, rows, groups, width)
        full = jnp.where(x == 0, jnp.stack([ours, theirs], 1), jnp.stack([theirs, ours], 1))
        return full.transpose(2, 3, 0, 1, 4).reshape(rows, groups, 4 * width).astype(F32)

    def row_grad(g):
        rows, half = g.shape[0] // seqs, g.shape[1] // 2
        g = g.astype(BF16)
        keep = lax.dynamic_slice_in_dim(g, core * half, half, 1)
        recv = from_core(lax.dynamic_slice_in_dim(g, (1 - core) * half, half, 1))
        both = (keep.astype(F32) + recv.astype(F32)).astype(BF16)
        part = lax.psum_scatter(both, "z", scatter_dimension=0, tiled=True)
        part = over_reps(part)
        other = from_x(part)
        ours = jnp.where(core == x, part, other)
        theirs = from_core(jnp.where(core == x, other, part))
        full = jnp.where(
            core == 0,
            jnp.concatenate([ours, theirs], 1),
            jnp.concatenate([theirs, ours], 1),
        )
        return full.astype(F32)

    mods = modulation + time_mod[0]
    shift1, scale1, gate1, shift2, scale2, gate2 = [mods[i] for i in range(6)]

    self_normed, self_inverse = layer_norm(states)
    self_in = (self_normed * (1.0 + scale1) + shift1).astype(BF16)
    x_self = gather4(self_in)
    tables = gather4(jnp.concatenate(rope_tables(grid_pos), 1))
    cosine, sine = tables[..., :HD], tables[..., HD:]
    full_qkv = column_block(w_qkv)
    full_out = row_block(w_out)
    full_cross = column_block(w_cross)
    full_crossout = row_block(w_crossout)
    full_up = column_block(w_up[:, None, :])
    full_down = row_block(w_down)
    bias = pick(attn_bias)
    gain = pick(qk_gain)
    width = bias.shape[1]
    heads = width // HD

    def rms_scale(v):
        return lax.rsqrt(v / dim + EPS)[..., None]

    project = mm(x_self, full_qkv)
    q_pre = project[..., :width] + bias[0]
    k_pre = project[..., width : 2 * width] + bias[1]
    value = (project[..., 2 * width :] + bias[2]).astype(BF16)
    squares = sum4(jnp.stack([jnp.sum(q_pre * q_pre, -1), jnp.sum(k_pre * k_pre, -1)], 1))
    q_inv, k_inv = rms_scale(squares[:, 0]), rms_scale(squares[:, 1])
    q_unit, k_unit = q_pre * q_inv, k_pre * k_inv
    query = turn(q_unit * gain[0], cosine, sine).astype(BF16)
    key = turn(k_unit * gain[1], cosine, sine).astype(BF16)
    packed = heads_swap(reorder(jnp.concatenate([query, key, value], -1)))
    packed = packed.reshape(-1, 3, heads, HD)
    q_h, k_h, v_h = packed[:, 0], packed[:, 1], packed[:, 2]
    scores = jnp.einsum("qhd,khd->hqk", q_h, k_h, preferred_element_type=F32) * SCALE
    top = jnp.max(scores, -1, keepdims=True)
    weight = jnp.exp(scores - top)
    total = jnp.sum(weight, -1, keepdims=True)
    probs = weight / total
    mixed = jnp.einsum("hqk,khd->qhd", probs.astype(BF16), v_h, preferred_element_type=F32)
    self_lse = top + jnp.log(total)
    mixed = mixed.astype(BF16).reshape(seqs, -1, width)
    mixed = reorder(heads_swap(mixed))
    branch = reduce4(lambda k: mm(mixed[k], full_out)) + attn_bias[3]
    after_self = states + branch * gate1

    x_text = gather4(text_emb)
    text_proj = mm(x_text, full_cross[:, width:])
    ck_pre = text_proj[..., :width] + bias[5]
    cross_v = (text_proj[..., width:] + bias[6]).astype(BF16)
    ck_inv = rms_scale(sum4(jnp.sum(ck_pre * ck_pre, -1)))
    ck_unit = ck_pre * ck_inv
    cross_k = (ck_unit * gain[3]).astype(BF16)
    text_kv = lax.all_gather(jnp.concatenate([cross_k, cross_v], -1), "z", axis=1, tiled=True)
    text_kv = text_kv.reshape(4, -1, 2, heads, HD)
    ck_h, cv_h = text_kv[:, :, 0], text_kv[:, :, 1]

    cross_normed, cross_inverse = layer_norm(after_self)
    cross_in = (cross_normed * norm_gain + norm_bias).astype(BF16)
    x_cross = gather4(cross_in)
    cq_pre = mm(x_cross, full_cross[:, :width]) + bias[4]
    cq_inv = rms_scale(sum4(jnp.sum(cq_pre * cq_pre, -1)))
    cq_unit = cq_pre * cq_inv
    cross_q = (cq_unit * gain[2]).astype(BF16)
    rows = cross_q.shape[1]
    cq_h = cross_q.reshape(4, rows, heads, HD)
    c_scores = jnp.einsum("cqhd,ckhd->chqk", cq_h, ck_h, preferred_element_type=F32) * SCALE
    c_top = jnp.max(c_scores, -1, keepdims=True)
    c_weight = jnp.exp(c_scores - c_top)
    c_total = jnp.sum(c_weight, -1, keepdims=True)
    c_probs = c_weight / c_total
    cross_mix = jnp.einsum("chqk,ckhd->cqhd", c_probs.astype(BF16), cv_h, preferred_element_type=F32)
    cross_mix = cross_mix.astype(BF16).reshape(4, rows, width)
    c_lse = c_top + jnp.log(c_total)
    cross_out = reduce4(lambda k: mm(cross_mix[k], full_crossout)) + attn_bias[7]
    after_cross = after_self + cross_out

    ffn_normed, ffn_inverse = layer_norm(after_cross)
    ffn_in = (ffn_normed * (1.0 + scale2) + shift2).astype(BF16)
    d_ffnout = (out_grad * gate2).astype(BF16)
    g_ffn = gather4(d_ffnout)
    x_ffn = gather4(ffn_in)
    hidden_pre = mm(x_ffn, full_up) + pick(up_bias)
    root = math.sqrt(2.0 / math.pi)
    bent = jnp.tanh(root * (hidden_pre + 0.044715 * hidden_pre**3))
    hidden = (0.5 * hidden_pre * (1.0 + bent)).astype(BF16)
    slope = 0.5 * (1.0 + bent) + 0.5 * hidden_pre * (1.0 - bent * bent) * root * (
        1.0 + 3.0 * 0.044715 * hidden_pre * hidden_pre
    )
    d_hpre32 = mm_t(g_ffn, full_down) * slope
    d_hpre = d_hpre32.astype(BF16)
    d_ffnin = reduce4(lambda k: mm_t(d_hpre[k], full_up))
    ffn_out = reduce4(lambda k: mm(hidden[k], full_down)) + down_bias
    block_out = after_cross + ffn_out * gate2
    up_grad = column_grad(outer(x_ffn, d_hpre), 1)[:, 0]
    down_grad = row_grad(outer(hidden, g_ffn))
    d_cross = out_grad + norm_backward(ffn_normed, ffn_inverse, d_ffnin * (1.0 + scale2))

    d_crossout = d_cross.astype(BF16)
    g_cross = gather4(d_crossout)
    d_cmix = mm_t(g_cross, full_crossout).astype(BF16)
    d_cmix_h = d_cmix.reshape(4, rows, heads, HD)
    c_scores = jnp.einsum("cqhd,ckhd->chqk", cq_h, ck_h, preferred_element_type=F32) * SCALE
    c_probs = jnp.exp(c_scores - c_lse)
    c_dp = jnp.einsum("cqhd,ckhd->chqk", d_cmix_h, cv_h, preferred_element_type=F32)
    c_ds = (c_probs * (c_dp - jnp.sum(c_probs * c_dp, -1, keepdims=True))).astype(BF16)
    d_cqn = jnp.einsum("chqk,ckhd->cqhd", c_ds, ck_h, preferred_element_type=F32) * SCALE
    d_ckn = jnp.einsum("chqk,cqhd->ckhd", c_ds, cq_h, preferred_element_type=F32) * SCALE
    d_cvn = jnp.einsum("chqk,cqhd->ckhd", c_probs.astype(BF16), d_cmix_h, preferred_element_type=F32)
    d_ckv = jnp.concatenate([d_ckn.reshape(4, -1, width), d_cvn.reshape(4, -1, width)], -1)
    d_ckv = d_ckv.astype(BF16).reshape(4, seqs, -1, 2 * width).transpose(1, 0, 2, 3)
    d_ckv = lax.psum_scatter(d_ckv, "z", scatter_dimension=0, tiled=True)[0]

    def rms_back(grad, unit, inverse, scale, extra_sum):
        d_unit = grad * scale
        mean = extra_sum / dim
        return inverse * (d_unit - unit * mean[..., None])

    def inner(grad, unit, scale):
        return jnp.sum(grad * scale * unit, -1)

    d_cqn = d_cqn.reshape(4, rows, width)
    cq_stat = sum4(inner(d_cqn, cq_unit, gain[2]))
    d_cq = rms_back(d_cqn, cq_unit, cq_inv, gain[2], cq_stat).astype(BF16)
    cq_gain = jnp.sum(d_cqn * cq_unit, (0, 1))
    d_crossin = reduce4(lambda k: mm_t(d_cq[k], full_cross[:, :width]))

    d_ckn = d_ckv[..., :width].astype(F32)
    d_cv = d_ckv[..., width:]
    ck_stat = sum4(inner(d_ckn, ck_unit, gain[3]))
    d_ck = rms_back(d_ckn, ck_unit, ck_inv, gain[3], ck_stat).astype(BF16)
    ck_gain = jnp.sum(d_ckn * ck_unit, (0, 1))
    d_text = jnp.concatenate([d_ck, d_cv], -1)
    text_grad = reduce4(lambda k: mm_t(d_text[k], full_cross[:, width:]))
    cross_grad = column_grad(
        jnp.concatenate([outer(x_cross, d_cq), outer(x_text, d_text)], 1), 3
    )
    crossout_grad = row_grad(outer(cross_mix, g_cross))
    d_self = d_cross + norm_backward(cross_normed, cross_inverse, d_crossin * norm_gain)

    d_branch = (d_self * gate1).astype(BF16)
    g_self = gather4(d_branch)
    d_mix = mm_t(g_self, full_out).astype(BF16)
    d_mix_h = heads_swap(reorder(d_mix)).reshape(-1, heads, HD)
    scores = jnp.einsum("qhd,khd->hqk", q_h, k_h, preferred_element_type=F32) * SCALE
    probs = jnp.exp(scores - self_lse)
    dp = jnp.einsum("qhd,khd->hqk", d_mix_h, v_h, preferred_element_type=F32)
    ds = (probs * (dp - jnp.sum(probs * dp, -1, keepdims=True))).astype(BF16)
    dq = jnp.einsum("hqk,khd->qhd", ds, k_h, preferred_element_type=F32) * SCALE
    dk = jnp.einsum("hqk,qhd->khd", ds, q_h, preferred_element_type=F32) * SCALE
    dv = jnp.einsum("hqk,qhd->khd", probs.astype(BF16), d_mix_h, preferred_element_type=F32)
    d_packed = jnp.stack([dq, dk, dv], 1).astype(BF16).reshape(seqs, -1, 3 * width)
    d_packed = reorder(heads_swap(d_packed))
    d_value = d_packed[..., 2 * width :]
    d_qn = turn(d_packed[..., :width].astype(F32), cosine, -sine)
    d_kn = turn(d_packed[..., width : 2 * width].astype(F32), cosine, -sine)
    stats = sum4(jnp.stack([inner(d_qn, q_unit, gain[0]), inner(d_kn, k_unit, gain[1])], 1))
    d_q = rms_back(d_qn, q_unit, q_inv, gain[0], stats[:, 0]).astype(BF16)
    d_k = rms_back(d_kn, k_unit, k_inv, gain[1], stats[:, 1]).astype(BF16)
    q_gain = jnp.sum(d_qn * q_unit, (0, 1))
    k_gain = jnp.sum(d_kn * k_unit, (0, 1))
    d_qkv = jnp.concatenate([d_q, d_k, d_value], -1)
    d_selfin = reduce4(lambda k: mm_t(d_qkv[k], full_qkv))
    qkv_grad = column_grad(outer(x_self, d_qkv), 3)
    outproj_grad = row_grad(outer(mixed, g_self))
    states_grad = d_self + norm_backward(self_normed, self_inverse, d_selfin * (1.0 + scale1))

    def column_sum(v):
        return jnp.sum(v.astype(F32), tuple(range(v.ndim - 1)))

    def over_z(v):
        v = v + lax.ppermute(v, "z", [(i, i ^ 1) for i in range(seqs)])
        return v + lax.ppermute(v, "z", [(i, i ^ 2) for i in range(seqs)])

    def over_clips(v):
        v = v + from_core(v)
        v = v + from_x(v)
        v = v + from_y(v)
        return over_reps(v)

    early = jnp.stack(
        [
            column_sum(d_ffnin),
            column_sum(d_ffnin * ffn_normed),
            column_sum(out_grad * ffn_out),
            spread(column_sum(d_cq)),
            spread(column_sum(d_ck)),
            spread(column_sum(d_cv)),
            column_sum(d_crossout),
            spread(cq_gain),
            spread(ck_gain),
            column_sum(d_crossin * cross_normed),
            column_sum(d_crossin),
            column_sum(d_ffnout),
            column_sum(d_branch),
            column_sum(d_self * branch),
        ]
    )
    upbias = over_clips(over_z(spread(column_sum(d_hpre))))
    early_clip = over_z(early)
    early_all = over_clips(early_clip)
    late = jnp.stack(
        [
            column_sum(d_selfin),
            column_sum(d_selfin * self_normed),
            spread(column_sum(d_q)),
            spread(column_sum(d_k)),
            spread(column_sum(d_value)),
            spread(q_gain),
            spread(k_gain),
        ]
    )
    late_clip = over_z(late)
    late_all = over_clips(late_clip)

    def mod_rows(e, l):
        return jnp.stack([l[0], l[1], e[13], e[0], e[1], e[2]])

    time_grad = mod_rows(early_clip, late_clip)[None]
    mod_grad = mod_rows(early_all, late_all)
    bias_grad = jnp.stack(
        [late_all[2], late_all[3], late_all[4], early_all[12]] + [early_all[i] for i in (3, 4, 5, 6)]
    )
    gain_grad = jnp.stack([late_all[5], late_all[6], early_all[7], early_all[8]])
    return (
        block_out,
        states_grad,
        text_grad,
        time_grad,
        qkv_grad,
        outproj_grad,
        cross_grad,
        crossout_grad,
        up_grad,
        down_grad,
        bias_grad,
        gain_grad,
        early_all[9],
        early_all[10],
        upbias,
        early_all[11],
        mod_grad,
    )


def solution(mesh):
    reps, shards, seqs = mesh.shape["replica"], mesh.shape["shard"], mesh.shape["seq"]
    fine = Mesh(
        mesh.devices.reshape(reps // 2, 2, shards // 2, 2, seqs), ("rep", "x", "y", "core", "z")
    )
    tokens = P(("rep", "x", "y", "core", "z"), None)
    clips = P(("rep", "x", "y", "core"), None, None)
    rows2 = P(("y", "core", "z"), None)
    rows3 = P(("y", "core", "z"), None, None)
    return jax.shard_map(
        on_device,
        mesh=fine,
        in_specs=(
            tokens, tokens, P(None, ("rep", "x", "y", "core", "z")), clips,
            rows3, rows2, rows3, rows2, rows2, rows2,
            P(), P(), P(), P(), P(), P(), P(), tokens,
        ),
        out_specs=(
            tokens, tokens, tokens, clips,
            rows3, rows2, rows3, rows2, rows2, rows2,
            P(), P(), P(), P(), P(), P(), P(),
        ),
        check_vma=False,
    )
```

time: 2210 us -> 1130 us (0.51)
  waiting for transfers between devices: 1660 us -> 484 us
  starting transfers between devices: 34.6 us -> 119 us
  local copies, waits for them, and re-layouts: 156 us -> 206 us
  matrix products: 220 us -> 188 us
    reduce_scatter x6 -> x7, waiting for transfers between devices: 772 us -> 0.01 us  [the longest x3 0.01 us: row_grad(): part = lax.psum_scatter(both, 'z', scatter_dimension=0, tiled=True)]
    all_gather x8 -> x7, waiting for transfers between devices: 507 us -> 10.3 us  [the longest x3 10.2 us: column_block(): full = lax.all_gather(both, ('core', 'z'), axis=1, tiled=True)]
    ppermute x0 -> x102, waiting for transfers between devices: none -> 369 us  [the longest x30 112 us: from_y(): return lax.ppermute(a, 'y', SWAP)]
    psum x2 -> x0, waiting for transfers between devices: 228 us -> none  [the longest x1 125 us: on_device(): lax.psum((bias_local, gain_local, lngain_local, lnbias_local, upbias_loca...]
    ppermute x0 -> x102, starting transfers between devices: none -> 103 us  [the longest x21 33.5 us: from_xy(): return lax.ppermute(a, ('x', 'y'), [(i, 3 - i) for i in range(4)])]
    all_to_all x8 -> x4, waiting for transfers between devices: 146 us -> 105 us  [heads_swap(): return lax.all_to_all(a, 'z', split_axis=0, concat_axis=0, tiled=True)]
    reshape x17, local copies, waits for them, and re-layouts: 33 us -> 69.5 us  [the longest x6 56.8 us: row_block(): full.reshape(2, seqs * rows, half).transpose(1, 0, 2)]
    dot_general x35 -> x54, matrix products: 220 us -> 188 us  [the longest x19 71.1 us: mm_t(): lax.dot_general(a, b, (((a.ndim - 1,), (1,)), ((), ())), preferred_elemen...]
  transfers between devices with their start and end apart: 26 -> 120, of which waited for: 18 -> 67; matrix products, arithmetic and copies ran while one was open for 17% -> 36% of each run, Pallas kernels for 0% -> 0%
where the time goes in v1:
time: 1130 us; the launch traced here: 1110 us
  waiting for transfers between devices  484 us (43%)
  local copies, waits for them, and re-layouts  206 us (18%)
  matrix products  188 us (17%)
  starting transfers between devices  119 us (11%)
  other arithmetic  99.6 us (9%)
  between operations  17.1 us (2%)
    ppermute x30, waiting for transfers between devices, from_y(): return lax.ppermute(a, 'y', SWAP)  112 us
    all_to_all x4, waiting for transfers between devices, heads_swap(): return lax.all_to_all(a, 'z', split_axis=0, concat_axis=0, tiled=True)  105 us
    ppermute x21, waiting for transfers between devices, from_xy(): return lax.ppermute(a, ('x', 'y'), [(i, 3 - i) for i in range(4)])  97.4 us
    dot_general x19, matrix products, mm_t(): lax.dot_general(a, b, (((a.ndim - 1,), (1,)), ((), ())), preferred_elemen...  71.1 us
    ppermute x3, waiting for transfers between devices, over_z(): v = v + lax.ppermute(v, 'z', [(i, i ^ 1) for i in range(seqs)])  61.2 us
    reshape x6, local copies, waits for them, and re-layouts, row_block(): full.reshape(2, seqs * rows, half).transpose(1, 0, 2)  56.8 us
    ppermute x30, waiting for transfers between devices, from_x(): return lax.ppermute(a, 'x', SWAP)  53.2 us
    dot_general x16, matrix products, mm(): lax.dot_general(a, b, (((a.ndim - 1,), (0,)), ((), ())), preferred_elemen...  46.9 us
  transfers between devices with their start and end apart: 120, of which 67 were waited for; matrix products, arithmetic and copies ran while one was open for 36% of the time, Pallas kernels for 0%

profile of v1, /device:TPU:0, one launch (start us, length us, event | category | flops | bytes accessed | tf_op | source)
XLA Modules:
  0.0 1115.0 jit_solution(16156421122203822195)
XLA Ops:
  14.5 4.9 collective-permute-done.17
  37.4 6.1 collective-permute-done.14
  45.5 7.6 collective-permute-done.16
  53.1 10.2 all-gather.12.cloned.1.call-done
  95.6 27.0 %collective-permute-done.34 = bf16[96,2240]{1,0:T(8,128)(2,1)} collective-permute-done((bf16[96,2240]{1,0:T(8,128)(2,1)}, bf16[96,2240]{1,0:T(8,128)(2,1)}, u32[]{:S(2)}, u32[]{:S(2)}) %collective-permute-start.34) | collective-permute-done | bytes 430112 | tf_op jit(solution)/shard_map/ppermute | solution.py:83
  125.0 6.0 fusion.109
  159.4 82.2 %all-to-all-done = bf16[4,195,1152]{2,1,0:T(8,128)(2,1)S(1)} async-done(((bf16[4,195,1152]{2,1,0:T(8,128)(2,1)}), bf16[4,195,1152]{2,1,0:T(8,128)(2,1)S(1)}, u32[]{:S(2)}, u32[]{:S(2)}) %all-to-all-start) | async-done | bytes 1797152 | tf_op jit(solution)/shard_map/all_to_all | solution.py:118
  265.6 21.7 %all-to-all-done.1 = bf16[4,195,384]{2,1,0:T(8,128)(2,1)S(1)} async-done(((bf16[4,195,384]{2,1,0:T(8,128)(2,1)}), bf16[4,195,384]{2,1,0:T(8,128)(2,1)S(1)}, u32[]{:S(2)}, u32[]{:S(2)}) %all-to-all-start.1) | async-done | bytes 599072 | tf_op jit(solution)/shard_map/all_to_all | solution.py:118
  293.7 9.2 collective-permute-done.11
  303.8 13.9 %collective-permute-done.13 = bf16[195,1536]{1,0:T(8,128)(2,1)S(1)} collective-permute-done((bf16[195,1536]{1,0:T(8,128)(2,1)S(1)}, bf16[195,1536]{1,0:T(8,128)(2,1)S(1)}, u32[]{:S(2)}, u32[]{:S(2)}) %collective-permute-start.13) | collective-permute-done | bytes 599072 | tf_op jit(solution)/shard_map/ppermute | solution.py:89
  325.2 6.4 collective-permute-done.21
  332.3 7.4 collective-permute-done.23
  349.1 5.0 copy.182
  375.3 10.8 collective-permute-done.28
  388.7 13.6 %collective-permute-done.30 = bf16[195,1536]{1,0:T(8,128)(2,1)S(1)} collective-permute-done((bf16[195,1536]{1,0:T(8,128)(2,1)S(1)}, bf16[195,1536]{1,0:T(8,128)(2,1)S(1)}, u32[]{:S(2)}, u32[]{:S(2)}) %collective-permute-start.30) | collective-permute-done | bytes 599072 | tf_op jit(solution)/shard_map/ppermute | solution.py:89
  412.8 9.0 collective-permute-done.31
  422.8 5.7 collective-permute-done.33
  428.5 13.4 %multiply_convert_fusion.1 = (bf16[4,195,2240]{2,1,0:T(8,128)(2,1)}, f32[4,195,2240]{2,1,0:T(8,128)}) fusion(f32[2240]{0:T(1024)S(1)} %fusion.130, bf16[1536,2240,1]{1,0,2:T(8,128)(2,1)} %bitcast.583, bf16[1,195,1536]{2,1,0:T(8,128)(2,1)} %bitcast.50, bf16[1,195,1536]{2,1,0:T(8,128)(2,1)} %bitcast.49, bf16[1,195,1536]{2,1,0:T(8,128)(2,1)} %bitcast.48, ...), kind=kOutput, calls=%fused_computation.22 | convolution fusion | flops 5388462080 | bytes 19769600 | tf_op jit(solution)/shard_map/dot_general | solution.py:60
  442.0 32.2 %copy.325 = bf16[2,2240,768]{2,0,1:T(2,128)(2,1)} copy(bf16[2,2240,768]{2,1,0:T(8,128)(2,1)} %bitcast.507) | data formatting | bytes 13762560 | tf_op jit(solution)/shard_map/reshape | solution.py:146
  474.2 15.7 %reshape.1261 = bf16[2240,1536,1]{1,0,2:T(8,128)(2,1)} reshape(bf16[2240,2,768]{2,1,0:T(2,128)(2,1)} %bitcast.478) | data formatting | bytes 13762560 | tf_op jit(solution)/shard_map/reshape | solution.py:146
  489.9 15.2 %convert_reduce_fusion = (f32[2240]{0:T(1024)S(1)}, bf16[4,195,2240]{2,1,0:T(8,128)(2,1)S(1)}) fusion(f32[4,195,2240]{2,1,0:T(8,128)} %get-tuple-element.274, f32[2240]{0:T(1024)S(1)} %fusion.130, bf16[2240,1536,1]{1,0,2:T(8,128)(2,1)} %reshape.1261, bf16[1,195,1536]{2,1,0:T(8,128)(2,1)} %bitcast.63, bf16[1,195,1536]{2,1,0:T(8,128)(2,1)} %bitcast.62, ...), kind=kOutput, calls=%fused_computation.21 | convolution fusion | flops 5409423360 | bytes 19778560 | tf_op jit(solution)/shard_map/dot_general | solution.py:64
  505.0 7.6 convolution_convert_fusion.8
  512.6 6.4 convolution_convert_fusion.7
  519.0 6.4 convolution_convert_fusion.6
  545.5 5.9 collective-permute-done.44
  551.3 5.0 multiply_reduce_fusion.8
  556.3 5.0 collective-permute-done.36
  563.2 7.0 collective-permute-done.38
  585.4 7.1 collective-permute-done.47
  597.5 4.8 multiply_reduce_fusion.2
  635.5 8.2 collective-permute-done.53
  653.6 8.6 collective-permute-done.54
  662.2 6.6 collective-permute-done.56
  679.6 5.2 fusion.40
  693.9 10.1 bitcast_convert_fusion
  716.7 5.7 add_convert_fusion
  723.5 12.1 %bitcast_convert_fusion.1 = bf16[1536,2240]{0,1:T(8,128)(2,1)} fusion(bf16[4,195,2240]{2,1,0:T(8,128)(2,1)} %copy-done.143, bf16[1,195,1536]{2,1,0:T(8,128)(2,1)} %bitcast.50, bf16[1,195,1536]{2,1,0:T(8,128)(2,1)} %bitcast.49, bf16[1,195,1536]{2,1,0:T(8,128)(2,1)} %bitcast.48, bf16[1,195,1536]{2,1,0:T(8,128)(2,1)S(1)} %copy-done.71), kind=kOutput, calls=%fused_computation.1 | convolution fusion | flops 5374433280 | bytes 12771840 | tf_op jit(solution)/shard_map/dot_general | solution.py:69
  735.6 9.7 copy.215
  751.4 4.9 multiply_reduce_fusion
  775.3 53.4 %collective-permute-done.97 = f32[8960]{0:T(1024)S(1)} collective-permute-done((f32[8960]{0:T(1024)S(1)}, f32[8960]{0:T(1024)S(1)}, u32[]{:S(2)}, u32[]{:S(2)}) %collective-permute-start.97) | collective-permute-done | bytes 35872 | tf_op jit(solution)/shard_map/ppermute | solution.py:359
  828.8 5.1 collective-permute-start.98
  833.9 31.5 %collective-permute-done.98 = f32[8960]{0:T(1024)S(1)} collective-permute-done((f32[8960]{0:T(1024)S(1)}, f32[8960]{0:T(1024)S(1)}, u32[]{:S(2)}, u32[]{:S(2)}) %collective-permute-start.98) | collective-permute-done | bytes 35872 | tf_op jit(solution)/shard_map/ppermute | solution.py:360
  926.3 5.7 fusion
  939.0 11.6 %collective-permute-done.62 = bf16[195,1536]{1,0:T(8,128)(2,1)S(1)} collective-permute-done((bf16[195,1536]{1,0:T(8,128)(2,1)S(1)}, bf16[195,1536]{1,0:T(8,128)(2,1)S(1)}, u32[]{:S(2)}, u32[]{:S(2)}) %collective-permute-start.62) | collective-permute-done | bytes 599072 | tf_op jit(solution)/shard_map/ppermute | solution.py:89
  1004.2 6.8 collective-permute-done.72
  1039.0 13.8 %collective-permute-done.89 = bf16[560,768]{1,0:T(8,128)(2,1)} collective-permute-done((bf16[560,768]{1,0:T(8,128)(2,1)}, bf16[560,768]{1,0:T(8,128)(2,1)}, u32[]{:S(2)}, u32[]{:S(2)}) %collective-permute-start.89) | collective-permute-done | bytes 860192 | tf_op jit(solution)/shard_map/ppermute | solution.py:86
  1059.3 6.3 collective-permute-done.74
  1071.1 7.8 collective-permute-done.87
  (860 shorter events, 506.6 us)
Async XLA Ops:
  7.2 56.2 %all-gather.12.cloned.1.call-start = ((), (), s32[]{:S(2)}) async-start(), calls=%async_computation.13 | async-start | bytes 3981312 | tf_op jit(solution)/shard_map/all_gather | solution.py:137
  20.3 104.7 %all-gather.8.cloned.1.call-start = ((), (), s32[]{:S(2)}) async-start(), calls=%async_computation.11 | async-start | bytes 3981312 | tf_op jit(solution)/shard_map/all_gather | solution.py:137
  29.4 232.5 %all-gather.10.cloned.1.call-start = ((), (), s32[]{:S(2)}) async-start(), calls=%async_computation.12 | async-start | bytes 1327104 | tf_op jit(solution)/shard_map/all_gather | solution.py:145
  31.8 313.6 %all-gather.16.cloned.1.call-start = ((), (), s32[]{:S(2)}) async-start(), calls=%async_computation.15 | async-start | bytes 1327104 | tf_op jit(solution)/shard_map/all_gather | solution.py:145
  36.4 312.8 %all-gather.14.cloned.1.call-start = ((), (), s32[]{:S(2)}) async-start(), calls=%async_computation.14 | async-start | bytes 3932160 | tf_op jit(solution)/shard_map/all_gather | solution.py:241
  75.0 353.6 %all-gather.18.cloned.1.call-start = ((), (), s32[]{:S(2)}) async-start(), calls=%async_computation.16 | async-start | bytes 7962624 | tf_op jit(solution)/shard_map/all_gather | solution.py:137
  81.5 43.4 %collective-permute-start = (bf16[195,1536]{1,0:T(8,128)(2,1)}, bf16[195,1536]{1,0:T(8,128)(2,1)}, u32[]{:S(2)}, u32[]{:S(2)}) collective-permute-start(bf16[195,1536]{1,0:T(8,128)(2,1)} %add_convert_fusion.3), channel_id=1, source_target_pairs={{0,8},{8,0},{1,9},{9,1},{2,10},{10,2},{3,11},{11,3},{4,12},{12,4},... | collective-permute-start | bytes 1797128 | tf_op jit(solution)/shard_map/ppermute | solution.py:83
  90.4 32.1 %collective-permute-start.34 = (bf16[96,2240]{1,0:T(8,128)(2,1)}, bf16[96,2240]{1,0:T(8,128)(2,1)}, u32[]{:S(2)}, u32[]{:S(2)}) collective-permute-start(bf16[96,2240]{1,0:T(8,128)(2,1)} %bitcast.465), channel_id=1, source_target_pairs={{0,8},{8,0},{1,9},{9,1},{2,10},{10,2},{3,11},{11,3},{4,12},{12,4},... | collective-permute-start | bytes 1290248 | tf_op jit(solution)/shard_map/ppermute | solution.py:83
  91.4 33.5 %collective-permute-start.1 = (bf16[195,1536]{1,0:T(8,128)(2,1)}, bf16[195,1536]{1,0:T(8,128)(2,1)}, u32[]{:S(2)}, u32[]{:S(2)}) collective-permute-start(bf16[195,1536]{1,0:T(8,128)(2,1)} %add_convert_fusion.3), channel_id=1, source_target_pairs={{0,16},{16,0},{1,17},{17,1},{2,18},{18,2},{3,19},{19,3},{4,20},{20... | collective-permute-start | bytes 1797128 | tf_op jit(solution)/shard_map/ppermute | solution.py:86
  92.0 32.9 %collective-permute-start.2 = (bf16[195,1536]{1,0:T(8,128)(2,1)}, bf16[195,1536]{1,0:T(8,128)(2,1)}, u32[]{:S(2)}, u32[]{:S(2)}) collective-permute-start(bf16[195,1536]{1,0:T(8,128)(2,1)} %add_convert_fusion.3), channel_id=1, source_target_pairs={{0,24},{8,16},{16,8},{24,0},{1,25},{9,17},{17,9},{25,1},{2,26},{10... | collective-permute-start | bytes 1797128 | tf_op jit(solution)/shard_map/ppermute | solution.py:89
  153.5 88.1 %all-to-all-start = ((bf16[4,195,1152]{2,1,0:T(8,128)(2,1)}), bf16[4,195,1152]{2,1,0:T(8,128)(2,1)S(1)}, u32[]{:S(2)}, u32[]{:S(2)}) async-start(bf16[4,195,1152]{2,1,0:T(8,128)(2,1)} %maximum_select_fusion.1), calls=%async_computation | async-start | bytes 3686400 | tf_op jit(solution)/shard_map/all_to_all | solution.py:118
  159.4 99.8 %collective-permute-start.35 = (bf16[560,768]{1,0:T(8,128)(2,1)}, bf16[560,768]{1,0:T(8,128)(2,1)}, u32[]{:S(2)}, u32[]{:S(2)}) collective-permute-start(bf16[560,768]{1,0:T(8,128)(2,1)} %constant_dynamic-slice_fusion.16), channel_id=1, source_target_pairs={{0,4},{4,0},{1,5},{5,1},{2,6},{6,2},{3,7},{7,3},{8,12},{12,8},{9,1... | collective-permute-start | bytes 2580488 | tf_op jit(solution)/shard_map/ppermute | solution.py:92
  255.7 31.7 %all-to-all-start.1 = ((bf16[4,195,384]{2,1,0:T(8,128)(2,1)}), bf16[4,195,384]{2,1,0:T(8,128)(2,1)S(1)}, u32[]{:S(2)}, u32[]{:S(2)}) async-start(bf16[4,195,384]{2,1,0:T(8,128)(2,1)} %reshape.1224), calls=%async_computation.1 | async-start | bytes 1228800 | tf_op jit(solution)/shard_map/all_to_all | solution.py:118
  259.2 182.8 %all-gather.20.cloned.1.call-start = ((), (), s32[]{:S(2)}) async-start(), calls=%async_computation.17 | async-start | bytes 7741440 | tf_op jit(solution)/shard_map/all_gather | solution.py:145
  261.6 513.2 %reduce-scatter.16.cloned.1.call-start = ((), (), s32[]{:S(2)}) async-start(), calls=%async_computation.22 | async-start | bytes 737280 | tf_op jit(solution)/shard_map/reduce_scatter | solution.py:176
  291.3 26.4 %collective-permute-start.13 = (bf16[195,1536]{1,0:T(8,128)(2,1)S(1)}, bf16[195,1536]{1,0:T(8,128)(2,1)S(1)}, u32[]{:S(2)}, u32[]{:S(2)}) collective-permute-start(bf16[195,1536]{1,0:T(8,128)(2,1)S(1)} %convolution_convert_fusion.15), channel_id=1, source_target_pairs={{0,24},{8,16},{16,8},{24,0},{1,25},{9,17},{17,9},{25,1},{2,26},{10... | collective-permute-start | bytes 1797128 | tf_op jit(solution)/shard_map/ppermute | solution.py:89
  373.2 29.1 %collective-permute-start.30 = (bf16[195,1536]{1,0:T(8,128)(2,1)S(1)}, bf16[195,1536]{1,0:T(8,128)(2,1)S(1)}, u32[]{:S(2)}, u32[]{:S(2)}) collective-permute-start(bf16[195,1536]{1,0:T(8,128)(2,1)S(1)} %convolution_convert_fusion.12), channel_id=1, source_target_pairs={{0,24},{8,16},{16,8},{24,0},{1,25},{9,17},{17,9},{25,1},{2,26},{10... | collective-permute-start | bytes 1797128 | tf_op jit(solution)/shard_map/ppermute | solution.py:89
  407.3 21.2 %collective-permute-start.33 = (bf16[195,1536]{1,0:T(8,128)(2,1)}, bf16[195,1536]{1,0:T(8,128)(2,1)}, u32[]{:S(2)}, u32[]{:S(2)}) collective-permute-start(bf16[195,1536]{1,0:T(8,128)(2,1)} %add_convert_fusion.1), channel_id=1, source_target_pairs={{0,24},{8,16},{16,8},{24,0},{1,25},{9,17},{17,9},{25,1},{2,26},{10... | collective-permute-start | bytes 1797128 | tf_op jit(solution)/shard_map/ppermute | solution.py:89
  409.9 79.9 %collective-permute-start.39 = (bf16[195,1536]{1,0:T(8,128)(2,1)S(1)}, bf16[195,1536]{1,0:T(8,128)(2,1)}, u32[]{:S(2)}, u32[]{:S(2)}) collective-permute-start(bf16[195,1536]{1,0:T(8,128)(2,1)S(1)} %get-tuple-element.72), channel_id=1, source_target_pairs={{0,8},{8,0},{1,9},{9,1},{2,10},{10,2},{3,11},{11,3},{4,12},{12,4},... | collective-permute-start | bytes 1797128 | tf_op jit(solution)/shard_map/ppermute | solution.py:83
  411.0 78.8 %collective-permute-start.40 = (bf16[195,1536]{1,0:T(8,128)(2,1)S(1)}, bf16[195,1536]{1,0:T(8,128)(2,1)}, u32[]{:S(2)}, u32[]{:S(2)}) collective-permute-start(bf16[195,1536]{1,0:T(8,128)(2,1)S(1)} %get-tuple-element.72), channel_id=1, source_target_pairs={{0,16},{16,0},{1,17},{17,1},{2,18},{18,2},{3,19},{19,3},{4,20},{20... | collective-permute-start | bytes 1797128 | tf_op jit(solution)/shard_map/ppermute | solution.py:86
  421.8 68.0 %collective-permute-start.41 = (bf16[195,1536]{1,0:T(8,128)(2,1)S(1)}, bf16[195,1536]{1,0:T(8,128)(2,1)}, u32[]{:S(2)}, u32[]{:S(2)}) collective-permute-start(bf16[195,1536]{1,0:T(8,128)(2,1)S(1)} %get-tuple-element.72), channel_id=1, source_target_pairs={{0,24},{8,16},{16,8},{24,0},{1,25},{9,17},{17,9},{25,1},{2,26},{10... | collective-permute-start | bytes 1797128 | tf_op jit(solution)/shard_map/ppermute | solution.py:89
  526.9 24.4 %collective-permute-start.44 = (bf16[195,1536]{1,0:T(8,128)(2,1)}, bf16[195,1536]{1,0:T(8,128)(2,1)}, u32[]{:S(2)}, u32[]{:S(2)}) collective-permute-start(bf16[195,1536]{1,0:T(8,128)(2,1)} %convolution_convert_fusion.6), channel_id=1, source_target_pairs={{0,24},{8,16},{16,8},{24,0},{1,25},{9,17},{17,9},{25,1},{2,26},{10... | collective-permute-start | bytes 1797128 | tf_op jit(solution)/shard_map/ppermute | solution.py:89
  539.5 21.8 %collective-permute-start.36 = (bf16[195,1536]{1,0:T(8,128)(2,1)S(1)}, bf16[195,1536]{1,0:T(8,128)(2,1)S(1)}, u32[]{:S(2)}, u32[]{:S(2)}) collective-permute-start(bf16[195,1536]{1,0:T(8,128)(2,1)S(1)} %convolution_convert_fusion.11), channel_id=1, source_target_pairs={{0,8},{8,0},{1,9},{9,1},{2,10},{10,2},{3,11},{11,3},{4,12},{12,4},... | collective-permute-start | bytes 1797128 | tf_op jit(solution)/shard_map/ppermute | solution.py:83
  540.6 22.6 %collective-permute-start.37 = (bf16[195,1536]{1,0:T(8,128)(2,1)S(1)}, bf16[195,1536]{1,0:T(8,128)(2,1)S(1)}, u32[]{:S(2)}, u32[]{:S(2)}) collective-permute-start(bf16[195,1536]{1,0:T(8,128)(2,1)S(1)} %convolution_convert_fusion.10), channel_id=1, source_target_pairs={{0,16},{16,0},{1,17},{17,1},{2,18},{18,2},{3,19},{19,3},{4,20},{20... | collective-permute-start | bytes 1797128 | tf_op jit(solution)/shard_map/ppermute | solution.py:86
  543.5 26.7 %collective-permute-start.38 = (bf16[195,1536]{1,0:T(8,128)(2,1)}, bf16[195,1536]{1,0:T(8,128)(2,1)S(1)}, u32[]{:S(2)}, u32[]{:S(2)}) collective-permute-start(bf16[195,1536]{1,0:T(8,128)(2,1)} %convolution_convert_fusion.9), channel_id=1, source_target_pairs={{0,24},{8,16},{16,8},{24,0},{1,25},{9,17},{17,9},{25,1},{2,26},{10... | collective-permute-start | bytes 1797128 | tf_op jit(solution)/shard_map/ppermute | solution.py:89
  631.6 21.0 %collective-permute-start.82 = (bf16[384,768]{1,0:T(8,128)(2,1)S(1)}, bf16[384,768]{1,0:T(8,128)(2,1)S(1)}, u32[]{:S(2)}, u32[]{:S(2)}) collective-permute-start(bf16[384,768]{1,0:T(8,128)(2,1)S(1)} %constant_dynamic-slice_fusion.10), channel_id=1, source_target_pairs={{0,4},{4,0},{1,5},{5,1},{2,6},{6,2},{3,7},{7,3},{8,12},{12,8},{9,1... | collective-permute-start | bytes 1769480 | tf_op jit(solution)/shard_map/ppermute | solution.py:92
  653.6 233.6 %reduce-scatter.12.cloned.1.call-start = ((), (), s32[]{:S(2)}) async-start(), calls=%async_computation.20 | async-start | bytes 737280 | tf_op jit(solution)/shard_map/reduce_scatter | solution.py:176
  674.2 279.2 %reduce-scatter.8.cloned.1.call-start = ((), (), s32[]{:S(2)}) async-start(), calls=%async_computation.18 | async-start | bytes 3932160 | tf_op jit(solution)/shard_map/reduce_scatter | solution.py:299
  713.2 37.9 %all-to-all-start.2 = ((bf16[4,195,384]{2,1,0:T(8,128)(2,1)}), bf16[4,195,384]{2,1,0:T(8,128)(2,1)S(1)}, u32[]{:S(2)}, u32[]{:S(2)}) async-start(bf16[4,195,384]{2,1,0:T(8,128)(2,1)} %maximum_select_fusion.18), calls=%async_computation.2 | async-start | bytes 1228800 | tf_op jit(solution)/shard_map/all_to_all | solution.py:118
  716.7 315.7 %reduce-scatter.20.cloned.1.call-start = ((), (), s32[]{:S(2)}) async-start(), calls=%async_computation.24 | async-start | bytes 4300800 | tf_op jit(solution)/shard_map/reduce_scatter | solution.py:176
  749.3 145.4 %collective-permute-start.85 = (bf16[2,4,96,2240]{3,2,1,0:T(8,128)(2,1)}, bf16[2,4,96,2240]{3,2,1,0:T(8,128)(2,1)}, u32[]{:S(2)}, u32[]{:S(2)}) collective-permute-start(bf16[2,4,96,2240]{3,2,1,0:T(8,128)(2,1)} %dynamic-slice_bitcast_fusion), channel_id=1, source_target_pairs={{0,4},{4,0},{1,5},{5,1},{2,6},{6,2},{3,7},{7,3},{8,12},{12,8},{9,1... | collective-permute-start | bytes 10321928 | tf_op jit(solution)/shard_map/ppermute | solution.py:92
  768.4 133.4 %all-to-all-start.3 = ((bf16[4,195,1152]{2,1,0:T(8,128)(2,1)}), bf16[4,195,1152]{2,1,0:T(8,128)(2,1)S(1)}, u32[]{:S(2)}, u32[]{:S(2)}) async-start(bf16[4,195,1152]{2,1,0:T(8,128)(2,1)} %convert_element_type.458), calls=%async_computation.3 | async-start | bytes 3686400 | tf_op jit(solution)/shard_map/all_to_all | solution.py:118
  772.5 263.6 %reduce-scatter.18.cloned.1.call-start = ((), (), s32[]{:S(2)}) async-start(), calls=%async_computation.23 | async-start | bytes 4423680 | tf_op jit(solution)/shard_map/reduce_scatter | solution.py:158
  772.7 56.0 %collective-permute-start.97 = (f32[8960]{0:T(1024)S(1)}, f32[8960]{0:T(1024)S(1)}, u32[]{:S(2)}, u32[]{:S(2)}) collective-permute-start(f32[8960]{0:T(1024)S(1)} %mul.981), channel_id=1, source_target_pairs={{0,1},{1,0},{2,3},{3,2},{4,5},{5,4},{6,7},{7,6},{8,9},{9,8},{10,11... | collective-permute-start | bytes 107528 | tf_op jit(solution)/shard_map/ppermute | solution.py:359
  774.8 104.2 %collective-permute-start.83 = (bf16[96,768]{1,0:T(8,128)(2,1)}, bf16[96,768]{1,0:T(8,128)(2,1)}, u32[]{:S(2)}, u32[]{:S(2)}) collective-permute-start(bf16[96,768]{1,0:T(8,128)(2,1)} %reduce-scatter.16.cloned.1.call-done), channel_id=1, source_target_pairs={{0,16},{16,0},{1,17},{17,1},{2,18},{18,2},{3,19},{19,3},{4,20},{20... | collective-permute-start | bytes 442376 | tf_op jit(solution)/shard_map/ppermute | solution.py:86
  828.8 36.7 %collective-permute-start.98 = (f32[8960]{0:T(1024)S(1)}, f32[8960]{0:T(1024)S(1)}, u32[]{:S(2)}, u32[]{:S(2)}) collective-permute-start(f32[8960]{0:T(1024)S(1)} %add.750), channel_id=1, source_target_pairs={{0,2},{1,3},{2,0},{3,1},{4,6},{5,7},{6,4},{7,5},{8,10},{9,11},{10,... | collective-permute-start | bytes 107528 | tf_op jit(solution)/shard_map/ppermute | solution.py:360
  900.6 156.3 %reduce-scatter.10.cloned.1.call-start = ((), (), s32[]{:S(2)}) async-start(), calls=%async_computation.19 | async-start | bytes 2211840 | tf_op jit(solution)/shard_map/reduce_scatter | solution.py:158
  924.6 26.0 %collective-permute-start.62 = (bf16[195,1536]{1,0:T(8,128)(2,1)S(1)}, bf16[195,1536]{1,0:T(8,128)(2,1)S(1)}, u32[]{:S(2)}, u32[]{:S(2)}) collective-permute-start(bf16[195,1536]{1,0:T(8,128)(2,1)S(1)} %convolution_convert_fusion), channel_id=1, source_target_pairs={{0,24},{8,16},{16,8},{24,0},{1,25},{9,17},{17,9},{25,1},{2,26},{10... | collective-permute-start | bytes 1797128 | tf_op jit(solution)/shard_map/ppermute | solution.py:89
  934.9 26.3 %collective-permute-start.73 = (bf16[2,4,96,1152]{3,2,0,1:T(8,128)(2,1)}, bf16[2,4,96,1152]{3,2,0,1:T(8,128)(2,1)}, u32[]{:S(2)}, u32[]{:S(2)}) collective-permute-start(bf16[2,4,96,1152]{3,2,0,1:T(8,128)(2,1)} %bitcast.464), channel_id=1, source_target_pairs={{0,4},{4,0},{1,5},{5,1},{2,6},{6,2},{3,7},{7,3},{8,12},{12,8},{9,1... | collective-permute-start | bytes 5308424 | tf_op jit(solution)/shard_map/ppermute | solution.py:92
  964.3 104.6 %reduce-scatter.14.cloned.1.call-start = ((), (), s32[]{:S(2)}) async-start(), calls=%async_computation.21 | async-start | bytes 2211840 | tf_op jit(solution)/shard_map/reduce_scatter | solution.py:158
  972.0 43.5 %collective-permute-start.79 = (bf16[2,4,96,1152]{3,2,0,1:T(8,128)(2,1)}, bf16[2,4,96,1152]{3,2,0,1:T(8,128)(2,1)}, u32[]{:S(2)}, u32[]{:S(2)}) collective-permute-start(bf16[2,4,96,1152]{3,2,0,1:T(8,128)(2,1)} %bitcast.463), channel_id=1, source_target_pairs={{0,4},{4,0},{1,5},{5,1},{2,6},{6,2},{3,7},{7,3},{8,12},{12,8},{9,1... | collective-permute-start | bytes 5308424 | tf_op jit(solution)/shard_map/ppermute | solution.py:92
  1000.7 27.5 %collective-permute-start.66 = (bf16[128,1536]{1,0:T(8,128)(2,1)}, bf16[128,1536]{1,0:T(8,128)(2,1)}, u32[]{:S(2)}, u32[]{:S(2)}) collective-permute-start(bf16[128,1536]{1,0:T(8,128)(2,1)} %convolution_convert_fusion.20), channel_id=1, source_target_pairs={{0,8},{8,0},{1,9},{9,1},{2,10},{10,2},{3,11},{11,3},{4,12},{12,4},... | collective-permute-start | bytes 1179656 | tf_op jit(solution)/shard_map/ppermute | solution.py:83
  1000.8 27.4 %collective-permute-start.67 = (bf16[128,1536]{1,0:T(8,128)(2,1)}, bf16[128,1536]{1,0:T(8,128)(2,1)}, u32[]{:S(2)}, u32[]{:S(2)}) collective-permute-start(bf16[128,1536]{1,0:T(8,128)(2,1)} %convolution_convert_fusion.19), channel_id=1, source_target_pairs={{0,16},{16,0},{1,17},{17,1},{2,18},{18,2},{3,19},{19,3},{4,20},{20... | collective-permute-start | bytes 1179656 | tf_op jit(solution)/shard_map/ppermute | solution.py:86
  1032.4 20.4 %collective-permute-start.89 = (bf16[560,768]{1,0:T(8,128)(2,1)}, bf16[560,768]{1,0:T(8,128)(2,1)}, u32[]{:S(2)}, u32[]{:S(2)}) collective-permute-start(bf16[560,768]{1,0:T(8,128)(2,1)} %reduce-scatter.20.cloned.1.call-done), channel_id=1, source_target_pairs={{0,16},{16,0},{1,17},{17,1},{2,18},{18,2},{3,19},{19,3},{4,20},{20... | collective-permute-start | bytes 2580488 | tf_op jit(solution)/shard_map/ppermute | solution.py:86
  1055.0 27.4 %collective-permute-start.90 = (bf16[560,768]{1,0:T(8,128)(2,1)}, bf16[560,768]{1,0:T(8,128)(2,1)}, u32[]{:S(2)}, u32[]{:S(2)}) collective-permute-start(bf16[560,768]{1,0:T(8,128)(2,1)} %get-tuple-element.120), channel_id=1, source_target_pairs={{0,4},{4,0},{1,5},{5,1},{2,6},{6,2},{3,7},{7,3},{8,12},{12,8},{9,1... | collective-permute-start | bytes 2580488 | tf_op jit(solution)/shard_map/ppermute | solution.py:92
  1056.1 22.8 %collective-permute-start.87 = (bf16[2,96,2240]{2,1,0:T(8,128)(2,1)}, bf16[2,96,2240]{2,1,0:T(8,128)(2,1)}, u32[]{:S(2)}, u32[]{:S(2)}) collective-permute-start(bf16[2,96,2240]{2,1,0:T(8,128)(2,1)} %maximum_select_fusion.14), channel_id=1, source_target_pairs={{0,16},{16,0},{1,17},{17,1},{2,18},{18,2},{3,19},{19,3},{4,20},{20... | collective-permute-start | bytes 2580488 | tf_op jit(solution)/shard_map/ppermute | solution.py:86
  1066.5 27.1 %collective-permute-start.75 = (bf16[2,96,1152]{2,1,0:T(8,128)(2,1)}, bf16[2,96,1152]{2,1,0:T(8,128)(2,1)}, u32[]{:S(2)}, u32[]{:S(2)}) collective-permute-start(bf16[2,96,1152]{2,1,0:T(8,128)(2,1)} %maximum_select_fusion.23), channel_id=1, source_target_pairs={{0,16},{16,0},{1,17},{17,1},{2,18},{18,2},{3,19},{19,3},{4,20},{20... | collective-permute-start | bytes 1327112 | tf_op jit(solution)/shard_map/ppermute | solution.py:86
  1081.6 20.4 %collective-permute-start.81 = (bf16[2,96,1152]{2,1,0:T(8,128)(2,1)}, bf16[2,96,1152]{2,1,0:T(8,128)(2,1)}, u32[]{:S(2)}, u32[]{:S(2)}) collective-permute-start(bf16[2,96,1152]{2,1,0:T(8,128)(2,1)} %maximum_select_fusion.24), channel_id=1, source_target_pairs={{0,16},{16,0},{1,17},{17,1},{2,18},{18,2},{3,19},{19,3},{4,20},{20... | collective-permute-start | bytes 1327112 | tf_op jit(solution)/shard_map/ppermute | solution.py:86
  (225 other events, 2458.6 us)
Sparse Core Ops, SparseCore 0:
  20.4 42.9 all-gather.11
  65.5 40.2 all-gather.7
  108.0 21.7 all-gather.9
  131.3 22.2 all-gather.15
  155.6 93.9 all-gather.13
  251.6 78.3 all-gather.17
  331.6 67.7 all-gather.19
  653.7 19.9 reduce-scatter.15
  676.5 20.4 reduce-scatter.11
  699.8 68.5 reduce-scatter.7
  771.3 97.5 reduce-scatter.19
  900.7 63.7 reduce-scatter.17
  967.4 43.9 reduce-scatter.9
  1018.7 38.2 reduce-scatter.13

commit v2 on v1

v2 whole, which is shorter than its diff:
```python
import math
from types import SimpleNamespace

import jax
import jax.numpy as jnp
import numpy as np
from jax import lax
from jax.experimental import pallas as pl
from jax.experimental.pallas import tpu as pltpu
from jax.experimental.layout import Layout, with_layout_constraint
from jax.sharding import Mesh, PartitionSpec as P

HD = 128
EPS = 1e-06
F32 = jnp.float32
BF16 = jnp.bfloat16
SCALE = 1.0 / math.sqrt(HD)
SWAP = [(0, 1), (1, 0)]
ROWS = 16
FLOPS = 1_150_000_000
BYTES = 3_600_000


def rope_tables(grid_pos):
    pairs = HD // 2
    width = pairs // 3
    first = pairs - 2 * width
    index = np.arange(pairs)
    part = np.where(index < first, 0, np.where(index < first + width, 1, 2))
    offset = np.where(part == 0, index, np.where(part == 1, index - first, index - first - width))
    frequency = 10000.0 ** (-offset / np.where(part == 0, first, width))
    position = grid_pos.astype(F32)
    angles = 0.0
    for axis in range(3):
        lane = np.repeat(frequency * (part == axis), 2)
        angles = angles + position[axis][:, None] * jnp.asarray(lane, F32)[None, :]
    sign = np.where(np.arange(HD) % 2 == 0, -1.0, 1.0)
    return jnp.cos(angles), jnp.sin(angles) * jnp.asarray(sign, F32)[None, :]


def layer_norm(values):
    center = values - jnp.mean(values, -1, keepdims=True)
    inverse = lax.rsqrt(jnp.mean(center * center, -1, keepdims=True) + EPS)
    return center * inverse, inverse


def norm_backward(normed, inverse, grad_in):
    return inverse * (
        grad_in
        - jnp.mean(grad_in, -1, keepdims=True)
        - normed * jnp.mean(grad_in * normed, -1, keepdims=True)
    )


def mm(a, b):
    return lax.dot_general(a, b, (((a.ndim - 1,), (0,)), ((), ())), preferred_element_type=F32)


def mm_t(a, b):
    return lax.dot_general(a, b, (((a.ndim - 1,), (1,)), ((), ())), preferred_element_type=F32)


def rows_mm(a, w):
    return jnp.concatenate([mm(a, w[0]), mm(a, w[1])], -1)


def after(value, *done):
    return lax.optimization_barrier((value, done))[0]


def outer(a, b):
    lead = tuple(range(a.ndim - 1))
    return lax.dot_general(a, b, ((lead, lead), ((), ())), preferred_element_type=F32)


def column_chunks(total, size):
    return [(at, min(size, total - at)) for at in range(0, total, size)]


class Links:
    def __init__(self, named, stats, line):
        self.named = named
        self.used = 0
        self.started = []
        self.x, self.y, self.z = [lax.axis_index(n) for n in ("x", "y", "z")]
        self.seqs = lax.axis_size("z")
        barrier = pltpu.get_barrier_semaphore()
        peers = [{"x": 1 - self.x}, {"y": 1 - self.y}]
        if stats:
            peers.append({"x": 1 - self.x, "y": 1 - self.y})
        if line:
            peers += [{"z": (self.z + step) % self.seqs} for step in range(1, self.seqs)]
        for peer in peers:
            pl.semaphore_signal(
                barrier, inc=1, device_id=peer, device_id_type=pl.DeviceIdType.MESH
            )
        pl.semaphore_wait(barrier, len(peers))

    def clip_of(self, piece):
        return ((piece // 2 + self.x) % 2) * 2 + (piece % 2 + self.y) % 2

    def send(self, axis, src, dst):
        where = {a: 1 - lax.axis_index(a) for a in axis}
        index = self.used
        self.used += 1
        sems = self.named.sems
        copy = pltpu.make_async_remote_copy(
            src_ref=src,
            dst_ref=dst,
            send_sem=sems.at[0, index],
            recv_sem=sems.at[1, index],
            device_id=where,
            device_id_type=pl.DeviceIdType.MESH,
        )
        copy.start()
        self.started.append((None, copy))
        return copy

    def send_line(self, src, dst, to, slot, lane=0):
        sems = self.named.line
        copy = pltpu.make_async_remote_copy(
            src_ref=src,
            dst_ref=dst,
            send_sem=sems.at[0, lane, slot],
            recv_sem=sems.at[1, lane, self.z],
            device_id={"z": to},
            device_id_type=pl.DeviceIdType.MESH,
        )

        @pl.when(to != self.z)
        def _():
            copy.start()

        @pl.when(to == self.z)
        def _():
            dst[...] = src[...]

        self.started.append((to != self.z, copy))

    def wait_line(self, ref, source, lane=0):
        sems = self.named.line
        copy = pltpu.make_async_remote_copy(
            src_ref=ref,
            dst_ref=ref,
            send_sem=sems.at[0, lane, 0],
            recv_sem=sems.at[1, lane, source],
            device_id={"z": (self.z + 1) % self.seqs},
            device_id_type=pl.DeviceIdType.MESH,
        )

        @pl.when(source != self.z)
        def _():
            copy.wait_recv()

    def finish(self):
        for needed, copy in self.started:
            if needed is None:
                copy.wait_send()
            else:
                pl.when(needed)(copy.wait_send)


def split_rows(tokens):
    return ((tokens // 2 + ROWS - 1) // ROWS) * ROWS


def row_steps(tokens, body):
    @pl.loop(0, tokens // ROWS)
    def _(step):
        body(pl.ds(pl.multiple_of(step * ROWS, ROWS), ROWS), step)


def reduce_slice(links, refs, partial, middle, keep=None):
    mine, near, far, total = refs.mine, refs.near, refs.far, refs.total
    tokens = total.shape[0]
    half = split_rows(tokens)
    top, low = pl.ds(0, half), pl.ds(half, tokens - half)

    def store_low(slot):
        def store(columns, value):
            mine[slot, :, columns] = value.astype(BF16)

        return store

    def store_full(columns, value):
        total[:, columns] = value

    partial(refs, 3, store_low(2))
    far_x = links.send("x", mine.at[2, top], far.at[top])
    far_y = links.send("y", mine.at[2, low], far.at[low])
    partial(refs, 2, store_low(1))
    x_top = links.send("x", mine.at[1, top], near.at[1, top])
    partial(refs, 1, store_low(0))
    y_low = links.send("y", mine.at[0, low], near.at[0, low])
    far_x.wait_recv()
    mine[0, top] = (mine[0, top].astype(F32) + far[top].astype(F32)).astype(BF16)
    y_top = links.send("y", mine.at[0, top], near.at[0, top])
    far_y.wait_recv()
    mine[1, low] = (mine[1, low].astype(F32) + far[low].astype(F32)).astype(BF16)
    x_low = links.send("x", mine.at[1, low], near.at[1, low])
    partial(refs, 0, store_full)
    for copy in (x_top, y_low, y_top, x_low):
        copy.wait_recv()

    def body(rows, step):
        value = total[rows] + near[0, rows].astype(F32) + near[1, rows].astype(F32)
        sent = middle(refs, rows, step, value)
        if keep is not None:
            keep[0, rows] = sent

    row_steps(tokens, body)


def gather_begin(links, held):
    return links.send("x", held.at[0], held.at[2]), links.send("y", held.at[0], held.at[1])


def gather_relay(links, held, first):
    tokens = held.shape[1]
    half = split_rows(tokens)
    top, low = pl.ds(0, half), pl.ds(half, tokens - half)
    from_x, from_y = first
    from_x.wait_recv()
    far_top = links.send("y", held.at[2, top], held.at[3, top])
    from_y.wait_recv()
    far_low = links.send("x", held.at[1, low], held.at[3, low])
    return far_top, far_low


def gather_end(far):
    for copy in far:
        copy.wait_recv()


def gather_slice(links, refs, held, product, also=()):
    arrays = (held,) + tuple(also)
    first = [gather_begin(links, array) for array in arrays]
    product(refs, 0, held.at[0])
    far = [gather_relay(links, array, copies) for array, copies in zip(arrays, first)]
    product(refs, 1, held.at[1])
    product(refs, 2, held.at[2])
    for copies in far:
        gather_end(copies)
    product(refs, 3, held.at[3])


def sum_stats(links, refs):
    stat, other = refs.stat, refs.stats_in
    copies = [
        links.send("y", stat, other.at[0]),
        links.send("x", stat, other.at[1]),
        links.send("xy", stat, other.at[2]),
    ]
    for copy in copies:
        copy.wait_recv()
    for copy in copies:
        copy.wait_send()
    del links.started[-3:]
    for k in range(4):
        refs.stat_sum[k] = (
            stat[k] + other[0, k ^ 1] + other[1, k ^ 2] + other[2, k ^ 3]
        )


def to_row(column):
    size = column.shape[0]
    same = lax.broadcasted_iota(jnp.int32, (size, size), 0) == lax.broadcasted_iota(
        jnp.int32, (size, size), 1
    )
    return jnp.sum(jnp.where(same, column, 0.0), 0, keepdims=True)


def to_column(row):
    size = row.shape[1]
    same = lax.broadcasted_iota(jnp.int32, (size, size), 0) == lax.broadcasted_iota(
        jnp.int32, (size, size), 1
    )
    return jnp.sum(jnp.where(same, row, 0.0), 1, keepdims=True)


def run_kernel(name, cid, inputs, outputs, body, scratch, cost, stats=False, line=0):
    names_in, names_out = list(inputs), list(outputs)
    spaces = dict(sems=pltpu.SemaphoreType.DMA((2, 24)))
    if line:
        spaces.update(line=pltpu.SemaphoreType.DMA((2, line, 4)))
    if stats:
        spaces.update(
            stat=pltpu.VMEM((4, 8, 256), F32),
            stat_sum=pltpu.VMEM((4, 8, 256), F32),
            stats_in=pltpu.VMEM((3, 4, 8, 256), F32),
        )
    for key, (shape, dtype) in scratch.items():
        spaces[key] = pltpu.VMEM(shape, dtype)

    def kernel(*refs):
        named = SimpleNamespace(**dict(zip(names_in + names_out + list(spaces), refs)))
        links = Links(named, stats, line)
        body(links, named)
        links.finish()

    vmem = pl.BlockSpec(memory_space=pltpu.VMEM)
    result = pl.pallas_call(
        kernel,
        name=name,
        out_shape=[jax.ShapeDtypeStruct(*outputs[n]) for n in names_out],
        in_specs=[vmem] * len(names_in),
        out_specs=[vmem] * len(names_out),
        scratch_shapes=list(spaces.values()),
        cost_estimate=pl.CostEstimate(
            flops=cost * FLOPS, bytes_accessed=cost * BYTES, transcendentals=0
        ),
        compiler_params=pltpu.CompilerParams(
            collective_id=cid, has_side_effects=True, vmem_limit_bytes=60 * 1024 * 1024
        ),
    )(*[inputs[n] for n in names_in])
    return SimpleNamespace(**dict(zip(names_out, result)))


def reduce_scratch(tokens, dim):
    return dict(
        mine=((3, tokens, dim), BF16),
        near=((2, tokens, dim), BF16),
        far=((tokens, dim), BF16),
        total=((tokens, dim), F32),
    )


def add_rows(ref, index, value, step):
    @pl.when(step == 0)
    def _():
        ref[index] = jnp.zeros_like(ref[index])

    ref[index] += value[:8] + value[8:]


def fold_rows(value):
    return jnp.sum(value.reshape(value.shape[0] // 8, 8, value.shape[1]), 0)


def rows_partial(a, w):
    def partial(refs, k, store):
        piece = getattr(refs, a)[k]
        width = getattr(refs, w).shape[2]
        for half in range(2):
            for at, size in column_chunks(width, 384):
                store(
                    pl.ds(half * width + at, size),
                    mm(piece, getattr(refs, w)[half, :, pl.ds(at, size)]),
                )

    return partial


def turned_partial(a, w, size=256):
    def partial(refs, k, store):
        deep = getattr(refs, a).shape[2]

        @pl.loop(0, getattr(refs, w).shape[0] // size)
        def _(step):
            rows = pl.ds(pl.multiple_of(step * size, size), size)
            store(rows, mm_t(getattr(refs, a)[k], getattr(refs, w)[rows, pl.ds(0, deep)]))

    return partial


def rows_turned(piece, w):
    width = w.shape[2]
    return mm_t(piece[:, pl.ds(0, width)], w[0]) + mm_t(piece[:, pl.ds(width, width)], w[1])


def mm_l(a, b):
    return lax.dot_general(a, b, (((0,), (0,)), ((), ())), preferred_element_type=F32)


def swap_pairs(values):
    even = lax.broadcasted_iota(jnp.int32, values.shape, 1) % 2 == 0
    return jnp.where(even, pltpu.roll(values, HD - 1, 1), pltpu.roll(values, 1, 1))


def softmax(scores):
    weight = jnp.exp(scores - jnp.max(scores, -1, keepdims=True))
    return weight * (1.0 / jnp.sum(weight, -1, keepdims=True))


def head_at(h, base=0):
    return pl.ds(base + h * HD, HD)


def on_device(
    states, text_emb, grid_pos, time_mod, w_qkv, w_out, w_cross, w_crossout, w_up, w_down,
    attn_bias, qk_gain, norm_gain, norm_bias, up_bias, down_bias, modulation, out_grad,
):
    x, y, core = lax.axis_index("x"), lax.axis_index("y"), lax.axis_index("core")
    seqs = lax.axis_size("z")
    reps = lax.axis_size("rep")
    own_tokens, dim = states.shape
    tokens = -(-own_tokens // ROWS) * ROWS
    block = y * 2 + x
    pad = ((0, tokens - own_tokens), (0, 0))
    states_p = jnp.pad(states, pad)
    out_grad_p = jnp.pad(out_grad, pad)

    def from_y(a):
        return lax.ppermute(a, "y", SWAP)

    def from_x(a):
        return lax.ppermute(a, "x", SWAP)

    def from_xy(a):
        return lax.ppermute(a, ("x", "y"), [(i, 3 - i) for i in range(4)])

    def from_core(a):
        return lax.ppermute(a, "core", SWAP)

    def gather4(a):
        far, xs, ys = from_xy(a), from_x(a), from_y(a)
        return jnp.stack([a, ys, xs, far])

    def reduce4(term):
        far = from_xy(term(3).astype(BF16))
        xs = from_x(term(2).astype(BF16))
        ys = from_y(term(1).astype(BF16))
        return term(0) + ys.astype(F32) + xs.astype(F32) + far.astype(F32)

    def sum4(stat):
        far, xs, ys = from_xy(stat), from_x(stat), from_y(stat)
        return (
            stat
            + jnp.stack([ys[1], ys[0], ys[3], ys[2]])
            + jnp.stack([xs[2], xs[3], xs[0], xs[1]])
            + jnp.stack([far[3], far[2], far[1], far[0]])
        )

    def pick(v, blocks=4):
        return lax.dynamic_index_in_dim(
            v.reshape(v.shape[:-1] + (blocks, v.shape[-1] // blocks)), block, v.ndim - 1, False
        )

    def spread(v):
        hot = (jnp.arange(4) == block).astype(F32)
        full = v[..., None, :] * hot[:, None]
        return full.reshape(v.shape[:-1] + (4 * v.shape[-1],))

    def column_block(w, *done):
        rows, groups, width = w.shape[0], w.shape[1], w.shape[2] // 4
        mine = lax.dynamic_index_in_dim(w.reshape(rows, groups, 2, 2, width), x, 3, False)
        keep = lax.dynamic_index_in_dim(mine, y, 2, False).reshape(rows, groups * width)
        send = lax.dynamic_index_in_dim(mine, 1 - y, 2, False).reshape(rows, groups * width)
        recv = from_y(send)
        both = jnp.where(y == 0, jnp.stack([keep, recv]), jnp.stack([recv, keep]))
        full = lax.all_gather(after(both, *done), ("core", "z"), axis=1, tiled=True)
        return full.reshape(-1, groups * width)

    def row_block(w, *done):
        rows, half = w.shape[0], w.shape[1] // 2
        keep = lax.dynamic_slice_in_dim(w, core * half, half, 1)
        recv = from_core(lax.dynamic_slice_in_dim(w, (1 - core) * half, half, 1))
        mine = jnp.where(core == x, keep, recv)
        full = lax.all_gather(after(mine, *done), ("core", "z"), axis=0, tiled=True)
        return full.reshape(2, seqs * rows, half)

    def over_reps(a):
        return lax.psum(a, "rep") if reps > 1 else a

    def column_core(g):
        g = g.astype(BF16).reshape(2, 2, seqs, -1, g.shape[1])
        keep = lax.dynamic_index_in_dim(g, core, 1, False)
        recv = from_core(lax.dynamic_index_in_dim(g, 1 - core, 1, False))
        both = (keep.astype(F32) + recv.astype(F32)).astype(BF16)
        return both.transpose(1, 0, 2, 3).reshape(-1, g.shape[4])

    def row_core(g):
        half = g.shape[1] // 2
        g = g.astype(BF16)
        keep = lax.dynamic_slice_in_dim(g, core * half, half, 1)
        recv = from_core(lax.dynamic_slice_in_dim(g, (1 - core) * half, half, 1))
        return (keep.astype(F32) + recv.astype(F32)).astype(BF16)

    def scatter_z(a):
        return over_reps(lax.psum_scatter(a, "z", scatter_dimension=0, tiled=True))

    def column_done(part, groups):
        width = part.shape[1] // groups
        part = part.reshape(2, -1, groups * width)
        keep = lax.dynamic_index_in_dim(part, y, 0, False)
        recv = from_y(lax.dynamic_index_in_dim(part, 1 - y, 0, False))
        ours = jnp.where(y == 0, jnp.stack([keep, recv]), jnp.stack([recv, keep]))
        theirs = from_x(ours)
        rows = ours.shape[1]
        ours = ours.reshape(2, rows, groups, width)
        theirs = theirs.reshape(2, rows, groups, width)
        full = jnp.where(x == 0, jnp.stack([ours, theirs], 1), jnp.stack([theirs, ours], 1))
        return full.transpose(2, 3, 0, 1, 4).reshape(rows, groups, 4 * width).astype(F32)

    def row_done(part):
        other = from_x(part)
        ours = jnp.where(core == x, part, other)
        theirs = from_core(jnp.where(core == x, other, part))
        full = jnp.where(
            core == 0,
            jnp.concatenate([ours, theirs], 1),
            jnp.concatenate([theirs, ours], 1),
        )
        return full.astype(F32)

    mods = modulation + time_mod[0]
    shift1, scale1, gate1, shift2, scale2, gate2 = [mods[i] for i in range(6)]

    def vectors(*rows):
        return jnp.stack(rows + (jnp.zeros_like(rows[0]),) * (8 - len(rows)))

    full_qkv = column_block(w_qkv)
    full_out = row_block(w_out, full_qkv)
    full_cross = column_block(w_cross, full_qkv)
    text_z = lax.all_gather(after(text_emb, full_qkv), "z", axis=0, tiled=True)
    full_crossout = row_block(w_crossout, full_qkv)
    full_up = column_block(w_up[:, None, :], full_qkv)
    full_down = row_block(w_down, full_qkv)
    bias = pick(attn_bias)
    gain = pick(qk_gain)
    width = bias.shape[1]
    heads = width // HD
    hidden_width = full_up.shape[1]
    own_tables = jnp.pad(jnp.concatenate(rope_tables(grid_pos), 1), pad)
    d_ffnout = (out_grad_p * gate2).astype(BF16)

    def rms_scale(v):
        return lax.rsqrt(v / dim + EPS)[..., None]

    wide = ((tokens, dim), F32)
    held = ((4, tokens, dim), BF16)
    head_block = ((4, tokens, width), F32)

    blocks3 = 3 * width
    clip_rows = seqs * tokens

    def middle(refs, rows):
        normed, _ = layer_norm(refs.states[rows])
        vec = refs.vec
        return (normed * vec[0:1] + vec[1:2]).astype(BF16)

    def body(links, refs):
        refs.stat[...] = jnp.zeros_like(refs.stat)

        def rows_in(rows, step):
            refs.held[0, rows] = middle(refs, rows)

        def send_heads(k, columns, lane):
            links.send_line(
                refs.sent.at[k, :, columns], refs.packed.at[links.z, :, columns],
                links.clip_of(k), k, lane,
            )

        early, late = pl.ds(2 * width, width), pl.ds(0, 2 * width)

        def product(refs, k, piece):
            pre = mm(piece[...], refs.w[:, early]) + refs.bias[0:1, early]
            refs.sent[k, :, early] = pre.astype(BF16)
            send_heads(k, early, 0)
            for part in range(2):
                columns = pl.ds(part * width, width)
                pre = mm(piece[...], refs.w[:, columns]) + refs.bias[0:1, columns]
                refs.unit[k, :, columns] = pre
                square = jnp.sum(pre * pre, -1, keepdims=True)
                refs.stat[k, pl.ds(part, 1), pl.ds(0, tokens)] = to_row(square)

        refs.tables[0] = refs.own_tables[...]
        refs.grads[0] = refs.own_grads[...]
        row_steps(tokens, rows_in)
        gather_slice(links, refs, refs.held, product, (refs.tables,))
        sum_stats(links, refs)
        refs.inv[...] = lax.rsqrt(refs.stat_sum[...] / dim + EPS)
        first = gather_begin(links, refs.grads)
        for k in (3, 2, 1, 0):
            cosine, sine = refs.tables[k, :, pl.ds(0, HD)], refs.tables[k, :, pl.ds(HD, HD)]
            for part in range(2):
                inverse = to_column(refs.inv[k, pl.ds(part, 1), pl.ds(0, tokens)])
                for h in range(heads):
                    at = head_at(h, part * width)
                    unit = refs.unit[k, :, at] * inverse
                    refs.unit[k, :, at] = unit
                    scaled = unit * refs.gain[pl.ds(part, 1), head_at(h)]
                    turned = scaled * cosine + swap_pairs(scaled) * sine
                    refs.sent[k, :, at] = turned.astype(BF16)
            send_heads(k, late, 1)
        gather_end(gather_relay(links, refs.grads, first))
        for source in range(seqs):
            links.wait_line(refs.packed.at[source, :, early], source, 0)
            links.wait_line(refs.packed.at[source, :, late], source, 1)

    gains8 = jnp.pad(gain, ((0, 4), (0, 0)))
    first = run_kernel(
        "self_in", 1,
        dict(
            states=states_p, vec=vectors(1.0 + scale1, shift1), w=full_qkv,
            bias=jnp.broadcast_to(bias[:3].reshape(1, -1), (8, blocks3)),
            gain=gains8, own_tables=own_tables, own_grads=d_ffnout,
        ),
        dict(
            held=held, unit=((4, tokens, 2 * width), F32), inv=((4, 8, 256), F32),
            packed=((seqs, tokens, blocks3), BF16), grads=held,
            tables=((4, tokens, 2 * HD), F32),
        ),
        body, dict(sent=((4, tokens, blocks3), BF16)), stats=True, line=2, cost=70,
    )
    x_self, self_unit, self_inv, packed = first.held, first.unit, first.inv, first.packed
    g_ffn, tables = first.grads, first.tables

    texts = text_z.shape[0]
    text_z = with_layout_constraint(after(text_z, packed), Layout((0, 1)))
    text_pieces = [text_z, from_y(text_z), from_x(text_z), from_xy(text_z)]

    def masked_scores(q, keys):
        scores = mm_t(q, keys) * SCALE
        column = lax.broadcasted_iota(jnp.int32, scores.shape, 1)
        return jnp.where(column % tokens < own_tokens, scores, -1e30)

    def middle(refs, rows, step, total):
        vec = refs.vec
        branch = total + vec[0:1]
        refs.branch[rows] = branch
        joined = refs.states[rows] + branch * vec[1:2]
        refs.joined[rows] = joined
        normed, _ = layer_norm(joined)
        return (normed * vec[2:3] + vec[3:4]).astype(BF16)

    def product(refs, k, piece):
        pre = mm(piece[...], refs.w2[:, pl.ds(0, width)]) + refs.bias[0:1]
        refs.unit[k] = pre
        refs.stat[k, pl.ds(0, 1), pl.ds(0, tokens)] = to_row(jnp.sum(pre * pre, -1, keepdims=True))

    def body(links, refs):
        refs.stat[...] = jnp.zeros_like(refs.stat)
        packed = refs.packed
        for turn in (1, 2, 3, 0):
            to = (links.z + turn) % seqs
            for h in range(heads):
                keys = packed[:, :, head_at(h, width)].reshape(clip_rows, HD)
                values = packed[:, :, head_at(h, 2 * width)].reshape(clip_rows, HD)
                probs = softmax(masked_scores(packed[to, :, head_at(h)], keys))
                refs.outs[turn, :, head_at(h)] = mm(probs.astype(BF16), values).astype(BF16)
            links.send_line(
                refs.outs.at[turn], refs.mixed.at[links.clip_of(links.z)], to, turn
            )
        reduce_product = rows_partial("mixed", "w")

        def partial(refs, k, store):
            links.wait_line(refs.mixed.at[k], links.clip_of(k))
            reduce_product(refs, k, store)

        reduce_slice(links, refs, partial, middle, refs.held)
        gather_slice(links, refs, refs.held, product)
        sum_stats(links, refs)
        refs.inv[...] = lax.rsqrt(refs.stat_sum[...] / dim + EPS)

        @pl.loop(0, 4)
        def _(k):
            inverse = to_column(refs.inv[k, pl.ds(0, 1), pl.ds(0, tokens)])
            refs.unit[k] = refs.unit[k] * inverse

    second = run_kernel(
        "self_attend", 2,
        dict(
            packed=packed, w=full_out, states=states_p,
            vec=vectors(attn_bias[3], gate1, norm_gain, norm_bias),
            w2=full_cross, bias=jnp.broadcast_to(bias[4:5], (8, width)),
        ),
        dict(
            mixed=((4, tokens, width), BF16), branch=wide, joined=wide, held=held,
            unit=head_block, inv=((4, 8, 256), F32),
        ),
        body,
        dict(outs=((seqs, tokens, width), BF16), **reduce_scratch(tokens, dim)),
        stats=True, line=1,
        cost=80,
    )
    mixed, branch, after_self = second.mixed, second.branch, second.joined
    x_cross, cq_unit, cq_inv = second.held, second.unit, second.inv

    x_text = jnp.stack(after(text_pieces, cq_inv))
    text_proj = mm(x_text, full_cross[:, width:])
    ck_pre = text_proj[..., :width] + bias[5]
    cross_v = (text_proj[..., width:] + bias[6]).astype(BF16)
    ck_inv = rms_scale(sum4(jnp.sum(ck_pre * ck_pre, -1)))
    ck_unit = ck_pre * ck_inv
    cross_k = (ck_unit * gain[3]).astype(BF16)
    text_kv = jnp.concatenate([cross_k, cross_v], -1)

    def cross_heads(refs, k, h):
        q = (refs.unit[k, :, head_at(h)] * refs.gain[2:3, head_at(h)]).astype(BF16)
        keys = refs.kv[k, :, head_at(h)]
        values = refs.kv[k, :, head_at(h, width)]
        return q, keys, values, softmax(mm_t(q, keys) * SCALE)

    def middle(refs, rows, step, total):
        vec = refs.vec
        joined = refs.start[rows] + (total + vec[0:1])
        refs.joined[rows] = joined
        normed, _ = layer_norm(joined)
        return (normed * vec[1:2] + vec[2:3]).astype(BF16)

    root = math.sqrt(2.0 / math.pi)

    def product(refs, k, piece):
        for at, size in column_chunks(hidden_width, 640):
            columns = pl.ds(at, size)
            pre = mm(piece[...], refs.w2[:, columns]) + refs.bias[0:1, columns]
            bent = jnp.tanh(root * (pre + 0.044715 * pre * pre * pre))
            refs.hidden[k, :, columns] = (0.5 * pre * (1.0 + bent)).astype(BF16)
            refs.slope[k, :, columns] = 0.5 * (1.0 + bent) + 0.5 * pre * (
                1.0 - bent * bent
            ) * root * (1.0 + 3.0 * 0.044715 * pre * pre)

    def body(links, refs):
        reduce_product = rows_partial("mix", "w")

        def partial(refs, k, store):
            for h in range(heads):
                _, _, values, probs = cross_heads(refs, k, h)
                refs.mix[k, :, head_at(h)] = mm(probs.astype(BF16), values).astype(BF16)
            reduce_product(refs, k, store)

        reduce_slice(links, refs, partial, middle, refs.held)
        gather_slice(links, refs, refs.held, product)

    third = run_kernel(
        "cross_attend", 3,
        dict(
            unit=cq_unit, gain=gains8, kv=text_kv,
            w=full_crossout, start=after_self,
            vec=vectors(attn_bias[7], 1.0 + scale2, shift2),
            w2=full_up,
            bias=jnp.broadcast_to(pick(up_bias)[None], (8, hidden_width)),
        ),
        dict(
            mix=((4, tokens, width), BF16), joined=wide, held=held,
            hidden=((4, tokens, hidden_width), BF16),
            slope=((4, tokens, hidden_width), F32),
        ),
        body, reduce_scratch(tokens, dim),
        cost=60,
    )
    cross_mix, after_cross, x_ffn, hidden = third.mix, third.joined, third.held, third.hidden

    down_core = row_core(outer(hidden, g_ffn))
    down_part = scatter_z(down_core)
    inner_partial = turned_partial("d_hpre", "w_up")

    def ffn_partial(refs, k, store):
        w = refs.w_down
        deep = w.shape[2]
        for at, size in column_chunks(hidden_width, 640):
            columns = pl.ds(at, size)
            grad = mm_t(refs.g[k, :, pl.ds(0, deep)], w[0, columns])
            grad = grad + mm_t(refs.g[k, :, pl.ds(deep, deep)], w[1, columns])
            refs.d_hpre[k, :, columns] = (grad * refs.slope[k, :, columns]).astype(BF16)
        inner_partial(refs, k, store)

    def middle(refs, rows, step, total):
        normed, inverse = layer_norm(refs.joined[rows])
        d_cross = refs.top[rows] + norm_backward(normed, inverse, total * refs.vec[0:1])
        refs.d_cross[rows] = d_cross
        low = d_cross.astype(BF16)
        add_rows(refs.sums, 0, total, step)
        add_rows(refs.sums, 1, total * normed, step)
        add_rows(refs.sums, 2, low.astype(F32), step)
        return low

    def product(refs, k, piece):
        refs.d_mix[k] = rows_turned(piece, refs.w2).astype(BF16)

    def body(links, refs):
        reduce_slice(links, refs, ffn_partial, middle, refs.held)
        gather_slice(links, refs, refs.held, product)

    fourth = run_kernel(
        "ffn_back", 4,
        dict(
            g=after(g_ffn, down_core), w_down=full_down, slope=third.slope, w_up=full_up,
            joined=after_cross, top=out_grad_p, vec=vectors(1.0 + scale2),
            w2=full_crossout,
        ),
        dict(
            d_hpre=((4, tokens, hidden_width), BF16), d_cross=wide, held=held,
            d_mix=((4, tokens, width), BF16), sums=((3, 8, dim), F32),
        ),
        body, reduce_scratch(tokens, dim),
        cost=72,
    )
    d_hpre, d_cross, g_cross, d_cmix = fourth.d_hpre, fourth.d_cross, fourth.held, fourth.d_mix
    sums4 = jnp.sum(fourth.sums, 1)
    up_core = column_core(outer(x_ffn, d_hpre))
    up_part = scatter_z(up_core)

    def rms_back(grad, unit, inverse, mean):
        return inverse * (grad - unit * mean)

    def middle(refs, rows, step, total):
        normed, inverse = layer_norm(refs.joined[rows])
        vec = refs.vec
        d_self = refs.top[rows] + norm_backward(normed, inverse, total * vec[0:1])
        refs.d_self[rows] = d_self
        low = (d_self * vec[1:2]).astype(BF16)
        add_rows(refs.sums, 0, total * normed, step)
        add_rows(refs.sums, 1, total, step)
        add_rows(refs.sums, 2, low.astype(F32), step)
        add_rows(refs.sums, 3, d_self * refs.branch[rows], step)
        return low

    def body(links, refs):
        refs.stat[...] = jnp.zeros_like(refs.stat)
        refs.gains[...] = jnp.zeros_like(refs.gains)

        @pl.loop(0, 4)
        def _(k):
            square = jnp.zeros((tokens, 1), F32)
            for h in range(heads):
                q, keys, values, probs = cross_heads(refs, k, h)
                d_mix = refs.d_mix[k, :, head_at(h)]
                d_probs = mm_t(d_mix, values)
                delta = jnp.sum(probs * d_probs, -1, keepdims=True)
                d_scores = (probs * (d_probs - delta)).astype(BF16)
                d_q = mm(d_scores, keys) * SCALE
                refs.d_kv[k, :, head_at(h)] = (mm_l(d_scores, q) * SCALE).astype(BF16)
                refs.d_kv[k, :, head_at(h, width)] = mm_l(probs.astype(BF16), d_mix).astype(BF16)
                unit = refs.unit[k, :, head_at(h)]
                refs.gains[:, head_at(h)] += fold_rows(d_q * unit)
                d_q = d_q * refs.gain[2:3, head_at(h)]
                refs.d_unit[k, :, head_at(h)] = d_q
                square = square + jnp.sum(d_q * unit, -1, keepdims=True)
            refs.stat[k, pl.ds(0, 1), pl.ds(0, tokens)] = to_row(square)

        sum_stats(links, refs)

        @pl.loop(0, 4)
        def _(k):
            inverse = to_column(refs.inv[k, pl.ds(0, 1), pl.ds(0, tokens)])
            mean = to_column(refs.stat_sum[k, pl.ds(0, 1), pl.ds(0, tokens)]) / dim
            refs.d_pre[k] = rms_back(refs.d_unit[k], refs.unit[k], inverse, mean).astype(BF16)

        def product(refs, k, piece):
            refs.outs[k] = rows_turned(piece, refs.w2).astype(BF16)
            links.send_line(
                refs.outs.at[k], refs.d_heads.at[links.z], links.clip_of(k), k
            )

        reduce_slice(links, refs, turned_partial("d_pre", "w"), middle, refs.held)
        gather_slice(links, refs, refs.held, product)
        for source in range(seqs):
            links.wait_line(refs.d_heads.at[source], source)

    fifth = run_kernel(
        "cross_back", 5,
        dict(
            unit=cq_unit, inv=cq_inv, gain=gains8, kv=text_kv,
            d_mix=after(d_cmix, up_core, down_part),
            w=full_cross, joined=after_self, top=d_cross, branch=branch,
            vec=vectors(norm_gain, gate1), w2=full_out,
        ),
        dict(
            d_pre=((4, tokens, width), BF16), d_kv=((4, texts, 2 * width), BF16),
            gains=((8, width), F32), d_self=wide, held=held,
            d_heads=((seqs, tokens, width), BF16), sums=((4, 8, dim), F32),
        ),
        body,
        dict(
            d_unit=((4, tokens, width), F32), outs=((4, tokens, width), BF16),
            **reduce_scratch(tokens, dim),
        ),
        stats=True, line=1,
        cost=80,
    )
    d_cq, d_self, g_self, d_heads = fifth.d_pre, fifth.d_self, fifth.held, fifth.d_heads
    cq_gain = jnp.sum(fifth.gains, 0)
    sums5 = jnp.sum(fifth.sums, 1)
    d_ckv = after(fifth.d_kv, up_part).reshape(4, seqs, -1, 2 * width).transpose(1, 0, 2, 3)
    d_ckv = lax.psum_scatter(d_ckv, "z", scatter_dimension=0, tiled=True)[0]
    outproj_core = row_core(outer(mixed, g_self))
    crossout_core = row_core(outer(after(cross_mix, d_self), g_cross))

    d_ckn = d_ckv[..., :width].astype(F32)
    d_cv = d_ckv[..., width:]
    zpos = lax.axis_index("z")
    own = texts // seqs
    ck_unit = lax.dynamic_slice_in_dim(ck_unit, zpos * own, own, 1)
    ck_inv = lax.dynamic_slice_in_dim(ck_inv, zpos * own, own, 1)
    x_text = lax.dynamic_slice_in_dim(x_text, zpos * own, own, 1)
    d_cku = d_ckn * gain[3]
    ck_stat = sum4(jnp.sum(d_cku * ck_unit, -1)) / dim
    d_ck = rms_back(d_cku, ck_unit, ck_inv, ck_stat[..., None]).astype(BF16)
    ck_gain = jnp.sum(d_ckn * ck_unit, (0, 1))
    d_text = jnp.concatenate([d_ck, d_cv], -1)
    text_grad = reduce4(lambda k: mm_t(d_text[k], full_cross[:, width:]))
    cross_core = column_core(jnp.concatenate([outer(x_cross, d_cq), outer(x_text, d_text)], 1))
    cross_part = scatter_z(cross_core)
    outproj_part = scatter_z(after(outproj_core, cross_core))
    crossout_part = scatter_z(after(crossout_core, cross_core))

    def middle(refs, rows, step, total):
        normed, inverse = layer_norm(refs.states[rows])
        refs.out[rows] = refs.top[rows] + norm_backward(
            normed, inverse, total * refs.vec[0:1]
        )
        add_rows(refs.sums, 0, total, step)
        add_rows(refs.sums, 1, total * normed, step)

    def body(links, refs):
        refs.stat[...] = jnp.zeros_like(refs.stat)
        refs.gains[...] = jnp.zeros_like(refs.gains)
        packed, d_heads = refs.packed, refs.d_heads
        for h in range(heads):
            refs.d_keys[...] = jnp.zeros_like(refs.d_keys)
            refs.d_values[...] = jnp.zeros_like(refs.d_values)

            @pl.loop(0, seqs)
            def _(i):
                keys = packed[:, :, head_at(h, width)].reshape(clip_rows, HD)
                values = packed[:, :, head_at(h, 2 * width)].reshape(clip_rows, HD)
                q = packed[i, :, head_at(h)]
                d_mix = d_heads[i, :, head_at(h)]
                probs = softmax(masked_scores(q, keys))
                d_probs = mm_t(d_mix, values)
                delta = jnp.sum(probs * d_probs, -1, keepdims=True)
                d_scores = (probs * (d_probs - delta)).astype(BF16)
                refs.outs[h, i, :, pl.ds(0, HD)] = (mm(d_scores, keys) * SCALE).astype(BF16)
                refs.d_keys[...] += mm_l(d_scores, q)
                refs.d_values[...] += mm_l(probs.astype(BF16), d_mix)

            for i in range(seqs):
                rows = pl.ds(i * tokens, tokens)
                refs.outs[h, i, :, pl.ds(HD, HD)] = (refs.d_keys[rows] * SCALE).astype(BF16)
                refs.outs[h, i, :, pl.ds(2 * HD, HD)] = refs.d_values[rows].astype(BF16)
            for step in range(seqs):
                to = (links.z + 1 + step) % seqs
                links.send_line(
                    refs.outs.at[h, to],
                    refs.arrived.at[h, links.clip_of(links.z)],
                    to, step, h,
                )
        for k in range(4):
            for h in range(heads):
                links.wait_line(refs.arrived.at[h, k], links.clip_of(k), h)

        @pl.loop(0, 4)
        def _(k):
            for part in range(2):
                square = jnp.zeros((tokens, 1), F32)
                for h in range(heads):
                    at = head_at(h, part * width)
                    grad = refs.arrived[h, k, :, pl.ds(part * HD, HD)].astype(F32)
                    grad = grad * refs.tables[k, :, pl.ds(0, HD)] - swap_pairs(grad) * refs.tables[k, :, pl.ds(HD, HD)]
                    unit = refs.unit[k, :, at]
                    refs.gains[part, :, head_at(h)] += fold_rows(grad * unit)
                    grad = grad * refs.gain[pl.ds(part, 1), head_at(h)]
                    refs.d_unit[k, :, at] = grad
                    square = square + jnp.sum(grad * unit, -1, keepdims=True)
                refs.stat[k, pl.ds(part, 1), pl.ds(0, tokens)] = to_row(square)
            for h in range(heads):
                refs.d_qkv[k, :, head_at(h, 2 * width)] = refs.arrived[
                    h, k, :, pl.ds(2 * HD, HD)
                ]

        sum_stats(links, refs)

        @pl.loop(0, 4)
        def _(k):
            for part in range(2):
                row = (k, pl.ds(part, 1), pl.ds(0, tokens))
                inverse = to_column(refs.inv[row])
                mean = to_column(refs.stat_sum[row]) / dim
                at = pl.ds(part * width, width)
                refs.d_qkv[k, :, at] = rms_back(
                    refs.d_unit[k, :, at], refs.unit[k, :, at], inverse, mean
                ).astype(BF16)

        reduce_slice(links, refs, turned_partial("d_qkv", "w"), middle)

    sixth = run_kernel(
        "self_back", 6,
        dict(
            packed=packed, d_heads=d_heads, unit=self_unit, inv=self_inv,
            gain=gains8, tables=tables, w=full_qkv, states=states_p,
            top=after(d_self, crossout_core, outproj_core, cross_core), vec=vectors(1.0 + scale1),
        ),
        dict(
            d_qkv=((4, tokens, blocks3), BF16), gains=((2, 8, width), F32),
            out=wide, sums=((2, 8, dim), F32),
        ),
        body,
        dict(
            outs=((heads, seqs, tokens, 3 * HD), BF16),
            arrived=((heads, 4, tokens, 3 * HD), BF16),
            d_keys=((clip_rows, HD), F32), d_values=((clip_rows, HD), F32),
            d_unit=((4, tokens, 2 * width), F32),
            **reduce_scratch(tokens, dim),
        ),
        stats=True, line=heads,
        cost=120,
    )
    d_qkv = sixth.d_qkv
    d_qkv_sum = jnp.sum(d_qkv.astype(F32), (0, 1))
    q_gain, k_gain = jnp.sum(sixth.gains, 1)
    states_grad = sixth.out[:own_tokens]
    sums6 = jnp.sum(sixth.sums, 1)
    qkv_core = column_core(outer(x_self, d_qkv))
    qkv_part = scatter_z(qkv_core)

    ffn_out = reduce4(lambda k: rows_mm(hidden[k], full_down)) + down_bias
    block_out = (after_cross + ffn_out * gate2)[:own_tokens]
    up_grad = column_done(up_part, 1)[:, 0]
    down_grad = row_done(down_part)
    qkv_grad = column_done(qkv_part, 3)
    outproj_grad = row_done(outproj_part)
    cross_grad = column_done(cross_part, 3)
    crossout_grad = row_done(crossout_part)

    def column_sum(v):
        return jnp.sum(v.astype(F32), tuple(range(v.ndim - 1)))

    def over_z(v):
        v = v + lax.ppermute(v, "z", [(i, i ^ 1) for i in range(seqs)])
        return v + lax.ppermute(v, "z", [(i, i ^ 2) for i in range(seqs)])

    def over_clips(v):
        v = v + from_core(v)
        v = v + from_x(v)
        v = v + from_y(v)
        return over_reps(v)

    early = jnp.stack(
        [
            sums4[0],
            sums4[1],
            column_sum(out_grad_p * ffn_out),
            spread(column_sum(d_cq)),
            spread(column_sum(d_ck)),
            spread(column_sum(d_cv)),
            sums4[2],
            spread(cq_gain),
            spread(ck_gain),
            sums5[0],
            sums5[1],
            column_sum(d_ffnout),
            sums5[2],
            sums5[3],
        ]
    )
    upbias = over_clips(over_z(spread(column_sum(d_hpre))))
    early_clip = over_z(early)
    early_all = over_clips(early_clip)
    late = jnp.stack(
        [
            sums6[0],
            sums6[1],
            spread(d_qkv_sum[:width]),
            spread(d_qkv_sum[width : 2 * width]),
            spread(d_qkv_sum[2 * width :]),
            spread(q_gain),
            spread(k_gain),
        ]
    )
    late_clip = over_z(late)
    late_all = over_clips(late_clip)

    def mod_rows(e, l):
        return jnp.stack([l[0], l[1], e[13], e[0], e[1], e[2]])

    time_grad = mod_rows(early_clip, late_clip)[None]
    mod_grad = mod_rows(early_all, late_all)
    bias_grad = jnp.stack(
        [late_all[2], late_all[3], late_all[4], early_all[12]] + [early_all[i] for i in (3, 4, 5, 6)]
    )
    gain_grad = jnp.stack([late_all[5], late_all[6], early_all[7], early_all[8]])
    return (
        block_out, states_grad, text_grad, time_grad, qkv_grad, outproj_grad, cross_grad,
        crossout_grad, up_grad, down_grad, bias_grad, gain_grad, early_all[9], early_all[10],
        upbias, early_all[11], mod_grad,
    )


def solution(mesh):
    reps, shards, seqs = mesh.shape["replica"], mesh.shape["shard"], mesh.shape["seq"]
    fine = Mesh(
        mesh.devices.reshape(reps // 2, 2, shards // 2, 2, seqs), ("rep", "x", "y", "core", "z")
    )
    tokens = P(("rep", "x", "y", "core", "z"), None)
    clips = P(("rep", "x", "y", "core"), None, None)
    rows2 = P(("y", "core", "z"), None)
    rows3 = P(("y", "core", "z"), None, None)
    return jax.shard_map(
        on_device,
        mesh=fine,
        in_specs=(
            tokens, tokens, P(None, ("rep", "x", "y", "core", "z")), clips,
            rows3, rows2, rows3, rows2, rows2, rows2,
            P(), P(), P(), P(), P(), P(), P(), tokens,
        ),
        out_specs=(
            tokens, tokens, tokens, clips,
            rows3, rows2, rows3, rows2, rows2, rows2,
            P(), P(), P(), P(), P(), P(), P(),
        ),
        check_vma=False,
    )
```

time: 1130 us -> 1040 us (0.920)
  Pallas kernels: 0 us -> 555 us
  waiting for transfers between devices: 484 us -> 152 us
  local copies, waits for them, and re-layouts: 206 us -> 89.5 us
  matrix products: 188 us -> 76.3 us
  starting transfers between devices: 119 us -> 57.2 us
  other arithmetic: 99.6 us -> 83.2 us
    pallas_call x0 -> x6, Pallas kernels: none -> 555 us  [run_kernel(): pl.pallas_call(kernel, name=name, out_shape=[jax.ShapeDtypeStruct(*output...]
    all_to_all x4 -> x0, waiting for transfers between devices: 105 us -> none  [heads_swap(): return lax.all_to_all(a, 'z', split_axis=0, concat_axis=0, tiled=True)]
    ppermute x21 -> x5, waiting for transfers between devices: 97.4 us -> 0.01 us  [from_xy(): return lax.ppermute(a, ('x', 'y'), [(i, 3 - i) for i in range(4)])]
    ppermute x30 -> x14, waiting for transfers between devices: 112 us -> 38.6 us  [from_y(): return lax.ppermute(a, 'y', SWAP)]
    reshape x13 -> x1, local copies, waits for them, and re-layouts: 66.8 us -> 3.83 us  [on_device(): after(fifth.d_kv, up_part).reshape(4, seqs, -1, 2 * width)]
    dot_general x19 -> x4, matrix products: 71.1 us -> 12.3 us  [mm_t(): lax.dot_general(a, b, (((a.ndim - 1,), (1,)), ((), ())), preferred_elemen...]
    ppermute x3, waiting for transfers between devices: 61.2 us -> 3.58 us  [over_z(): v = v + lax.ppermute(v, 'z', [(i, i ^ 1) for i in range(seqs)])]
    ppermute x3, waiting for transfers between devices: 39.9 us -> 3.39 us  [over_z(): return v + lax.ppermute(v, 'z', [(i, i ^ 2) for i in range(seqs)])]
  transfers between devices with their start and end apart: 120 -> 68, of which waited for: 67 -> 25; matrix products, arithmetic and copies ran while one was open for 36% -> 22% of each run, Pallas kernels for 0% -> 54%
where the time goes in v2:
time: 1040 us; the launch traced here: 1030 us
  Pallas kernels  555 us (53%)
  waiting for transfers between devices  152 us (15%)
  local copies, waits for them, and re-layouts  89.5 us (9%)
  other arithmetic  83.2 us (8%)
  matrix products  76.3 us (7%)
  starting transfers between devices  57.2 us (6%)
  between operations  15.7 us (2%)
    pallas_call x6, Pallas kernels, run_kernel(): pl.pallas_call(kernel, name=name, out_shape=[jax.ShapeDtypeStruct(*output...  555 us
    all_gather x3, waiting for transfers between devices, column_block(): full = lax.all_gather(after(both, *done), ('core', 'z'), axis=1, tiled=True)  43 us
    dot_general x7, matrix products, outer(): lax.dot_general(a, b, ((lead, lead), ((), ())), preferred_element_type=F32)  39.3 us
    ppermute x14, waiting for transfers between devices, from_y(): return lax.ppermute(a, 'y', SWAP)  38.6 us
    ppermute x14, waiting for transfers between devices, from_x(): return lax.ppermute(a, 'x', SWAP)  26.2 us
    dot_general x9, matrix products, mm(): lax.dot_general(a, b, (((a.ndim - 1,), (0,)), ((), ())), preferred_elemen...  24.8 us
    reduce_scatter x1, waiting for transfers between devices, on_device(): d_ckv = lax.psum_scatter(d_ckv, 'z', scatter_dimension=0, tiled=True)[0]  22.9 us
    ppermute x14, starting transfers between devices, from_y(): return lax.ppermute(a, 'y', SWAP)  21.5 us
  transfers between devices with their start and end apart: 68, of which 25 were waited for; matrix products, arithmetic and copies ran while one was open for 22% of the time, Pallas kernels for 54%

profile of v2, /device:TPU:0, one launch (start us, length us, event | category | flops | bytes accessed | tf_op | source)
XLA Modules:
  0.0 1028.4 jit_solution(4121917840013163965)
XLA Ops:
  10.9 3.1 collective-permute-start
  14.5 4.9 collective-permute-done
  20.3 43.0 %all-gather.8.cloned.1.call-done = bf16[2,768,1152]{2,1,0:T(8,128)(2,1)} async-done(((bf16[2,96,1152]{2,1,0:T(8,128)(2,1)}), bf16[2,768,1152]{2,1,0:T(8,128)(2,1)}) %all-gather.8.cloned.1.call-update) | async-done | bytes 3538960 | tf_op jit(solution)/shard_map/all_gather | solution.py:451
  69.7 5.6 collective-permute-done.2
  77.2 3.4 reshape_broadcast_in_dim.3
  103.6 104.2 %self_in.1 = (bf16[4,208,1536]{2,1,0:T(8,128)(2,1)}, f32[4,208,768]{2,1,0:T(8,128)}, f32[4,8,256]{2,1,0:T(8,128)}, bf16[4,208,1152]{2,1,0:T(8,128)(2,1)}, bf16[4...) custom-call(f32[208,1536]{1,0:T(8,128)} %pad.15.refs_0_.refs_2_.refs_7_, f32[8,1536]{1,0:T(8,128)} %get-tuple-element.176.refs_1_, ...), custom_call_target="tpu_custom_call" | custom-call | flops 80499998720 | bytes 252000000 | tf_op jit(solution)/shard_map/self_in/pallas_call | solution.py:302
  212.9 122.2 %self_attend.1 = (bf16[4,208,384]{2,1,0:T(8,128)(2,1)}, f32[208,1536]{1,0:T(8,128)}, f32[208,1536]{1,0:T(8,128)}, bf16[4,208,1536]{2,1,0:T(8,128)(2,1)}, f32[4,208,384]{2,1,0:T(8,128)}, /*index=5*/f32[4,8,256]{2,1,0:T(8,128)}) custom-call(bf16[4,208,1152]{2,1,0:T(8,128)(2,1)} %get-tuple-element.68.refs_0_, bf16[2,384,768]{2,1,0:T(8,128)(2,1)} %bitcast.298, ...), custom_call_target="tpu_custom_call" | custom-call | flops 92000002048 | bytes 288000000 | tf_op jit(solution)/shard_map/self_attend/pallas_call | solution.py:302
  335.1 8.4 fusion.10
  355.5 5.2 multiply_convert_fusion
  363.3 59.0 %cross_attend.1 = (bf16[4,208,384]{2,1,0:T(8,128)(2,1)}, f32[208,1536]{1,0:T(8,128)}, bf16[4,208,1536]{2,1,0:T(8,128)(2,1)}, bf16[4,208,2240]{2,1,0:T(8,128)(2,1)}, f32[4,208,2240]{2,1,0:T(8,128)}) custom-call(f32[4,208,384]{2,1,0:T(8,128)} %get-tuple-element.71.refs_0_, f32[8,384]{1,0:T(8,128)} %pad.16.refs_4_.refs_1_.refs_2_, ...), custom_call_target="tpu_custom_call" | custom-call | flops 69000003584 | bytes 216000000 | tf_op jit(solution)/shard_map/cross_attend/pallas_call | solution.py:302
  422.4 10.3 bitcast_convert_fusion.1
  436.6 6.3 collective-permute-done.15
  442.9 4.6 add_convert_fusion
  447.6 74.5 %ffn_back.1 = (bf16[4,208,2240]{2,1,0:T(8,128)(2,1)}, f32[208,1536]{1,0:T(8,128)}, bf16[4,208,1536]{2,1,0:T(8,128)(2,1)}, bf16[4,208,384]{2,1,0:T(8,128)(2,1)}, f32[3,8,1536]{2,1,0:T(8,128)}) custom-call(bf16[4,208,1536]{2,1,0:T(8,128)(2,1)} %get-tuple-element.86.refs_0_, bf16[2,2240,768]{2,1,0:T(8,128)(2,1)} %bitcast.291, ...), custom_call_target="tpu_custom_call" | custom-call | flops 82800001024 | bytes 259200000 | tf_op jit(solution)/shard_map/ffn_back/pallas_call | solution.py:302
  522.0 11.3 %bitcast_convert_fusion = bf16[1536,2240]{0,1:T(8,128)(2,1)} fusion(bf16[4,208,1536]{2,1,0:T(8,128)(2,1)S(1)} %copy-done.52, bf16[4,208,2240]{2,1,0:T(8,128)(2,1)} %get-tuple-element.90), kind=kOutput, calls=%fused_computation | convolution fusion | flops 5728665600 | bytes 13164544 | tf_op jit(solution)/shard_map/dot_general | solution.py:73
  533.4 9.7 copy.76
  545.4 6.3 collective-permute-done.16
  551.7 3.9 fusion.2
  557.9 77.6 %cross_back.1 = (bf16[4,208,384]{2,1,0:T(8,128)(2,1)}, bf16[4,512,768]{2,1,0:T(8,128)(2,1)}, f32[8,384]{1,0:T(8,128)}, f32[208,1536]{1,0:T(8,128)}, bf16[4,208,1...) custom-call(f32[4,208,384]{2,1,0:T(8,128)} %get-tuple-element.71.refs_0_, ...), custom_call_target="tpu_custom_call" | custom-call | flops 92000002048 | bytes 288000000 | tf_op jit(solution)/shard_map/cross_back/pallas_call | solution.py:302
  635.6 3.8 copy.127
  641.3 6.0 pad_maximum_fusion
  648.0 3.1 fusion.50
  651.1 3.1 fusion.41
  655.0 5.0 collective-permute-start.12
  662.7 3.5 collective-permute-start.13
  671.6 3.6 collective-permute-done.49
  675.5 4.2 fusion.18
  679.7 3.4 collective-permute-done.50
  683.1 22.9 %reduce-scatter.12.cloned.1.call-done = bf16[1,4,128,768]{3,2,1,0:T(8,128)(2,1)} async-done(((bf16[4,4,128,768]{3,2,1,0:T(8,128)(2,1)}), bf16[1,4,128,768]{3,2,1,0:T(8,128)(2,1)}) %reduce-scatter.12.cloned.1.call-update) | async-done | bytes 786448 | tf_op jit(solution)/shard_map/reduce_scatter | solution.py:877
  710.4 3.7 fusion.8
  722.2 3.0 bitcast_convert_fusion.2
  745.7 3.2 fusion.4
  749.0 3.2 fusion.7
  752.4 11.3 %collective-permute-done.41 = bf16[560,768]{1,0:T(8,128)(2,1)} collective-permute-done((bf16[560,768]{1,0:T(8,128)(2,1)}, bf16[560,768]{1,0:T(8,128)(2,1)}, u32[]{:S(2)}, u32[]{:S(2)}) %collective-permute-start.41) | collective-permute-done | bytes 860192 | tf_op jit(solution)/shard_map/ppermute | solution.py:407
  771.7 3.7 fusion.30
  775.5 6.7 collective-permute-done.39
  784.9 117.1 %self_back.1 = (bf16[4,208,1152]{2,1,0:T(8,128)(2,1)}, f32[2,8,384]{2,1,0:T(8,128)}, f32[208,1536]{1,0:T(8,128)}, f32[2,8,1536]{2,1,0:T(8,128)}) custom-call(bf16[4,208,1152]{2,1,0:T(8,128)(2,1)} %get-tuple-element.68.refs_0_, bf16[4,208,384]{2,1,0:T(8,128)(2,1)} %get-tuple-element.94.refs_1_, f32[4,208,768]{2,1,0:T(8,128)} %get-tuple-element.95.refs_2_, ...), custom_call_target="tpu_custom_call" | custom-call | flops 138000007168 | bytes 432000000 | tf_op jit(solution)/shard_map/self_back/pallas_call | solution.py:302
  902.0 6.0 fusion
  918.6 3.9 collective-permute-start.26
  922.5 3.3 convolution_convert_fusion.1
  932.6 3.3 convolution_convert_fusion
  940.9 3.1 fusion.3
  950.3 4.7 reshape.902
  958.7 4.0 convert_add_fusion.3
  971.8 3.9 collective-permute-done.48
  980.3 3.5 collective-permute-done.37
  989.2 6.2 collective-permute-done.35
  999.2 4.9 collective-permute-done.31
  (428 shorter events, 191.9 us)
Async XLA Ops:
  7.2 56.2 %all-gather.8.cloned.1.call-start = ((), (), s32[]{:S(2)}) async-start(), calls=%async_computation.7 | async-start | bytes 3981312 | tf_op jit(solution)/shard_map/all_gather | solution.py:451
  10.9 8.5 collective-permute-start
  20.3 187.5 %all-gather.14.cloned.1.call-start = ((), (), s32[]{:S(2)}) async-start(), calls=%async_computation.10 | async-start | bytes 1966080 | tf_op jit(solution)/shard_map/all_gather | solution.py:515
  63.4 148.9 %all-gather.10.cloned.1.call-start = ((), (), s32[]{:S(2)}) async-start(), calls=%async_computation.8 | async-start | bytes 1327104 | tf_op jit(solution)/shard_map/all_gather | solution.py:459
  66.0 146.2 %all-gather.12.cloned.1.call-start = ((), (), s32[]{:S(2)}) async-start(), calls=%async_computation.9 | async-start | bytes 3981312 | tf_op jit(solution)/shard_map/all_gather | solution.py:451
  67.6 7.7 collective-permute-start.2
  76.2 286.5 %all-gather.16.cloned.1.call-start = ((), (), s32[]{:S(2)}) async-start(), calls=%async_computation.11 | async-start | bytes 1327104 | tf_op jit(solution)/shard_map/all_gather | solution.py:459
  77.2 271.1 %collective-permute-start.11 = (bf16[560,768]{1,0:T(8,128)(2,1)}, bf16[560,768]{1,0:T(8,128)(2,1)}, u32[]{:S(2)}, u32[]{:S(2)}) collective-permute-start(bf16[560,768]{1,0:T(8,128)(2,1)} %constant_dynamic-slice_fusion.13), channel_id=1, source_target_pairs={{0,4},{4,0},{1,5},{5,1},{2,6},{6,2},{3,7},{7,3},{8,12},{12,8},{9,1... | collective-permute-start | bytes 2580488 | tf_op jit(solution)/shard_map/ppermute | solution.py:413
  82.6 19.3 %collective-permute-start.10 = (bf16[96,2240]{1,0:T(8,128)(2,1)S(1)}, bf16[96,2240]{1,0:T(8,128)(2,1)S(1)}, u32[]{:S(2)}, u32[]{:S(2)}) collective-permute-start(bf16[96,2240]{1,0:T(8,128)(2,1)S(1)} %bitcast.266), channel_id=1, source_target_pairs={{0,8},{8,0},{1,9},{9,1},{2,10},{10,2},{3,11},{11,3},{4,12},{12,4},... | collective-permute-start | bytes 1290248 | tf_op jit(solution)/shard_map/ppermute | solution.py:404
  91.9 270.8 %all-gather.18.cloned.1.call-start = ((), (), s32[]{:S(2)}) async-start(), calls=%async_computation.12 | async-start | bytes 7962624 | tf_op jit(solution)/shard_map/all_gather | solution.py:451
  102.9 344.6 %all-gather.20.cloned.1.call-start = ((), (), s32[]{:S(2)}) async-start(), calls=%async_computation.13 | async-start | bytes 7741440 | tf_op jit(solution)/shard_map/all_gather | solution.py:459
  207.8 127.2 %collective-permute-start.5 = (bf16[512,1536]{1,0:T(8,128)(2,1)}, bf16[512,1536]{1,0:T(8,128)(2,1)S(1)}, u32[]{:S(2)}, u32[]{:S(2)}) collective-permute-start(bf16[512,1536]{1,0:T(8,128)(2,1)} %all-gather.14.cloned.1.call-done), channel_id=1, source_target_pairs={{0,24},{8,16},{16,8},{24,0},{1,25},{9,17},{17,9},{25,1},{2,26},{10... | collective-permute-start | bytes 4718600 | tf_op jit(solution)/shard_map/ppermute | solution.py:410
  207.9 127.2 %collective-permute-start.4 = (bf16[512,1536]{1,0:T(8,128)(2,1)}, bf16[512,1536]{1,0:T(8,128)(2,1)}, u32[]{:S(2)}, u32[]{:S(2)}) collective-permute-start(bf16[512,1536]{1,0:T(8,128)(2,1)} %all-gather.14.cloned.1.call-done), channel_id=1, source_target_pairs={{0,16},{16,0},{1,17},{17,1},{2,18},{18,2},{3,19},{19,3},{4,20},{20... | collective-permute-start | bytes 4718600 | tf_op jit(solution)/shard_map/ppermute | solution.py:407
  210.9 124.2 %collective-permute-start.3 = (bf16[512,1536]{1,0:T(8,128)(2,1)}, bf16[512,1536]{1,0:T(8,128)(2,1)}, u32[]{:S(2)}, u32[]{:S(2)}) collective-permute-start(bf16[512,1536]{1,0:T(8,128)(2,1)} %all-gather.14.cloned.1.call-done), channel_id=1, source_target_pairs={{0,8},{8,0},{1,9},{9,1},{2,10},{10,2},{3,11},{11,3},{4,12},{12,4},... | collective-permute-start | bytes 4718600 | tf_op jit(solution)/shard_map/ppermute | solution.py:404
  349.4 208.6 %reduce-scatter.8.cloned.1.call-start = ((), (), s32[]{:S(2)}) async-start(), calls=%async_computation.14 | async-start | bytes 4300800 | tf_op jit(solution)/shard_map/reduce_scatter | solution.py:480
  447.5 188.1 %reduce-scatter.10.cloned.1.call-start = ((), (), s32[]{:S(2)}) async-start(), calls=%async_computation.15 | async-start | bytes 4423680 | tf_op jit(solution)/shard_map/reduce_scatter | solution.py:480
  557.7 148.3 %reduce-scatter.12.cloned.1.call-start = ((), (), s32[]{:S(2)}) async-start(), calls=%async_computation.16 | async-start | bytes 3932160 | tf_op jit(solution)/shard_map/reduce_scatter | solution.py:877
  639.5 338.2 %reduce-scatter.20.cloned.1.call-start = ((), (), s32[]{:S(2)}) async-start(), calls=%async_computation.20 | async-start | bytes 737280 | tf_op jit(solution)/shard_map/reduce_scatter | solution.py:480
  655.0 77.6 %collective-permute-start.12 = (bf16[208,1536]{1,0:T(8,128)(2,1)}, bf16[208,1536]{1,0:T(8,128)(2,1)}, u32[]{:S(2)}, u32[]{:S(2)}) collective-permute-start(bf16[208,1536]{1,0:T(8,128)(2,1)} %pad_maximum_fusion.4), channel_id=1, source_target_pairs={{0,8},{8,0},{1,9},{9,1},{2,10},{10,2},{3,11},{11,3},{4,12},{12,4},... | collective-permute-start | bytes 1916936 | tf_op jit(solution)/shard_map/ppermute | solution.py:404
  662.7 70.0 %collective-permute-start.13 = (bf16[208,1536]{1,0:T(8,128)(2,1)}, bf16[208,1536]{1,0:T(8,128)(2,1)}, u32[]{:S(2)}, u32[]{:S(2)}) collective-permute-start(bf16[208,1536]{1,0:T(8,128)(2,1)} %pad_maximum_fusion.5), channel_id=1, source_target_pairs={{0,16},{16,0},{1,17},{17,1},{2,18},{18,2},{3,19},{19,3},{4,20},{20... | collective-permute-start | bytes 1916936 | tf_op jit(solution)/shard_map/ppermute | solution.py:407
  670.9 61.8 %collective-permute-start.14 = (bf16[208,1536]{1,0:T(8,128)(2,1)}, bf16[208,1536]{1,0:T(8,128)(2,1)}, u32[]{:S(2)}, u32[]{:S(2)}) collective-permute-start(bf16[208,1536]{1,0:T(8,128)(2,1)} %pad_maximum_fusion.6), channel_id=1, source_target_pairs={{0,24},{8,16},{16,8},{24,0},{1,25},{9,17},{17,9},{25,1},{2,26},{10... | collective-permute-start | bytes 1916936 | tf_op jit(solution)/shard_map/ppermute | solution.py:410
  675.2 7.9 collective-permute-start.50
  683.1 46.9 %collective-permute-start.51 = (f32[8960]{0:T(1024)S(1)}, f32[8960]{0:T(1024)S(1)}, u32[]{:S(2)}, u32[]{:S(2)}) collective-permute-start(f32[8960]{0:T(1024)S(1)} %add.363), channel_id=1, source_target_pairs={{0,4},{4,0},{1,5},{5,1},{2,6},{6,2},{3,7},{7,3},{8,12},{12,8},{9,1... | collective-permute-start | bytes 107528 | tf_op jit(solution)/shard_map/ppermute | solution.py:413
  727.0 18.8 %collective-permute-start.22 = (bf16[2,4,96,1152]{3,2,0,1:T(8,128)(2,1)}, bf16[2,4,96,1152]{3,2,0,1:T(8,128)(2,1)}, u32[]{:S(2)}, u32[]{:S(2)}) collective-permute-start(bf16[2,4,96,1152]{3,2,0,1:T(8,128)(2,1)} %bitcast.225), channel_id=1, source_target_pairs={{0,4},{4,0},{1,5},{5,1},{2,6},{6,2},{3,7},{7,3},{8,12},{12,8},{9,1... | collective-permute-start | bytes 5308424 | tf_op jit(solution)/shard_map/ppermute | solution.py:413
  732.6 11.1 %collective-permute-start.17 = (bf16[384,768]{1,0:T(8,128)(2,1)S(1)}, bf16[384,768]{1,0:T(8,128)(2,1)}, u32[]{:S(2)}, u32[]{:S(2)}) collective-permute-start(bf16[384,768]{1,0:T(8,128)(2,1)S(1)} %constant_dynamic-slice_fusion.11), channel_id=1, source_target_pairs={{0,4},{4,0},{1,5},{5,1},{2,6},{6,2},{3,7},{7,3},{8,12},{12,8},{9,1... | collective-permute-start | bytes 1769480 | tf_op jit(solution)/shard_map/ppermute | solution.py:413
  742.2 21.5 %collective-permute-start.41 = (bf16[560,768]{1,0:T(8,128)(2,1)}, bf16[560,768]{1,0:T(8,128)(2,1)}, u32[]{:S(2)}, u32[]{:S(2)}) collective-permute-start(bf16[560,768]{1,0:T(8,128)(2,1)} %reduce-scatter.8.cloned.1.call-done), channel_id=1, source_target_pairs={{0,16},{16,0},{1,17},{17,1},{2,18},{18,2},{3,19},{19,3},{4,20},{20... | collective-permute-start | bytes 2580488 | tf_op jit(solution)/shard_map/ppermute | solution.py:407
  748.9 229.9 %reduce-scatter.16.cloned.1.call-start = ((), (), s32[]{:S(2)}) async-start(), calls=%async_computation.18 | async-start | bytes 737280 | tf_op jit(solution)/shard_map/reduce_scatter | solution.py:480
  752.3 15.0 %collective-permute-start.18 = (bf16[384,768]{1,0:T(8,128)(2,1)S(1)}, bf16[384,768]{1,0:T(8,128)(2,1)}, u32[]{:S(2)}, u32[]{:S(2)}) collective-permute-start(bf16[384,768]{1,0:T(8,128)(2,1)S(1)} %constant_dynamic-slice_fusion.10), channel_id=1, source_target_pairs={{0,4},{4,0},{1,5},{5,1},{2,6},{6,2},{3,7},{7,3},{8,12},{12,8},{9,1... | collective-permute-start | bytes 1769480 | tf_op jit(solution)/shard_map/ppermute | solution.py:413
  769.4 217.1 %reduce-scatter.18.cloned.1.call-start = ((), (), s32[]{:S(2)}) async-start(), calls=%async_computation.19 | async-start | bytes 2211840 | tf_op jit(solution)/shard_map/reduce_scatter | solution.py:480
  769.5 12.7 %collective-permute-start.39 = (bf16[96,2240]{1,0:T(8,128)(2,1)S(1)}, bf16[96,2240]{1,0:T(8,128)(2,1)S(1)}, u32[]{:S(2)}, u32[]{:S(2)}) collective-permute-start(bf16[96,2240]{1,0:T(8,128)(2,1)S(1)} %get-tuple-element.149), channel_id=1, source_target_pairs={{0,8},{8,0},{1,9},{9,1},{2,10},{10,2},{3,11},{11,3},{4,12},{12,4},... | collective-permute-start | bytes 1290248 | tf_op jit(solution)/shard_map/ppermute | solution.py:404
  783.3 160.7 %collective-permute-start.40 = (bf16[2,96,2240]{2,1,0:T(8,128)(2,1)}, bf16[2,96,2240]{2,1,0:T(8,128)(2,1)}, u32[]{:S(2)}, u32[]{:S(2)}) collective-permute-start(bf16[2,96,2240]{2,1,0:T(8,128)(2,1)} %maximum_select_fusion.6), channel_id=1, source_target_pairs={{0,16},{16,0},{1,17},{17,1},{2,18},{18,2},{3,19},{19,3},{4,20},{20... | collective-permute-start | bytes 2580488 | tf_op jit(solution)/shard_map/ppermute | solution.py:407
  784.8 211.5 %reduce-scatter.14.cloned.1.call-start = ((), (), s32[]{:S(2)}) async-start(), calls=%async_computation.17 | async-start | bytes 2211840 | tf_op jit(solution)/shard_map/reduce_scatter | solution.py:480
  909.7 31.2 %collective-permute-start.30 = (bf16[2,4,96,1152]{3,2,0,1:T(8,128)(2,1)}, bf16[2,4,96,1152]{3,2,0,1:T(8,128)(2,1)}, u32[]{:S(2)}, u32[]{:S(2)}) collective-permute-start(bf16[2,4,96,1152]{3,2,0,1:T(8,128)(2,1)} %bitcast.226), channel_id=1, source_target_pairs={{0,4},{4,0},{1,5},{5,1},{2,6},{6,2},{3,7},{7,3},{8,12},{12,8},{9,1... | collective-permute-start | bytes 5308424 | tf_op jit(solution)/shard_map/ppermute | solution.py:413
  918.6 12.0 %collective-permute-start.26 = (f32[7,1536]{1,0:T(8,128)}, f32[7,1536]{1,0:T(8,128)}, u32[]{:S(2)}, u32[]{:S(2)}) collective-permute-start(f32[7,1536]{1,0:T(8,128)} %stack.234), channel_id=1, source_target_pairs={{0,1},{1,0},{2,3},{3,2},{4,5},{5,4},{6,7},{7,6},{8,9},{9,8},{10,11... | collective-permute-start | bytes 129032 | tf_op jit(solution)/shard_map/ppermute | solution.py:1021
  930.5 8.3 collective-permute-start.28
  935.9 22.8 %collective-permute-start.25 = (bf16[128,1536]{1,0:T(8,128)(2,1)}, bf16[128,1536]{1,0:T(8,128)(2,1)}, u32[]{:S(2)}, u32[]{:S(2)}) collective-permute-start(bf16[128,1536]{1,0:T(8,128)(2,1)} %convolution_convert_fusion), channel_id=1, source_target_pairs={{0,24},{8,16},{16,8},{24,0},{1,25},{9,17},{17,9},{25,1},{2,26},{10... | collective-permute-start | bytes 1179656 | tf_op jit(solution)/shard_map/ppermute | solution.py:410
  937.3 21.4 %collective-permute-start.24 = (bf16[128,1536]{1,0:T(8,128)(2,1)}, bf16[128,1536]{1,0:T(8,128)(2,1)}, u32[]{:S(2)}, u32[]{:S(2)}) collective-permute-start(bf16[128,1536]{1,0:T(8,128)(2,1)} %convolution_convert_fusion.1), channel_id=1, source_target_pairs={{0,16},{16,0},{1,17},{17,1},{2,18},{18,2},{3,19},{19,3},{4,20},{20... | collective-permute-start | bytes 1179656 | tf_op jit(solution)/shard_map/ppermute | solution.py:407
  938.9 19.9 %collective-permute-start.23 = (bf16[128,1536]{1,0:T(8,128)(2,1)}, bf16[128,1536]{1,0:T(8,128)(2,1)}, u32[]{:S(2)}, u32[]{:S(2)}) collective-permute-start(bf16[128,1536]{1,0:T(8,128)(2,1)} %convolution_convert_fusion.2), channel_id=1, source_target_pairs={{0,8},{8,0},{1,9},{9,1},{2,10},{10,2},{3,11},{11,3},{4,12},{12,4},... | collective-permute-start | bytes 1179656 | tf_op jit(solution)/shard_map/ppermute | solution.py:404
  940.9 14.2 %collective-permute-start.43 = (f32[7,1536]{1,0:T(8,128)}, f32[7,1536]{1,0:T(8,128)}, u32[]{:S(2)}, u32[]{:S(2)}) collective-permute-start(f32[7,1536]{1,0:T(8,128)} %add.352), channel_id=1, source_target_pairs={{0,4},{4,0},{1,5},{5,1},{2,6},{6,2},{3,7},{7,3},{8,12},{12,8},{9,1... | collective-permute-start | bytes 129032 | tf_op jit(solution)/shard_map/ppermute | solution.py:413
  944.0 13.7 %collective-permute-start.29 = (f32[14,1536]{1,0:T(8,128)}, f32[14,1536]{1,0:T(8,128)}, u32[]{:S(2)}, u32[]{:S(2)}) collective-permute-start(f32[14,1536]{1,0:T(8,128)} %add.353), channel_id=1, source_target_pairs={{0,2},{1,3},{2,0},{3,1},{4,6},{5,7},{6,4},{7,5},{8,10},{9,11},{10,... | collective-permute-start | bytes 258056 | tf_op jit(solution)/shard_map/ppermute | solution.py:1022
  955.9 8.8 collective-permute-start.44
  958.6 7.5 collective-permute-start.46
  978.9 6.5 collective-permute-start.33
  984.8 13.4 %collective-permute-start.38 = (bf16[96,768]{1,0:T(8,128)(2,1)S(1)}, bf16[96,768]{1,0:T(8,128)(2,1)S(1)}, u32[]{:S(2)}, u32[]{:S(2)}) collective-permute-start(bf16[96,768]{1,0:T(8,128)(2,1)S(1)} %get-tuple-element.159), channel_id=1, source_target_pairs={{0,4},{4,0},{1,5},{5,1},{2,6},{6,2},{3,7},{7,3},{8,12},{12,8},{9,1... | collective-permute-start | bytes 442376 | tf_op jit(solution)/shard_map/ppermute | solution.py:413
  987.5 7.9 collective-permute-start.35
  995.5 13.1 %collective-permute-start.36 = (bf16[2,96,1152]{2,1,0:T(8,128)(2,1)S(1)}, bf16[2,96,1152]{2,1,0:T(8,128)(2,1)S(1)}, u32[]{:S(2)}, u32[]{:S(2)}) collective-permute-start(bf16[2,96,1152]{2,1,0:T(8,128)(2,1)S(1)} %maximum_select_fusion.12), channel_id=1, source_target_pairs={{0,16},{16,0},{1,17},{17,1},{2,18},{18,2},{3,19},{19,3},{4,20},{20... | collective-permute-start | bytes 1327112 | tf_op jit(solution)/shard_map/ppermute | solution.py:407
  997.4 6.7 collective-permute-start.31
  1004.2 12.5 %collective-permute-start.32 = (bf16[2,96,1152]{2,1,0:T(8,128)(2,1)S(1)}, bf16[2,96,1152]{2,1,0:T(8,128)(2,1)S(1)}, u32[]{:S(2)}, u32[]{:S(2)}) collective-permute-start(bf16[2,96,1152]{2,1,0:T(8,128)(2,1)S(1)} %maximum_select_fusion.11), channel_id=1, source_target_pairs={{0,16},{16,0},{1,17},{17,1},{2,18},{18,2},{3,19},{19,3},{4,20},{20... | collective-permute-start | bytes 1327112 | tf_op jit(solution)/shard_map/ppermute | solution.py:407
  (79 other events, 982.8 us)
Sparse Core Ops, SparseCore 0:
  20.4 42.9 all-gather.7
  64.9 35.8 all-gather.13
  103.0 30.2 all-gather.9
  135.3 69.0 all-gather.11
  206.5 31.0 all-gather.15
  239.6 70.8 all-gather.17
  349.5 69.2 all-gather.19
  447.6 63.0 reduce-scatter.7
  557.8 74.3 reduce-scatter.9
  639.6 66.4 reduce-scatter.11
  749.0 21.0 reduce-scatter.19
  772.9 20.4 reduce-scatter.15
  796.2 60.8 reduce-scatter.17
  944.1 39.4 reduce-scatter.13

commit v3 on v2

--- a/solution.py
+++ b/solution.py
@@ -7,7 +7,6 @@
 from jax import lax
 from jax.experimental import pallas as pl
 from jax.experimental.pallas import tpu as pltpu
-from jax.experimental.layout import Layout, with_layout_constraint
 from jax.sharding import Mesh, PartitionSpec as P
 
 HD = 128
@@ -340,12 +339,13 @@
 def rows_partial(a, w):
     def partial(refs, k, store):
         piece = getattr(refs, a)[k]
-        width = getattr(refs, w).shape[2]
+        blocks = getattr(refs, w)
+        deep, width = piece.shape[1], blocks.shape[2]
         for half in range(2):
-            for at, size in column_chunks(width, 384):
+            for part in range(2):
                 store(
-                    pl.ds(half * width + at, size),
-                    mm(piece, getattr(refs, w)[half, :, pl.ds(at, size)]),
+                    pl.ds((half * 2 + part) * width, width),
+                    mm(piece, blocks[part, pl.ds(half * deep, deep), :]),
                 )
 
     return partial
@@ -364,8 +364,13 @@
 
 
 def rows_turned(piece, w):
-    width = w.shape[2]
-    return mm_t(piece[:, pl.ds(0, width)], w[0]) + mm_t(piece[:, pl.ds(width, width)], w[1])
+    deep, width = w.shape[1] // 2, w.shape[2]
+    total = 0.0
+    for half in range(2):
+        for part in range(2):
+            columns = pl.ds((half * 2 + part) * width, width)
+            total = total + mm_t(piece[:, columns], w[part, pl.ds(half * deep, deep), :])
+    return total
 
 
 def mm_l(a, b):
@@ -441,23 +446,36 @@
         full = v[..., None, :] * hot[:, None]
         return full.reshape(v.shape[:-1] + (4 * v.shape[-1],))
 
-    def column_block(w, *done):
+    def column_own(w):
         rows, groups, width = w.shape[0], w.shape[1], w.shape[2] // 4
         mine = lax.dynamic_index_in_dim(w.reshape(rows, groups, 2, 2, width), x, 3, False)
         keep = lax.dynamic_index_in_dim(mine, y, 2, False).reshape(rows, groups * width)
         send = lax.dynamic_index_in_dim(mine, 1 - y, 2, False).reshape(rows, groups * width)
         recv = from_y(send)
-        both = jnp.where(y == 0, jnp.stack([keep, recv]), jnp.stack([recv, keep]))
-        full = lax.all_gather(after(both, *done), ("core", "z"), axis=1, tiled=True)
-        return full.reshape(-1, groups * width)
-
-    def row_block(w, *done):
-        rows, half = w.shape[0], w.shape[1] // 2
+        return jnp.where(y == 0, jnp.stack([keep, recv]), jnp.stack([recv, keep]))
+
+    def column_block(w):
+        full = lax.all_gather(column_own(w), ("core", "z"), axis=1, tiled=True)
+        return full.reshape(-1, full.shape[2])
+
+    def row_own(w):
+        half = w.shape[1] // 2
         keep = lax.dynamic_slice_in_dim(w, core * half, half, 1)
         recv = from_core(lax.dynamic_slice_in_dim(w, (1 - core) * half, half, 1))
-        mine = jnp.where(core == x, keep, recv)
-        full = lax.all_gather(after(mine, *done), ("core", "z"), axis=0, tiled=True)
-        return full.reshape(2, seqs * rows, half)
+        return jnp.where(core == x, keep, recv)
+
+    def row_block(w):
+        full = lax.all_gather(row_own(w), ("core", "z"), axis=0, tiled=True)
+        return full.reshape(2, -1, full.shape[1])
+
+    def attention_blocks(w_cross, *row_weights):
+        own = column_own(w_cross)
+        width = own.shape[2] // 3
+        blocks = [own[:, :, g * width : (g + 1) * width] for g in range(3)]
+        for w in row_weights:
+            mine = row_own(w)
+            blocks.append(jnp.stack([mine[:, :width], mine[:, width:]]))
+        return lax.all_gather(jnp.concatenate(blocks), ("core", "z"), axis=1, tiled=True)
 
     def over_reps(a):
         return lax.psum(a, "rep") if reps > 1 else a
@@ -510,12 +528,14 @@
         return jnp.stack(rows + (jnp.zeros_like(rows[0]),) * (8 - len(rows)))
 
     full_qkv = column_block(w_qkv)
-    full_out = row_block(w_out, full_qkv)
-    full_cross = column_block(w_cross, full_qkv)
-    text_z = lax.all_gather(after(text_emb, full_qkv), "z", axis=0, tiled=True)
-    full_crossout = row_block(w_crossout, full_qkv)
-    full_up = column_block(w_up[:, None, :], full_qkv)
-    full_down = row_block(w_down, full_qkv)
+    text_z = lax.all_gather(text_emb, "z", axis=0, tiled=True)
+    attend_w = attention_blocks(w_cross, w_out, w_crossout)
+    cross_wq, cross_wk, cross_wv = [
+        attend_w[2 * g : 2 * g + 2].reshape(dim, -1) for g in range(3)
+    ]
+    full_out, full_crossout = attend_w[6:8], attend_w[8:10]
+    full_up = column_block(w_up[:, None, :])
+    full_down = row_block(w_down)
     bias = pick(attn_bias)
     gain = pick(qk_gain)
     width = bias.shape[1]
@@ -565,12 +585,12 @@
                 refs.stat[k, pl.ds(part, 1), pl.ds(0, tokens)] = to_row(square)
 
         refs.tables[0] = refs.own_tables[...]
-        refs.grads[0] = refs.own_grads[...]
+        refs.texts[0] = refs.text[...]
         row_steps(tokens, rows_in)
         gather_slice(links, refs, refs.held, product, (refs.tables,))
         sum_stats(links, refs)
         refs.inv[...] = lax.rsqrt(refs.stat_sum[...] / dim + EPS)
-        first = gather_begin(links, refs.grads)
+        first = gather_begin(links, refs.texts)
         for k in (3, 2, 1, 0):
             cosine, sine = refs.tables[k, :, pl.ds(0, HD)], refs.tables[k, :, pl.ds(HD, HD)]
             for part in range(2):
@@ -583,32 +603,29 @@
                     turned = scaled * cosine + swap_pairs(scaled) * sine
                     refs.sent[k, :, at] = turned.astype(BF16)
             send_heads(k, late, 1)
-        gather_end(gather_relay(links, refs.grads, first))
+        gather_end(gather_relay(links, refs.texts, first))
         for source in range(seqs):
             links.wait_line(refs.packed.at[source, :, early], source, 0)
             links.wait_line(refs.packed.at[source, :, late], source, 1)
 
     gains8 = jnp.pad(gain, ((0, 4), (0, 0)))
+    texts = text_z.shape[0]
     first = run_kernel(
         "self_in", 1,
         dict(
             states=states_p, vec=vectors(1.0 + scale1, shift1), w=full_qkv,
             bias=jnp.broadcast_to(bias[:3].reshape(1, -1), (8, blocks3)),
-            gain=gains8, own_tables=own_tables, own_grads=d_ffnout,
+            gain=gains8, own_tables=own_tables, text=text_z,
         ),
         dict(
             held=held, unit=((4, tokens, 2 * width), F32), inv=((4, 8, 256), F32),
-            packed=((seqs, tokens, blocks3), BF16), grads=held,
+            packed=((seqs, tokens, blocks3), BF16), texts=((4, texts, dim), BF16),
             tables=((4, tokens, 2 * HD), F32),
         ),
         body, dict(sent=((4, tokens, blocks3), BF16)), stats=True, line=2, cost=70,
     )
     x_self, self_unit, self_inv, packed = first.held, first.unit, first.inv, first.packed
-    g_ffn, tables = first.grads, first.tables
-
-    texts = text_z.shape[0]
-    text_z = with_layout_constraint(after(text_z, packed), Layout((0, 1)))
-    text_pieces = [text_z, from_y(text_z), from_x(text_z), from_xy(text_z)]
+    x_text, tables = first.texts, first.tables
 
     def masked_scores(q, keys):
         scores = mm_t(q, keys) * SCALE
@@ -632,6 +649,8 @@
     def body(links, refs):
         refs.stat[...] = jnp.zeros_like(refs.stat)
         packed = refs.packed
+        refs.grads[0] = refs.own_grads[...]
+        first = gather_begin(links, refs.grads)
         for turn in (1, 2, 3, 0):
             to = (links.z + turn) % seqs
             for h in range(heads):
@@ -642,6 +661,7 @@
             links.send_line(
                 refs.outs.at[turn], refs.mixed.at[links.clip_of(links.z)], to, turn
             )
+        far = gather_relay(links, refs.grads, first)
         reduce_product = rows_partial("mixed", "w")
 
         def partial(refs, k, store):
@@ -650,6 +670,7 @@
 
         reduce_slice(links, refs, partial, middle, refs.held)
         gather_slice(links, refs, refs.held, product)
+        gather_end(far)
         sum_stats(links, refs)
         refs.inv[...] = lax.rsqrt(refs.stat_sum[...] / dim + EPS)
 
@@ -663,10 +684,11 @@
         dict(
             packed=packed, w=full_out, states=states_p,
             vec=vectors(attn_bias[3], gate1, norm_gain, norm_bias),
-            w2=full_cross, bias=jnp.broadcast_to(bias[4:5], (8, width)),
-        ),
-        dict(
-            mixed=((4, tokens, width), BF16), branch=wide, joined=wide, held=held,
+            w2=cross_wq, bias=jnp.broadcast_to(bias[4:5], (8, width)),
+            own_grads=d_ffnout,
+        ),
+        dict(
+            mixed=((4, tokens, width), BF16), branch=wide, joined=wide, held=held, grads=held,
             unit=head_block, inv=((4, 8, 256), F32),
         ),
         body,
@@ -674,13 +696,11 @@
         stats=True, line=1,
         cost=80,
     )
-    mixed, branch, after_self = second.mixed, second.branch, second.joined
+    mixed, branch, after_self, g_ffn = second.mixed, second.branch, second.joined, second.grads
     x_cross, cq_unit, cq_inv = second.held, second.unit, second.inv
 
-    x_text = jnp.stack(after(text_pieces, cq_inv))
-    text_proj = mm(x_text, full_cross[:, width:])
-    ck_pre = text_proj[..., :width] + bias[5]
-    cross_v = (text_proj[..., width:] + bias[6]).astype(BF16)
+    ck_pre = mm(x_text, cross_wk) + bias[5]
+    cross_v = (mm(x_text, cross_wv) + bias[6]).astype(BF16)
     ck_inv = rms_scale(sum4(jnp.sum(ck_pre * ck_pre, -1)))
     ck_unit = ck_pre * ck_inv
     cross_k = (ck_unit * gain[3]).astype(BF16)
@@ -854,7 +874,7 @@
         dict(
             unit=cq_unit, inv=cq_inv, gain=gains8, kv=text_kv,
             d_mix=after(d_cmix, up_core, down_part),
-            w=full_cross, joined=after_self, top=d_cross, branch=branch,
+            w=cross_wq, joined=after_self, top=d_cross, branch=branch,
             vec=vectors(norm_gain, gate1), w2=full_out,
         ),
         dict(
@@ -873,28 +893,14 @@
     d_cq, d_self, g_self, d_heads = fifth.d_pre, fifth.d_self, fifth.held, fifth.d_heads
     cq_gain = jnp.sum(fifth.gains, 0)
     sums5 = jnp.sum(fifth.sums, 1)
-    d_ckv = after(fifth.d_kv, up_part).reshape(4, seqs, -1, 2 * width).transpose(1, 0, 2, 3)
-    d_ckv = lax.psum_scatter(d_ckv, "z", scatter_dimension=0, tiled=True)[0]
+    d_kv, mixed, cross_mix = after((fifth.d_kv, mixed, cross_mix), up_part)
     outproj_core = row_core(outer(mixed, g_self))
-    crossout_core = row_core(outer(after(cross_mix, d_self), g_cross))
-
-    d_ckn = d_ckv[..., :width].astype(F32)
-    d_cv = d_ckv[..., width:]
-    zpos = lax.axis_index("z")
-    own = texts // seqs
-    ck_unit = lax.dynamic_slice_in_dim(ck_unit, zpos * own, own, 1)
-    ck_inv = lax.dynamic_slice_in_dim(ck_inv, zpos * own, own, 1)
-    x_text = lax.dynamic_slice_in_dim(x_text, zpos * own, own, 1)
-    d_cku = d_ckn * gain[3]
-    ck_stat = sum4(jnp.sum(d_cku * ck_unit, -1)) / dim
-    d_ck = rms_back(d_cku, ck_unit, ck_inv, ck_stat[..., None]).astype(BF16)
-    ck_gain = jnp.sum(d_ckn * ck_unit, (0, 1))
-    d_text = jnp.concatenate([d_ck, d_cv], -1)
-    text_grad = reduce4(lambda k: mm_t(d_text[k], full_cross[:, width:]))
-    cross_core = column_core(jnp.concatenate([outer(x_cross, d_cq), outer(x_text, d_text)], 1))
-    cross_part = scatter_z(cross_core)
-    outproj_part = scatter_z(after(outproj_core, cross_core))
-    crossout_part = scatter_z(after(crossout_core, cross_core))
+    crossout_core = row_core(outer(cross_mix, g_cross))
+    d_kv = d_kv.reshape(4, seqs, -1, 2 * width).transpose(1, 0, 2, 3)
+    parts = [d_kv.reshape(seqs, -1, 2 * width)]
+    parts += [v.reshape(seqs, -1, 2 * width) for v in (outproj_core, crossout_core)]
+    joint_core = jnp.concatenate(parts, 1)
+    joint_part = lax.psum_scatter(joint_core, "z", scatter_dimension=0, tiled=True)[0]
 
     def middle(refs, rows, step, total):
         normed, inverse = layer_norm(refs.states[rows])
@@ -980,7 +986,7 @@
         dict(
             packed=packed, d_heads=d_heads, unit=self_unit, inv=self_inv,
             gain=gains8, tables=tables, w=full_qkv, states=states_p,
-            top=after(d_self, crossout_core, outproj_core, cross_core), vec=vectors(1.0 + scale1),
+            top=after(d_self, joint_core), vec=vectors(1.0 + scale1),
         ),
         dict(
             d_qkv=((4, tokens, blocks3), BF16), gains=((2, 8, width), F32),
@@ -997,13 +1003,36 @@
         stats=True, line=heads,
         cost=120,
     )
-    d_qkv = sixth.d_qkv
+    d_qkv, hidden, d_hpre, d_cq, up_part, down_part = after(
+        (sixth.d_qkv, hidden, d_hpre, d_cq, up_part, down_part),
+        joint_part,
+    )
+    text_rows, weight_rows = parts[0].shape[1], parts[1].shape[1]
+    d_ckv = joint_part[:text_rows].reshape(4, -1, 2 * width)
+    outproj_part = over_reps(joint_part[text_rows : text_rows + weight_rows])
+    crossout_part = over_reps(joint_part[text_rows + weight_rows :])
     d_qkv_sum = jnp.sum(d_qkv.astype(F32), (0, 1))
     q_gain, k_gain = jnp.sum(sixth.gains, 1)
     states_grad = sixth.out[:own_tokens]
     sums6 = jnp.sum(sixth.sums, 1)
     qkv_core = column_core(outer(x_self, d_qkv))
     qkv_part = scatter_z(qkv_core)
+
+    d_ckn = d_ckv[..., :width].astype(F32)
+    d_cv = d_ckv[..., width:]
+    zpos = lax.axis_index("z")
+    own = texts // seqs
+    ck_unit = lax.dynamic_slice_in_dim(ck_unit, zpos * own, own, 1)
+    ck_inv = lax.dynamic_slice_in_dim(ck_inv, zpos * own, own, 1)
+    x_text = lax.dynamic_slice_in_dim(x_text, zpos * own, own, 1)
+    d_cku = d_ckn * gain[3]
+    ck_stat = sum4(jnp.sum(d_cku * ck_unit, -1)) / dim
+    d_ck = rms_back(d_cku, ck_unit, ck_inv, ck_stat[..., None]).astype(BF16)
+    ck_gain = jnp.sum(d_ckn * ck_unit, (0, 1))
+    d_text = jnp.concatenate([d_ck, d_cv], -1)
+    text_grad = reduce4(lambda k: mm_t(d_ck[k], cross_wk) + mm_t(d_cv[k], cross_wv))
+    cross_core = column_core(jnp.concatenate([outer(x_cross, d_cq), outer(x_text, d_text)], 1))
+    cross_part = scatter_z(cross_core)
 
     ffn_out = reduce4(lambda k: rows_mm(hidden[k], full_down)) + down_bias
     block_out = (after_cross + ffn_out * gate2)[:own_tokens]

time: 1040 us -> 1030 us (level)
  other arithmetic: 83.2 us -> 57.4 us
    reduce_scatter x1, waiting for transfers between devices: 22.9 us -> 0.01 us  [on_device(): lax.psum_scatter(joint_core, 'z', scatter_dimension=0, tiled=True)[0]]
    ppermute x14 -> x13, waiting for transfers between devices: 26.2 us -> 48.2 us  [from_x(): return lax.ppermute(a, 'x', SWAP)]
    ppermute x5 -> x4, waiting for transfers between devices: 0.01 us -> 19.9 us  [from_xy(): return lax.ppermute(a, ('x', 'y'), [(i, 3 - i) for i in range(4)])]
    all_gather x7 -> x5, waiting for transfers between devices: 43.1 us -> 26.1 us  [the longest x2 26.1 us: column_block(): full = lax.all_gather(column_own(w), ('core', 'z'), axis=1, tiled=True)]
    ppermute x3, waiting for transfers between devices: 3.39 us -> 19 us  [over_z(): return v + lax.ppermute(v, 'z', [(i, i ^ 2) for i in range(seqs)])]
    ppermute x3, starting transfers between devices: 4.04 us -> 18.4 us  [over_z(): v = v + lax.ppermute(v, 'z', [(i, i ^ 1) for i in range(seqs)])]
    ppermute x14 -> x13, waiting for transfers between devices: 38.6 us -> 30.2 us  [from_y(): return lax.ppermute(a, 'y', SWAP)]
    dot_general x9 -> x10, matrix products: 24.8 us -> 30.5 us  [mm(): lax.dot_general(a, b, (((a.ndim - 1,), (0,)), ((), ())), preferred_elemen...]
  transfers between devices with their start and end apart: 68 -> 61, of which waited for: 25 -> 24; matrix products, arithmetic and copies ran while one was open for 22% -> 21% of each run, Pallas kernels for 54% -> 54%
where the time goes in v3:
time: 1030 us; the launch traced here: 1020 us
  Pallas kernels  550 us (53%)
  waiting for transfers between devices  157 us (15%)
  local copies, waits for them, and re-layouts  99.4 us (10%)
  matrix products  80.2 us (8%)
  starting transfers between devices  63 us (6%)
  other arithmetic  57.4 us (6%)
  between operations  16.1 us (2%)
    pallas_call x6, Pallas kernels, run_kernel(): pl.pallas_call(kernel, name=name, out_shape=[jax.ShapeDtypeStruct(*output...  550 us
    ppermute x13, waiting for transfers between devices, from_x(): return lax.ppermute(a, 'x', SWAP)  48.2 us
    dot_general x7, matrix products, outer(): lax.dot_general(a, b, ((lead, lead), ((), ())), preferred_element_type=F32)  36.6 us
    dot_general x10, matrix products, mm(): lax.dot_general(a, b, (((a.ndim - 1,), (0,)), ((), ())), preferred_elemen...  30.5 us
    ppermute x13, waiting for transfers between devices, from_y(): return lax.ppermute(a, 'y', SWAP)  30.2 us
    all_gather x2, waiting for transfers between devices, column_block(): full = lax.all_gather(column_own(w), ('core', 'z'), axis=1, tiled=True)  26.1 us
    convert_element_type x6, local copies, waits for them, and re-layouts, column_done(): full.transpose(2, 3, 0, 1, 4).reshape(rows, groups, 4 * width).astype(F32)  21.5 us
  transfers between devices with their start and end apart: 61, of which 24 were waited for; matrix products, arithmetic and copies ran while one was open for 21% of the time, Pallas kernels for 54%

profile of v3, /device:TPU:0, one launch (start us, length us, event | category | flops | bytes accessed | tf_op | source)
XLA Modules:
  0.0 1022.9 jit_solution(7352381302841762964)
XLA Ops:
  11.7 3.1 collective-permute-start
  15.3 4.9 collective-permute-done
  28.9 3.1 collective-permute-done.1
  39.1 10.0 collective-permute-done.7
  65.8 26.1 %all-gather.6.cloned.1.call-done = bf16[2,768,1152]{2,1,0:T(8,128)(2,1)} async-done(((bf16[2,96,1152]{2,1,0:T(8,128)(2,1)}), bf16[2,768,1152]{2,1,0:T(8,128)(2,1)}) %all-gather.6.cloned.1.call-update) | async-done | bytes 3538960 | tf_op jit(solution)/shard_map/all_gather | solution.py:458
  92.5 104.2 %self_in.1 = (bf16[4,208,1536]{2,1,0:T(8,128)(2,1)}, f32[4,208,768]{2,1,0:T(8,128)}, f32[4,8,256]{2,1,0:T(8,128)}, bf16[4,208,1152]{2,1,0:T(8,128)(2,1)}, bf16[4...) custom-call(f32[208,1536]{1,0:T(8,128)} %pad.15.refs_0_.refs_2_.refs_7_, f32[8,1536]{1,0:T(8,128)} %get-tuple-element.170.refs_1_, ...), custom_call_target="tpu_custom_call" | custom-call | flops 80499998720 | bytes 252000000 | tf_op jit(solution)/shard_map/self_in/pallas_call | solution.py:301
  196.7 4.9 fusion.114
  203.7 5.1 multiply_reduce_fusion
  208.9 5.0 collective-permute-start.5
  215.9 86.0 %self_attend.1 = (bf16[4,208,384]{2,1,0:T(8,128)(2,1)}, f32[208,1536]{1,0:T(8,128)}, f32[208,1536]{1,0:T(8,128)}, bf16[4,208,1536]{2,1,0:T(8,128)(2,1)}, bf16[4,...) custom-call(bf16[4,208,1152]{2,1,0:T(8,128)(2,1)} %get-tuple-element.63.refs_0_, ...), custom_call_target="tpu_custom_call" | custom-call | flops 92000002048 | bytes 288000000 | tf_op jit(solution)/shard_map/self_attend/pallas_call | solution.py:301
  302.0 6.4 add_convert_fusion.1
  313.2 60.2 %cross_attend.1 = (bf16[4,208,384]{2,1,0:T(8,128)(2,1)}, f32[208,1536]{1,0:T(8,128)}, bf16[4,208,1536]{2,1,0:T(8,128)(2,1)}, bf16[4,208,2240]{2,1,0:T(8,128)(2,1)}, f32[4,208,2240]{2,1,0:T(8,128)}) custom-call(f32[4,208,384]{2,1,0:T(8,128)} %get-tuple-element.64.refs_0_, f32[8,384]{1,0:T(8,128)} %pad.16.refs_4_.refs_1_.refs_2_, ...), custom_call_target="tpu_custom_call" | custom-call | flops 69000003584 | bytes 216000000 | tf_op jit(solution)/shard_map/cross_attend/pallas_call | solution.py:301
  373.5 9.9 bitcast_convert_fusion.1
  387.2 6.3 collective-permute-done.8
  393.5 4.8 add_convert_fusion
  398.4 74.2 %ffn_back.1 = (bf16[4,208,2240]{2,1,0:T(8,128)(2,1)}, f32[208,1536]{1,0:T(8,128)}, bf16[4,208,1536]{2,1,0:T(8,128)(2,1)}, bf16[4,208,384]{2,1,0:T(8,128)(2,1)}, f32[3,8,1536]{2,1,0:T(8,128)}) custom-call(bf16[4,208,1536]{2,1,0:T(8,128)(2,1)} %get-tuple-element.71.refs_0_, bf16[2,2240,768]{2,1,0:T(8,128)(2,1)} %bitcast.347, ...), custom_call_target="tpu_custom_call" | custom-call | flops 82800001024 | bytes 259200000 | tf_op jit(solution)/shard_map/ffn_back/pallas_call | solution.py:301
  472.6 11.4 %bitcast_convert_fusion = bf16[1536,2240]{0,1:T(8,128)(2,1)} fusion(bf16[4,208,1536]{2,1,0:T(8,128)(2,1)S(1)} %copy-done.66, bf16[4,208,2240]{2,1,0:T(8,128)(2,1)} %get-tuple-element.108), kind=kOutput, calls=%fused_computation | convolution fusion | flops 5728665600 | bytes 13164544 | tf_op jit(solution)/shard_map/dot_general | solution.py:72
  484.0 10.6 %copy.87 = bf16[1536,2240]{1,0:T(8,128)(2,1)} copy(bf16[1536,2240]{0,1:T(8,128)(2,1)} %bitcast_convert_fusion) | data formatting | bytes 13762560 | tf_op jit(solution)/shard_map/convert_element_type | solution.py:484
  494.6 4.0 dynamic-slice_bitcast_fusion
  501.7 3.5 collective-permute-done.10
  505.2 3.9 fusion.2
  511.3 89.5 %cross_back.1 = (bf16[4,208,384]{2,1,0:T(8,128)(2,1)}, bf16[4,512,768]{2,1,0:T(8,128)(2,1)}, f32[8,384]{1,0:T(8,128)}, f32[208,1536]{1,0:T(8,128)}, bf16[4,208,1...) custom-call(f32[4,208,384]{2,1,0:T(8,128)} %get-tuple-element.64.refs_0_, ...), custom_call_target="tpu_custom_call" | custom-call | flops 92000002048 | bytes 288000000 | tf_op jit(solution)/shard_map/cross_back/pallas_call | solution.py:301
  603.2 3.3 fusion.5
  612.8 135.9 %self_back.1 = (bf16[4,208,1152]{2,1,0:T(8,128)(2,1)}, f32[2,8,384]{2,1,0:T(8,128)}, f32[208,1536]{1,0:T(8,128)}, f32[2,8,1536]{2,1,0:T(8,128)}) custom-call(bf16[4,208,1152]{2,1,0:T(8,128)(2,1)} %get-tuple-element.63.refs_0_, bf16[4,208,384]{2,1,0:T(8,128)(2,1)} %get-tuple-element.79.refs_1_, f32[4,208,768]{2,1,0:T(8,128)} %get-tuple-element.80.refs_2_, ...), custom_call_target="tpu_custom_call" | custom-call | flops 138000007168 | bytes 432000000 | tf_op jit(solution)/shard_map/self_back/pallas_call | solution.py:301
  750.4 3.3 fusion.38
  759.8 16.3 %collective-permute-start.46 = (f32[8960]{0:T(1024)S(1)}, f32[8960]{0:T(1024)S(1)}, u32[]{:S(2)}, u32[]{:S(2)}) collective-permute-start(f32[8960]{0:T(1024)S(1)} %mul.453), channel_id=1, source_target_pairs={{0,1},{1,0},{2,3},{3,2},{4,5},{5,4},{6,7},{7,6},{8,9},{9,8},{10,11... | collective-permute-start | bytes 107528 | tf_op jit(solution)/shard_map/ppermute | solution.py:1050
  776.2 5.9 fusion
  794.3 3.3 fusion.41
  797.8 3.5 fusion.50
  801.3 3.7 collective-permute-done.47
  809.7 12.9 %collective-permute-done.49 = f32[8960]{0:T(1024)S(1)} collective-permute-done((f32[8960]{0:T(1024)S(1)}, f32[8960]{0:T(1024)S(1)}, u32[]{:S(2)}, u32[]{:S(2)}) %collective-permute-start.49) | collective-permute-done | bytes 35872 | tf_op jit(solution)/shard_map/ppermute | solution.py:412
  830.6 11.3 %collective-permute-done.15 = bf16[208,1536]{1,0:T(8,128)(2,1)S(1)} collective-permute-done((bf16[208,1536]{1,0:T(8,128)(2,1)S(1)}, bf16[208,1536]{1,0:T(8,128)(2,1)S(1)}, u32[]{:S(2)}, u32[]{:S(2)}) %collective-permute-start.15) | collective-permute-done | bytes 639008 | tf_op jit(solution)/shard_map/ppermute | solution.py:415
  844.7 15.2 %collective-permute-done.38 = bf16[560,768]{1,0:T(8,128)(2,1)S(1)} collective-permute-done((bf16[560,768]{1,0:T(8,128)(2,1)S(1)}, bf16[560,768]{1,0:T(8,128)(2,1)S(1)}, u32[]{:S(2)}, u32[]{:S(2)}) %collective-permute-start.38) | collective-permute-done | bytes 860192 | tf_op jit(solution)/shard_map/ppermute | solution.py:412
  869.2 8.6 collective-permute-done.18
  882.9 3.0 bitcast_convert_fusion.2
  889.8 4.5 copy.99
  894.3 6.7 reshape.922
  903.3 3.7 fusion.33
  907.6 7.2 collective-permute-done.28
  917.0 2.6 copy.93
  919.5 3.8 reshape.919
  948.0 6.4 collective-permute-done.23
  964.2 8.9 collective-permute-done.25
  973.3 5.0 collective-permute-done.41
  979.8 2.7 collective-permute-done.42
  997.0 4.6 collective-permute-done.32
  1004.9 6.0 collective-permute-done.33
  1013.3 2.6 reshape.921
  (453 shorter events, 178.8 us)
Async XLA Ops:
  7.2 58.6 %all-gather.8.cloned.1.call-start = ((), (), s32[]{:S(2)}) async-start(), calls=%async_computation.6 | async-start | bytes 1966080 | tf_op jit(solution)/shard_map/all_gather | solution.py:531
  7.9 84.0 %all-gather.6.cloned.1.call-start = ((), (), s32[]{:S(2)}) async-start(), calls=%async_computation.5 | async-start | bytes 3981312 | tf_op jit(solution)/shard_map/all_gather | solution.py:458
  11.7 8.5 collective-permute-start
  21.1 175.6 %all-gather.10.cloned.1.call-start = ((), (), s32[]{:S(2)}) async-start(), calls=%async_computation.7 | async-start | bytes 6635520 | tf_op jit(solution)/shard_map/all_gather | solution.py:478
  24.0 8.1 collective-permute-start.1
  33.2 279.4 %all-gather.12.cloned.1.call-start = ((), (), s32[]{:S(2)}) async-start(), calls=%async_computation.8 | async-start | bytes 7962624 | tf_op jit(solution)/shard_map/all_gather | solution.py:458
  37.1 11.9 %collective-permute-start.7 = (bf16[96,2240]{1,0:T(8,128)(2,1)S(1)}, bf16[96,2240]{1,0:T(8,128)(2,1)S(1)}, u32[]{:S(2)}, u32[]{:S(2)}) collective-permute-start(bf16[96,2240]{1,0:T(8,128)(2,1)S(1)} %bitcast.325), channel_id=1, source_target_pairs={{0,8},{8,0},{1,9},{9,1},{2,10},{10,2},{3,11},{11,3},{4,12},{12,4},... | collective-permute-start | bytes 1290248 | tf_op jit(solution)/shard_map/ppermute | solution.py:409
  50.2 348.2 %all-gather.14.cloned.1.call-start = ((), (), s32[]{:S(2)}) async-start(), calls=%async_computation.9 | async-start | bytes 7741440 | tf_op jit(solution)/shard_map/all_gather | solution.py:468
  51.2 13.1 %collective-permute-start.9 = (bf16[560,768]{1,0:T(8,128)(2,1)}, bf16[560,768]{1,0:T(8,128)(2,1)}, u32[]{:S(2)}, u32[]{:S(2)}) collective-permute-start(bf16[560,768]{1,0:T(8,128)(2,1)} %constant_dynamic-slice_fusion.10), channel_id=1, source_target_pairs={{0,4},{4,0},{1,5},{5,1},{2,6},{6,2},{3,7},{7,3},{8,12},{12,8},{9,1... | collective-permute-start | bytes 2580488 | tf_op jit(solution)/shard_map/ppermute | solution.py:418
  65.5 445.8 %reduce-scatter.6.cloned.1.call-start = ((), (), s32[]{:S(2)}) async-start(), calls=%async_computation.10 | async-start | bytes 4300800 | tf_op jit(solution)/shard_map/reduce_scatter | solution.py:498
  208.9 99.5 %collective-permute-start.6 = (f32[4,512]{1,0:T(4,128)S(1)}, f32[4,512]{1,0:T(4,128)S(1)}, u32[]{:S(2)}, u32[]{:S(2)}) collective-permute-start(f32[4,512]{1,0:T(4,128)S(1)} %get-tuple-element.212), channel_id=1, source_target_pairs={{0,24},{8,16},{16,8},{24,0},{1,25},{9,17},{17,9},{25,1},{2,26},{10... | collective-permute-start | bytes 24584 | tf_op jit(solution)/shard_map/ppermute | solution.py:415
  208.9 99.5 %collective-permute-start.5 = (f32[4,512]{1,0:T(4,128)S(1)}, f32[4,512]{1,0:T(4,128)S(1)}, u32[]{:S(2)}, u32[]{:S(2)}) collective-permute-start(f32[4,512]{1,0:T(4,128)S(1)} %get-tuple-element.212), channel_id=1, source_target_pairs={{0,16},{16,0},{1,17},{17,1},{2,18},{18,2},{3,19},{19,3},{4,20},{20... | collective-permute-start | bytes 24584 | tf_op jit(solution)/shard_map/ppermute | solution.py:412
  213.9 94.5 %collective-permute-start.4 = (f32[4,512]{1,0:T(4,128)S(1)}, f32[4,512]{1,0:T(4,128)S(1)}, u32[]{:S(2)}, u32[]{:S(2)}) collective-permute-start(f32[4,512]{1,0:T(4,128)S(1)} %get-tuple-element.212), channel_id=1, source_target_pairs={{0,8},{8,0},{1,9},{9,1},{2,10},{10,2},{3,11},{11,3},{4,12},{12,4},... | collective-permute-start | bytes 24584 | tf_op jit(solution)/shard_map/ppermute | solution.py:409
  387.2 6.3 collective-permute-start.8
  398.3 204.8 %reduce-scatter.8.cloned.1.call-start = ((), (), s32[]{:S(2)}) async-start(), calls=%async_computation.11 | async-start | bytes 4423680 | tf_op jit(solution)/shard_map/reduce_scatter | solution.py:498
  498.7 6.6 collective-permute-start.10
  511.2 350.0 %reduce-scatter.10.cloned.1.call-start = ((), (), s32[]{:S(2)}) async-start(), calls=%async_computation.12 | async-start | bytes 5406720 | tf_op jit(solution)/shard_map/reduce_scatter | solution.py:903
  612.7 253.1 %reduce-scatter.12.cloned.1.call-start = ((), (), s32[]{:S(2)}) async-start(), calls=%async_computation.13 | async-start | bytes 2211840 | tf_op jit(solution)/shard_map/reduce_scatter | solution.py:498
  757.8 72.8 %collective-permute-start.13 = (bf16[208,1536]{1,0:T(8,128)(2,1)}, bf16[208,1536]{1,0:T(8,128)(2,1)}, u32[]{:S(2)}, u32[]{:S(2)}) collective-permute-start(bf16[208,1536]{1,0:T(8,128)(2,1)} %pad_maximum_fusion.2), channel_id=1, source_target_pairs={{0,8},{8,0},{1,9},{9,1},{2,10},{10,2},{3,11},{11,3},{4,12},{12,4},... | collective-permute-start | bytes 1916936 | tf_op jit(solution)/shard_map/ppermute | solution.py:409
  759.8 37.8 %collective-permute-start.46 = (f32[8960]{0:T(1024)S(1)}, f32[8960]{0:T(1024)S(1)}, u32[]{:S(2)}, u32[]{:S(2)}) collective-permute-start(f32[8960]{0:T(1024)S(1)} %mul.453), channel_id=1, source_target_pairs={{0,1},{1,0},{2,3},{3,2},{4,5},{5,4},{6,7},{7,6},{8,9},{9,8},{10,11... | collective-permute-start | bytes 107528 | tf_op jit(solution)/shard_map/ppermute | solution.py:1050
  782.3 10.0 collective-permute-start.26
  784.1 44.5 %collective-permute-start.36 = (bf16[96,2240]{1,0:T(8,128)(2,1)}, bf16[96,2240]{1,0:T(8,128)(2,1)S(1)}, u32[]{:S(2)}, u32[]{:S(2)}) collective-permute-start(bf16[96,2240]{1,0:T(8,128)(2,1)} %get-tuple-element.147), channel_id=1, source_target_pairs={{0,8},{8,0},{1,9},{9,1},{2,10},{10,2},{3,11},{11,3},{4,12},{12,4},... | collective-permute-start | bytes 1290248 | tf_op jit(solution)/shard_map/ppermute | solution.py:409
  794.3 200.2 %reduce-scatter.14.cloned.1.call-start = ((), (), s32[]{:S(2)}) async-start(), calls=%async_computation.14 | async-start | bytes 2211840 | tf_op jit(solution)/shard_map/reduce_scatter | solution.py:498
  797.7 7.2 collective-permute-start.47
  805.0 25.6 %collective-permute-start.14 = (bf16[208,1536]{1,0:T(8,128)(2,1)S(1)}, bf16[208,1536]{1,0:T(8,128)(2,1)S(1)}, u32[]{:S(2)}, u32[]{:S(2)}) collective-permute-start(bf16[208,1536]{1,0:T(8,128)(2,1)S(1)} %pad_maximum_fusion.3), channel_id=1, source_target_pairs={{0,16},{16,0},{1,17},{17,1},{2,18},{18,2},{3,19},{19,3},{4,20},{20... | collective-permute-start | bytes 1916936 | tf_op jit(solution)/shard_map/ppermute | solution.py:412
  806.4 16.2 %collective-permute-start.49 = (f32[8960]{0:T(1024)S(1)}, f32[8960]{0:T(1024)S(1)}, u32[]{:S(2)}, u32[]{:S(2)}) collective-permute-start(f32[8960]{0:T(1024)S(1)} %add.376), channel_id=1, source_target_pairs={{0,16},{16,0},{1,17},{17,1},{2,18},{18,2},{3,19},{19,3},{4,20},{20... | collective-permute-start | bytes 107528 | tf_op jit(solution)/shard_map/ppermute | solution.py:412
  823.7 18.2 %collective-permute-start.15 = (bf16[208,1536]{1,0:T(8,128)(2,1)S(1)}, bf16[208,1536]{1,0:T(8,128)(2,1)S(1)}, u32[]{:S(2)}, u32[]{:S(2)}) collective-permute-start(bf16[208,1536]{1,0:T(8,128)(2,1)S(1)} %pad_maximum_fusion.4), channel_id=1, source_target_pairs={{0,24},{8,16},{16,8},{24,0},{1,25},{9,17},{17,9},{25,1},{2,26},{10... | collective-permute-start | bytes 1916936 | tf_op jit(solution)/shard_map/ppermute | solution.py:415
  826.7 33.2 %collective-permute-start.38 = (bf16[560,768]{1,0:T(8,128)(2,1)S(1)}, bf16[560,768]{1,0:T(8,128)(2,1)S(1)}, u32[]{:S(2)}, u32[]{:S(2)}) collective-permute-start(bf16[560,768]{1,0:T(8,128)(2,1)S(1)} %copy-done.25), channel_id=1, source_target_pairs={{0,16},{16,0},{1,17},{17,1},{2,18},{18,2},{3,19},{19,3},{4,20},{20... | collective-permute-start | bytes 2580488 | tf_op jit(solution)/shard_map/ppermute | solution.py:412
  829.6 58.3 %collective-permute-start.37 = (bf16[2,96,2240]{2,1,0:T(8,128)(2,1)}, bf16[2,96,2240]{2,1,0:T(8,128)(2,1)}, u32[]{:S(2)}, u32[]{:S(2)}) collective-permute-start(bf16[2,96,2240]{2,1,0:T(8,128)(2,1)} %maximum_select_fusion.6), channel_id=1, source_target_pairs={{0,16},{16,0},{1,17},{17,1},{2,18},{18,2},{3,19},{19,3},{4,20},{20... | collective-permute-start | bytes 2580488 | tf_op jit(solution)/shard_map/ppermute | solution.py:412
  861.2 42.0 %collective-permute-start.39 = (bf16[560,768]{1,0:T(8,128)(2,1)}, bf16[560,768]{1,0:T(8,128)(2,1)}, u32[]{:S(2)}, u32[]{:S(2)}) collective-permute-start(bf16[560,768]{1,0:T(8,128)(2,1)} %get-tuple-element.136), channel_id=1, source_target_pairs={{0,4},{4,0},{1,5},{5,1},{2,6},{6,2},{3,7},{7,3},{8,12},{12,8},{9,1... | collective-permute-start | bytes 2580488 | tf_op jit(solution)/shard_map/ppermute | solution.py:418
  863.9 14.0 %collective-permute-start.18 = (f32[4,128]{1,0:T(4,128)S(1)}, f32[4,128]{1,0:T(4,128)S(1)}, u32[]{:S(2)}, u32[]{:S(2)}) collective-permute-start(f32[4,128]{1,0:T(4,128)S(1)} %get-tuple-element.110), channel_id=1, source_target_pairs={{0,24},{8,16},{16,8},{24,0},{1,25},{9,17},{17,9},{25,1},{2,26},{10... | collective-permute-start | bytes 6152 | tf_op jit(solution)/shard_map/ppermute | solution.py:415
  867.5 33.5 %collective-permute-start.27 = (bf16[96,1152]{1,0:T(8,128)(2,1)}, bf16[96,1152]{1,0:T(8,128)(2,1)S(1)}, u32[]{:S(2)}, u32[]{:S(2)}) collective-permute-start(bf16[96,1152]{1,0:T(8,128)(2,1)} %get-tuple-element.155), channel_id=1, source_target_pairs={{0,8},{8,0},{1,9},{9,1},{2,10},{10,2},{3,11},{11,3},{4,12},{12,4},... | collective-permute-start | bytes 663560 | tf_op jit(solution)/shard_map/ppermute | solution.py:409
  868.5 10.4 %collective-permute-start.17 = (f32[4,128]{1,0:T(4,128)S(1)}, f32[4,128]{1,0:T(4,128)S(1)}, u32[]{:S(2)}, u32[]{:S(2)}) collective-permute-start(f32[4,128]{1,0:T(4,128)S(1)} %get-tuple-element.110), channel_id=1, source_target_pairs={{0,16},{16,0},{1,17},{17,1},{2,18},{18,2},{3,19},{19,3},{4,20},{20... | collective-permute-start | bytes 6152 | tf_op jit(solution)/shard_map/ppermute | solution.py:412
  887.9 41.8 %collective-permute-start.31 = (bf16[2,4,96,1152]{3,2,1,0:T(8,128)(2,1)}, bf16[2,4,96,1152]{3,2,1,0:T(8,128)(2,1)}, u32[]{:S(2)}, u32[]{:S(2)}) collective-permute-start(bf16[2,4,96,1152]{3,2,1,0:T(8,128)(2,1)} %fusion.30), channel_id=1, source_target_pairs={{0,4},{4,0},{1,5},{5,1},{2,6},{6,2},{3,7},{7,3},{8,12},{12,8},{9,1... | collective-permute-start | bytes 5308424 | tf_op jit(solution)/shard_map/ppermute | solution.py:418
  901.9 12.9 %collective-permute-start.28 = (bf16[2,96,1152]{2,1,0:T(8,128)(2,1)}, bf16[2,96,1152]{2,1,0:T(8,128)(2,1)}, u32[]{:S(2)}, u32[]{:S(2)}) collective-permute-start(bf16[2,96,1152]{2,1,0:T(8,128)(2,1)} %maximum_select_fusion.11), channel_id=1, source_target_pairs={{0,16},{16,0},{1,17},{17,1},{2,18},{18,2},{3,19},{19,3},{4,20},{20... | collective-permute-start | bytes 1327112 | tf_op jit(solution)/shard_map/ppermute | solution.py:412
  925.1 34.6 %collective-permute-start.29 = (bf16[96,768]{1,0:T(8,128)(2,1)}, bf16[96,768]{1,0:T(8,128)(2,1)S(1)}, u32[]{:S(2)}, u32[]{:S(2)}) collective-permute-start(bf16[96,768]{1,0:T(8,128)(2,1)} %get-tuple-element.145), channel_id=1, source_target_pairs={{0,16},{16,0},{1,17},{17,1},{2,18},{18,2},{3,19},{19,3},{4,20},{20... | collective-permute-start | bytes 442376 | tf_op jit(solution)/shard_map/ppermute | solution.py:412
  926.5 35.2 %collective-permute-start.34 = (bf16[96,768]{1,0:T(8,128)(2,1)}, bf16[96,768]{1,0:T(8,128)(2,1)}, u32[]{:S(2)}, u32[]{:S(2)}) collective-permute-start(bf16[96,768]{1,0:T(8,128)(2,1)} %get-tuple-element.144), channel_id=1, source_target_pairs={{0,16},{16,0},{1,17},{17,1},{2,18},{18,2},{3,19},{19,3},{4,20},{20... | collective-permute-start | bytes 442376 | tf_op jit(solution)/shard_map/ppermute | solution.py:412
  927.3 19.0 %collective-permute-start.22 = (f32[7,1536]{1,0:T(8,128)S(1)}, f32[7,1536]{1,0:T(8,128)S(1)}, u32[]{:S(2)}, u32[]{:S(2)}) collective-permute-start(f32[7,1536]{1,0:T(8,128)S(1)} %stack.230), channel_id=1, source_target_pairs={{0,1},{1,0},{2,3},{3,2},{4,5},{5,4},{6,7},{7,6},{8,9},{9,8},{10,11... | collective-permute-start | bytes 129032 | tf_op jit(solution)/shard_map/ppermute | solution.py:1050
  944.2 13.1 %collective-permute-start.24 = (f32[14,1536]{1,0:T(8,128)S(1)}, f32[14,1536]{1,0:T(8,128)S(1)}, u32[]{:S(2)}, u32[]{:S(2)}) collective-permute-start(f32[14,1536]{1,0:T(8,128)S(1)} %stack.233), channel_id=1, source_target_pairs={{0,1},{1,0},{2,3},{3,2},{4,5},{5,4},{6,7},{7,6},{8,9},{9,8},{10,11... | collective-permute-start | bytes 258056 | tf_op jit(solution)/shard_map/ppermute | solution.py:1050
  946.3 8.2 collective-permute-start.23
  956.0 33.9 %collective-permute-start.19 = (bf16[128,1536]{1,0:T(8,128)(2,1)}, bf16[128,1536]{1,0:T(8,128)(2,1)S(1)}, u32[]{:S(2)}, u32[]{:S(2)}) collective-permute-start(bf16[128,1536]{1,0:T(8,128)(2,1)} %fusion.8), channel_id=1, source_target_pairs={{0,8},{8,0},{1,9},{9,1},{2,10},{10,2},{3,11},{11,3},{4,12},{12,4},... | collective-permute-start | bytes 1179656 | tf_op jit(solution)/shard_map/ppermute | solution.py:409
  957.3 32.6 %collective-permute-start.20 = (bf16[128,1536]{1,0:T(8,128)(2,1)}, bf16[128,1536]{1,0:T(8,128)(2,1)S(1)}, u32[]{:S(2)}, u32[]{:S(2)}) collective-permute-start(bf16[128,1536]{1,0:T(8,128)(2,1)} %fusion.9), channel_id=1, source_target_pairs={{0,16},{16,0},{1,17},{17,1},{2,18},{18,2},{3,19},{19,3},{4,20},{20... | collective-permute-start | bytes 1179656 | tf_op jit(solution)/shard_map/ppermute | solution.py:412
  958.8 31.1 %collective-permute-start.21 = (bf16[128,1536]{1,0:T(8,128)(2,1)S(1)}, bf16[128,1536]{1,0:T(8,128)(2,1)S(1)}, u32[]{:S(2)}, u32[]{:S(2)}) collective-permute-start(bf16[128,1536]{1,0:T(8,128)(2,1)S(1)} %fusion.10), channel_id=1, source_target_pairs={{0,24},{8,16},{16,8},{24,0},{1,25},{9,17},{17,9},{25,1},{2,26},{10... | collective-permute-start | bytes 1179656 | tf_op jit(solution)/shard_map/ppermute | solution.py:415
  959.7 13.4 %collective-permute-start.25 = (f32[14,1536]{1,0:T(8,128)S(1)}, f32[14,1536]{1,0:T(8,128)S(1)}, u32[]{:S(2)}, u32[]{:S(2)}) collective-permute-start(f32[14,1536]{1,0:T(8,128)S(1)} %add.364), channel_id=1, source_target_pairs={{0,2},{1,3},{2,0},{3,1},{4,6},{5,7},{6,4},{7,5},{8,10},{9,11},{10,... | collective-permute-start | bytes 258056 | tf_op jit(solution)/shard_map/ppermute | solution.py:1051
  961.7 16.6 %collective-permute-start.41 = (f32[7,1536]{1,0:T(8,128)S(1)}, f32[7,1536]{1,0:T(8,128)S(1)}, u32[]{:S(2)}, u32[]{:S(2)}) collective-permute-start(f32[7,1536]{1,0:T(8,128)S(1)} %add.368), channel_id=1, source_target_pairs={{0,16},{16,0},{1,17},{17,1},{2,18},{18,2},{3,19},{19,3},{4,20},{20... | collective-permute-start | bytes 129032 | tf_op jit(solution)/shard_map/ppermute | solution.py:412
  973.1 10.8 %collective-permute-start.35 = (bf16[96,768]{1,0:T(8,128)(2,1)S(1)}, bf16[96,768]{1,0:T(8,128)(2,1)S(1)}, u32[]{:S(2)}, u32[]{:S(2)}) collective-permute-start(bf16[96,768]{1,0:T(8,128)(2,1)S(1)} %get-tuple-element.138), channel_id=1, source_target_pairs={{0,4},{4,0},{1,5},{5,1},{2,6},{6,2},{3,7},{7,3},{8,12},{12,8},{9,1... | collective-permute-start | bytes 442376 | tf_op jit(solution)/shard_map/ppermute | solution.py:418
  995.5 6.0 collective-permute-start.32
  1001.6 9.3 collective-permute-start.33
  (86 other events, 1055.4 us)
Sparse Core Ops, SparseCore 0:
  9.6 39.7 all-gather.7
  51.5 40.3 all-gather.5
  94.1 99.2 all-gather.9
  194.9 82.8 all-gather.11
  279.3 68.1 all-gather.13
  398.4 76.0 reduce-scatter.5
  511.3 88.0 reduce-scatter.7
  612.8 118.1 reduce-scatter.9
  794.4 36.4 reduce-scatter.11
  933.4 42.7 reduce-scatter.13

commit v4 on v3

--- a/solution.py
+++ b/solution.py
@@ -67,6 +67,18 @@
     return lax.optimization_barrier((value, done))[0]
 
 
+def tied(value, done):
+    anywhere = pl.BlockSpec(memory_space=pl.ANY)
+    return pl.pallas_call(
+        lambda *refs: None,
+        name="tied",
+        out_shape=jax.ShapeDtypeStruct(value.shape, value.dtype),
+        in_specs=[anywhere] * 2,
+        out_specs=anywhere,
+        input_output_aliases={0: 0},
+    )(value, done)
+
+
 def outer(a, b):
     lead = tuple(range(a.ndim - 1))
     return lax.dot_general(a, b, ((lead, lead), ((), ())), preferred_element_type=F32)
@@ -77,7 +89,7 @@
 
 
 class Links:
-    def __init__(self, named, stats, line):
+    def __init__(self, named, stats, line, pair):
         self.named = named
         self.used = 0
         self.started = []
@@ -87,6 +99,8 @@
         peers = [{"x": 1 - self.x}, {"y": 1 - self.y}]
         if stats:
             peers.append({"x": 1 - self.x, "y": 1 - self.y})
+        if pair:
+            peers.append({"core": 1 - lax.axis_index("core")})
         if line:
             peers += [{"z": (self.z + step) % self.seqs} for step in range(1, self.seqs)]
         for peer in peers:
@@ -99,7 +113,9 @@
         return ((piece // 2 + self.x) % 2) * 2 + (piece % 2 + self.y) % 2
 
     def send(self, axis, src, dst):
-        where = {a: 1 - lax.axis_index(a) for a in axis}
+        return self.send_to({a: 1 - lax.axis_index(a) for a in axis}, src, dst)
+
+    def send_to(self, where, src, dst):
         index = self.used
         self.used += 1
         sems = self.named.sems
@@ -169,8 +185,8 @@
         body(pl.ds(pl.multiple_of(step * ROWS, ROWS), ROWS), step)
 
 
-def reduce_slice(links, refs, partial, middle, keep=None):
-    mine, near, far, total = refs.mine, refs.near, refs.far, refs.total
+def reduce_begin(links, refs, buffers, partial):
+    mine, near, far, total = buffers
     tokens = total.shape[0]
     half = split_rows(tokens)
     top, low = pl.ds(0, half), pl.ds(half, tokens - half)
@@ -180,9 +196,6 @@
             mine[slot, :, columns] = value.astype(BF16)
 
         return store
-
-    def store_full(columns, value):
-        total[:, columns] = value
 
     partial(refs, 3, store_low(2))
     far_x = links.send("x", mine.at[2, top], far.at[top])
@@ -191,14 +204,36 @@
     x_top = links.send("x", mine.at[1, top], near.at[1, top])
     partial(refs, 1, store_low(0))
     y_low = links.send("y", mine.at[0, low], near.at[0, low])
+    return far_x, far_y, x_top, y_low
+
+
+def reduce_relay(links, buffers, copies):
+    mine, near, far, total = buffers
+    tokens = total.shape[0]
+    half = split_rows(tokens)
+    top, low = pl.ds(0, half), pl.ds(half, tokens - half)
+    far_x, far_y, x_top, y_low = copies
     far_x.wait_recv()
     mine[0, top] = (mine[0, top].astype(F32) + far[top].astype(F32)).astype(BF16)
     y_top = links.send("y", mine.at[0, top], near.at[0, top])
     far_y.wait_recv()
     mine[1, low] = (mine[1, low].astype(F32) + far[low].astype(F32)).astype(BF16)
     x_low = links.send("x", mine.at[1, low], near.at[1, low])
+    return x_top, y_low, y_top, x_low
+
+
+def reduce_own(refs, buffers, partial):
+    total = buffers[3]
+
+    def store_full(columns, value):
+        total[:, columns] = value
+
     partial(refs, 0, store_full)
-    for copy in (x_top, y_low, y_top, x_low):
+
+
+def reduce_end(refs, buffers, copies, middle, keep=None):
+    mine, near, far, total = buffers
+    for copy in copies:
         copy.wait_recv()
 
     def body(rows, step):
@@ -207,7 +242,15 @@
         if keep is not None:
             keep[0, rows] = sent
 
-    row_steps(tokens, body)
+    row_steps(total.shape[0], body)
+
+
+def reduce_slice(links, refs, partial, middle, keep=None):
+    buffers = (refs.mine, refs.near, refs.far, refs.total)
+    copies = reduce_begin(links, refs, buffers, partial)
+    copies = reduce_relay(links, buffers, copies)
+    reduce_own(refs, buffers, partial)
+    reduce_end(refs, buffers, copies, middle, keep)
 
 
 def gather_begin(links, held):
@@ -277,7 +320,7 @@
     return jnp.sum(jnp.where(same, row, 0.0), 1, keepdims=True)
 
 
-def run_kernel(name, cid, inputs, outputs, body, scratch, cost, stats=False, line=0):
+def run_kernel(name, cid, inputs, outputs, body, scratch, cost, stats=False, line=0, pair=False):
     names_in, names_out = list(inputs), list(outputs)
     spaces = dict(sems=pltpu.SemaphoreType.DMA((2, 24)))
     if line:
@@ -293,7 +336,7 @@
 
     def kernel(*refs):
         named = SimpleNamespace(**dict(zip(names_in + names_out + list(spaces), refs)))
-        links = Links(named, stats, line)
+        links = Links(named, stats, line, pair)
         body(links, named)
         links.finish()
 
@@ -468,14 +511,21 @@
         full = lax.all_gather(row_own(w), ("core", "z"), axis=0, tiled=True)
         return full.reshape(2, -1, full.shape[1])
 
-    def attention_blocks(w_cross, *row_weights):
+    def row_halves(w):
+        mine = row_own(w)
+        half = mine.shape[1] // 2
+        return jnp.stack([mine[:, :half], mine[:, half:]])
+
+    def attention_blocks(w_cross, w_out):
         own = column_own(w_cross)
         width = own.shape[2] // 3
         blocks = [own[:, :, g * width : (g + 1) * width] for g in range(3)]
-        for w in row_weights:
-            mine = row_own(w)
-            blocks.append(jnp.stack([mine[:, :width], mine[:, width:]]))
+        blocks.append(row_halves(w_out))
         return lax.all_gather(jnp.concatenate(blocks), ("core", "z"), axis=1, tiled=True)
+
+    def up_block(w_up, w_crossout):
+        own = jnp.concatenate([column_own(w_up[:, None, :]), row_halves(w_crossout)], 2)
+        return lax.all_gather(own, ("core", "z"), axis=1, tiled=True)
 
     def over_reps(a):
         return lax.psum(a, "rep") if reps > 1 else a
@@ -529,18 +579,20 @@
 
     full_qkv = column_block(w_qkv)
     text_z = lax.all_gather(text_emb, "z", axis=0, tiled=True)
-    attend_w = attention_blocks(w_cross, w_out, w_crossout)
+    attend_w = attention_blocks(w_cross, w_out)
     cross_wq, cross_wk, cross_wv = [
         attend_w[2 * g : 2 * g + 2].reshape(dim, -1) for g in range(3)
     ]
-    full_out, full_crossout = attend_w[6:8], attend_w[8:10]
-    full_up = column_block(w_up[:, None, :])
+    full_out = attend_w[6:8]
+    up_w = up_block(w_up, w_crossout)
+    hidden_width = w_up.shape[1] // 4
+    full_crossout = up_w[:, :, hidden_width:]
+    full_up = up_w.reshape(dim, -1)
     full_down = row_block(w_down)
     bias = pick(attn_bias)
     gain = pick(qk_gain)
     width = bias.shape[1]
     heads = width // HD
-    hidden_width = full_up.shape[1]
     own_tables = jnp.pad(jnp.concatenate(rope_tables(grid_pos), 1), pad)
     d_ffnout = (out_grad_p * gate2).astype(BF16)
 
@@ -827,9 +879,26 @@
         add_rows(refs.sums, 3, d_self * refs.branch[rows], step)
         return low
 
+    def ffn_out_partial(refs, k, store):
+        half_width = refs.w_down.shape[2]
+        for half in range(2):
+            for at, size in column_chunks(half_width, 384):
+                store(
+                    pl.ds(half * half_width + at, size),
+                    mm(refs.hidden[k], refs.w_down[half, :, pl.ds(at, size)]),
+                )
+
+    def ffn_out_rows(refs, rows, step, total):
+        ffn_out = total + refs.vec[2:3]
+        refs.block_out[rows] = refs.crossed[rows] + ffn_out * refs.vec[3:4]
+        add_rows(refs.sums, 4, refs.out_grad[rows] * ffn_out, step)
+
     def body(links, refs):
         refs.stat[...] = jnp.zeros_like(refs.stat)
         refs.gains[...] = jnp.zeros_like(refs.gains)
+        ffn_buffers = (refs.ffn_mine, refs.ffn_near, refs.ffn_far, refs.ffn_total)
+        copies = reduce_begin(links, refs, ffn_buffers, ffn_out_partial)
+        reduce_own(refs, ffn_buffers, ffn_out_partial)
 
         @pl.loop(0, 4)
         def _(k):
@@ -851,6 +920,7 @@
             refs.stat[k, pl.ds(0, 1), pl.ds(0, tokens)] = to_row(square)
 
         sum_stats(links, refs)
+        copies = reduce_relay(links, ffn_buffers, copies)
 
         @pl.loop(0, 4)
         def _(k):
@@ -866,6 +936,7 @@
 
         reduce_slice(links, refs, turned_partial("d_pre", "w"), middle, refs.held)
         gather_slice(links, refs, refs.held, product)
+        reduce_end(refs, ffn_buffers, copies, ffn_out_rows)
         for source in range(seqs):
             links.wait_line(refs.d_heads.at[source], source)
 
@@ -875,17 +946,19 @@
             unit=cq_unit, inv=cq_inv, gain=gains8, kv=text_kv,
             d_mix=after(d_cmix, up_core, down_part),
             w=cross_wq, joined=after_self, top=d_cross, branch=branch,
-            vec=vectors(norm_gain, gate1), w2=full_out,
+            vec=vectors(norm_gain, gate1, down_bias, gate2), w2=full_out,
+            hidden=hidden, w_down=full_down, crossed=after_cross, out_grad=out_grad_p,
         ),
         dict(
             d_pre=((4, tokens, width), BF16), d_kv=((4, texts, 2 * width), BF16),
             gains=((8, width), F32), d_self=wide, held=held,
-            d_heads=((seqs, tokens, width), BF16), sums=((4, 8, dim), F32),
+            d_heads=((seqs, tokens, width), BF16), sums=((5, 8, dim), F32), block_out=wide,
         ),
         body,
         dict(
             d_unit=((4, tokens, width), F32), outs=((4, tokens, width), BF16),
             **reduce_scratch(tokens, dim),
+            **{"ffn_" + n: v for n, v in reduce_scratch(tokens, dim).items()},
         ),
         stats=True, line=1,
         cost=80,
@@ -914,6 +987,14 @@
         refs.stat[...] = jnp.zeros_like(refs.stat)
         refs.gains[...] = jnp.zeros_like(refs.gains)
         packed, d_heads = refs.packed, refs.d_heads
+        x, y, core = links.x, links.y, lax.axis_index("core")
+        refs.ups[y, x] = refs.up_part[y]
+        refs.downs[x] = refs.down_part[...]
+        over_y = links.send("y", refs.up_part.at[1 - y], refs.ups.at[y, x])
+        over_x = [
+            links.send("x", refs.up_part.at[y], refs.ups.at[y, x]),
+            links.send("x", refs.down_part, refs.downs.at[x]),
+        ]
         for h in range(heads):
             refs.d_keys[...] = jnp.zeros_like(refs.d_keys)
             refs.d_values[...] = jnp.zeros_like(refs.d_values)
@@ -943,6 +1024,23 @@
                     refs.arrived.at[h, links.clip_of(links.z)],
                     to, step, h,
                 )
+            if h == 0:
+                over_y.wait_recv()
+                over_x.append(links.send("x", refs.ups.at[1 - y, x], refs.ups.at[1 - y, x]))
+            if h == 1:
+                over_x[1].wait_recv()
+                over_core = links.send(("core",), refs.downs.at[1 - core], refs.columns)
+
+        for copy in (over_x[0], over_x[2], over_core):
+            copy.wait_recv()
+        for block in range(4):
+            refs.up_grad[:, pl.ds(block * hidden_width, hidden_width)] = refs.ups[
+                block // 2, block % 2
+            ].astype(F32)
+        half = refs.columns.shape[1]
+        for part, value in ((core, refs.downs.at[core]), (1 - core, refs.columns)):
+            at = pl.ds(pl.multiple_of(part * half, half), half)
+            refs.down_grad[:, at] = value[...].astype(F32)
         for k in range(4):
             for h in range(heads):
                 links.wait_line(refs.arrived.at[h, k], links.clip_of(k), h)
@@ -987,10 +1085,13 @@
             packed=packed, d_heads=d_heads, unit=self_unit, inv=self_inv,
             gain=gains8, tables=tables, w=full_qkv, states=states_p,
             top=after(d_self, joint_core), vec=vectors(1.0 + scale1),
+            up_part=up_part.reshape(2, -1, hidden_width), down_part=down_part,
         ),
         dict(
             d_qkv=((4, tokens, blocks3), BF16), gains=((2, 8, width), F32),
             out=wide, sums=((2, 8, dim), F32),
+            up_grad=((up_part.shape[0] // 2, 4 * hidden_width), F32),
+            down_grad=((down_part.shape[0], dim), F32),
         ),
         body,
         dict(
@@ -998,15 +1099,15 @@
             arrived=((heads, 4, tokens, 3 * HD), BF16),
             d_keys=((clip_rows, HD), F32), d_values=((clip_rows, HD), F32),
             d_unit=((4, tokens, 2 * width), F32),
+            ups=((2, 2, up_part.shape[0] // 2, hidden_width), BF16),
+            downs=((2,) + down_part.shape, BF16), columns=(down_part.shape, BF16),
             **reduce_scratch(tokens, dim),
         ),
-        stats=True, line=heads,
+        stats=True, line=heads, pair=True,
         cost=120,
     )
-    d_qkv, hidden, d_hpre, d_cq, up_part, down_part = after(
-        (sixth.d_qkv, hidden, d_hpre, d_cq, up_part, down_part),
-        joint_part,
-    )
+    d_qkv = tied(sixth.d_qkv, joint_part)
+    d_hpre, d_cq = after((d_hpre, d_cq), d_qkv)
     text_rows, weight_rows = parts[0].shape[1], parts[1].shape[1]
     d_ckv = joint_part[:text_rows].reshape(4, -1, 2 * width)
     outproj_part = over_reps(joint_part[text_rows : text_rows + weight_rows])
@@ -1034,10 +1135,8 @@
     cross_core = column_core(jnp.concatenate([outer(x_cross, d_cq), outer(x_text, d_text)], 1))
     cross_part = scatter_z(cross_core)
 
-    ffn_out = reduce4(lambda k: rows_mm(hidden[k], full_down)) + down_bias
-    block_out = (after_cross + ffn_out * gate2)[:own_tokens]
-    up_grad = column_done(up_part, 1)[:, 0]
-    down_grad = row_done(down_part)
+    block_out = fifth.block_out[:own_tokens]
+    up_grad, down_grad = sixth.up_grad, sixth.down_grad
     qkv_grad = column_done(qkv_part, 3)
     outproj_grad = row_done(outproj_part)
     cross_grad = column_done(cross_part, 3)
@@ -1046,21 +1145,11 @@
     def column_sum(v):
         return jnp.sum(v.astype(F32), tuple(range(v.ndim - 1)))
 
-    def over_z(v):
-        v = v + lax.ppermute(v, "z", [(i, i ^ 1) for i in range(seqs)])
-        return v + lax.ppermute(v, "z", [(i, i ^ 2) for i in range(seqs)])
-
-    def over_clips(v):
-        v = v + from_core(v)
-        v = v + from_x(v)
-        v = v + from_y(v)
-        return over_reps(v)
-
     early = jnp.stack(
         [
             sums4[0],
             sums4[1],
-            column_sum(out_grad_p * ffn_out),
+            sums5[4],
             spread(column_sum(d_cq)),
             spread(column_sum(d_ck)),
             spread(column_sum(d_cv)),
@@ -1074,9 +1163,6 @@
             sums5[3],
         ]
     )
-    upbias = over_clips(over_z(spread(column_sum(d_hpre))))
-    early_clip = over_z(early)
-    early_all = over_clips(early_clip)
     late = jnp.stack(
         [
             sums6[0],
@@ -1088,8 +1174,36 @@
             spread(k_gain),
         ]
     )
-    late_clip = over_z(late)
-    late_all = over_clips(late_clip)
+    upbias_rows = jnp.pad(spread(column_sum(d_hpre)), (0, -4 * hidden_width % dim)).reshape(-1, dim)
+    counts = early.shape[0], late.shape[0], upbias_rows.shape[0]
+    rows = -(-sum(counts) // 8) * 8
+    small = jnp.concatenate([early, late, upbias_rows])
+    small = jnp.pad(small, ((0, rows - sum(counts)), (0, 0)))
+
+    def body(links, refs):
+        refs.stages[0] = refs.small[...]
+        flip = links.z + 1 - 2 * (links.z % 2)
+        hops = [
+            {"z": flip}, {"z": (links.z + seqs // 2) % seqs},
+            {"core": 1 - lax.axis_index("core")}, {"x": 1 - links.x}, {"y": 1 - links.y},
+        ]
+        for step, where in enumerate(hops):
+            copy = links.send_to(where, refs.stages.at[step], refs.others.at[step])
+            copy.wait_recv()
+            refs.stages[step + 1] = refs.stages[step] + refs.others[step]
+        refs.clip[...] = refs.stages[2]
+        refs.all[...] = refs.stages[5]
+
+    shape = ((rows, dim), F32)
+    summed = run_kernel(
+        "small_sums", 8, dict(small=after(small, cross_core)), dict(clip=shape, all=shape),
+        body, dict(stages=((6, rows, dim), F32), others=((5, rows, dim), F32)),
+        line=1, pair=True, cost=25,
+    )
+    total = over_reps(summed.all)
+    early_clip, late_clip = summed.clip[: counts[0]], summed.clip[counts[0] :]
+    early_all, late_all = total[: counts[0]], total[counts[0] :]
+    upbias = total[counts[0] + counts[1] : sum(counts)].reshape(-1)[: 4 * hidden_width]
 
     def mod_rows(e, l):
         return jnp.stack([l[0], l[1], e[13], e[0], e[1], e[2]])

time: 1030 us -> 956 us (0.928)
  waiting for transfers between devices: 157 us -> 82.8 us
  Pallas kernels: 550 us -> 617 us
  starting transfers between devices: 63 us -> 24.1 us
  matrix products: 80.2 us -> 51.1 us
    pallas_call x6 -> x7, Pallas kernels: 550 us -> 617 us  [run_kernel(): pl.pallas_call(kernel, name=name, out_shape=[jax.ShapeDtypeStruct(*output...]
    ppermute x13 -> x7, waiting for transfers between devices: 48.2 us -> 10.7 us  [from_x(): return lax.ppermute(a, 'x', SWAP)]
    ppermute x6 -> x0, starting transfers between devices: 20.6 us -> none  [the longest x3 18.4 us: over_z(): v = v + lax.ppermute(v, 'z', [(i, i ^ 1) for i in range(seqs)])]
    ppermute x6 -> x0, waiting for transfers between devices: 19 us -> none  [the longest x3 19 us: over_z(): return v + lax.ppermute(v, 'z', [(i, i ^ 2) for i in range(seqs)])]
    dot_general x10 -> x2, matrix products: 30.5 us -> 11.5 us  [mm(): lax.dot_general(a, b, (((a.ndim - 1,), (0,)), ((), ())), preferred_elemen...]
    convert_element_type x6 -> x4, local copies, waits for them, and re-layouts: 21.5 us -> 7.98 us  [column_done(): full.transpose(2, 3, 0, 1, 4).reshape(rows, groups, 4 * width).astype(F32)]
    ppermute x13 -> x7, starting transfers between devices: 19.5 us -> 5.97 us  [from_x(): return lax.ppermute(a, 'x', SWAP)]
    ppermute x4 -> x3, waiting for transfers between devices: 19.9 us -> 8.31 us  [from_xy(): return lax.ppermute(a, ('x', 'y'), [(i, 3 - i) for i in range(4)])]
  transfers between devices with their start and end apart: 61 -> 39, of which waited for: 24 -> 17; matrix products, arithmetic and copies ran while one was open for 21% -> 19% of each run, Pallas kernels for 54% -> 65%
where the time goes in v4:
time: 956 us; the launch traced here: 945 us
  Pallas kernels  617 us (65%)
  local copies, waits for them, and re-layouts  103 us (11%)
  waiting for transfers between devices  82.8 us (9%)
  other arithmetic  51.2 us (5%)
  matrix products  51.1 us (5%)
  starting transfers between devices  24.1 us (3%)
  between operations  16 us (2%)
    pallas_call x7, Pallas kernels, run_kernel(): pl.pallas_call(kernel, name=name, out_shape=[jax.ShapeDtypeStruct(*output...  617 us
    dot_general x7, matrix products, outer(): lax.dot_general(a, b, ((lead, lead), ((), ())), preferred_element_type=F32)  33.7 us
    ppermute x8, waiting for transfers between devices, from_y(): return lax.ppermute(a, 'y', SWAP)  28.3 us
    all_gather x1, waiting for transfers between devices, column_block(): full = lax.all_gather(column_own(w), ('core', 'z'), axis=1, tiled=True)  21.5 us
  transfers between devices with their start and end apart: 39, of which 17 were waited for; matrix products, arithmetic and copies ran while one was open for 19% of the time, Pallas kernels for 65%

profile of v4, /device:TPU:0, one launch (start us, length us, event | category | flops | bytes accessed | tf_op | source)
XLA Modules:
  0.0 945.5 jit_solution(1709485243201395519)
XLA Ops:
  8.0 2.4 reshape.687
  11.7 3.1 collective-permute-start
  15.3 4.9 collective-permute-done
  26.3 5.8 collective-permute-done.1
  41.7 10.7 %collective-permute-done.6 = bf16[96,2240]{1,0:T(8,128)(2,1)S(1)} collective-permute-done((bf16[96,2240]{1,0:T(8,128)(2,1)S(1)}, bf16[96,2240]{1,0:T(8,128)(2,1)S(1)}, u32[]{:S(2)}, u32[]{:S(2)}) %collective-permute-start.6) | collective-permute-done | bytes 430112 | tf_op jit(solution)/shard_map/ppermute | solution.py:452
  58.7 2.5 pad.23.refs_0_.refs_2_.refs_7_
  66.1 2.1 convert_reduce_fusion.2
  70.4 21.5 %all-gather.6.cloned.1.call-done = bf16[2,768,1152]{2,1,0:T(8,128)(2,1)} async-done(((bf16[2,96,1152]{2,1,0:T(8,128)(2,1)}), bf16[2,768,1152]{2,1,0:T(8,128)(2,1)}) %all-gather.6.cloned.1.call-update) | async-done | bytes 3538960 | tf_op jit(solution)/shard_map/all_gather | solution.py:501
  92.5 100.6 %self_in.1 = (bf16[4,208,1536]{2,1,0:T(8,128)(2,1)}, f32[4,208,768]{2,1,0:T(8,128)}, f32[4,8,256]{2,1,0:T(8,128)}, bf16[4,208,1152]{2,1,0:T(8,128)(2,1)}, bf16[4...) custom-call(f32[208,1536]{1,0:T(8,128)} %pad.23.refs_0_.refs_2_.refs_7_, f32[8,1536]{1,0:T(8,128)} %get-tuple-element.226.refs_1_, ...), custom_call_target="tpu_custom_call" | custom-call | flops 80499998720 | bytes 252000000 | tf_op jit(solution)/shard_map/self_in/pallas_call | solution.py:344
  193.1 4.4 fusion.56
  198.2 5.1 multiply_reduce_fusion
  207.5 86.1 %self_attend.1 = (bf16[4,208,384]{2,1,0:T(8,128)(2,1)}, f32[208,1536]{1,0:T(8,128)}, f32[208,1536]{1,0:T(8,128)}, bf16[4,208,1536]{2,1,0:T(8,128)(2,1)}, bf16[4,...) custom-call(bf16[4,208,1152]{2,1,0:T(8,128)(2,1)} %get-tuple-element.65.refs_0_, ...), custom_call_target="tpu_custom_call" | custom-call | flops 92000002048 | bytes 288000000 | tf_op jit(solution)/shard_map/self_attend/pallas_call | solution.py:344
  293.6 6.4 add_convert_fusion.1
  300.2 2.2 multiply_convert_fusion
  302.3 2.0 pad_maximum_fusion.1.refs_2_.refs_3_
  304.4 2.9 slice.464.refs_3_.refs_7_
  308.0 59.4 %cross_attend.1 = (bf16[4,208,384]{2,1,0:T(8,128)(2,1)}, f32[208,1536]{1,0:T(8,128)}, bf16[4,208,1536]{2,1,0:T(8,128)(2,1)}, bf16[4,208,2240]{2,1,0:T(8,128)(2,1)}, f32[4,208,2240]{2,1,0:T(8,128)}) custom-call(f32[4,208,384]{2,1,0:T(8,128)} %get-tuple-element.66.refs_0_, f32[8,384]{1,0:T(8,128)} %pad.24.refs_4_.refs_1_.refs_2_, ...), custom_call_target="tpu_custom_call" | custom-call | flops 69000003584 | bytes 216000000 | tf_op jit(solution)/shard_map/cross_attend/pallas_call | solution.py:344
  367.4 10.3 %bitcast_convert_fusion.1 = bf16[2240,1536]{1,0:T(8,128)(2,1)S(1)} fusion(bf16[4,208,2240]{2,1,0:T(8,128)(2,1)} %get-tuple-element.71.refs_11_, bf16[4,208,1536]{2,1,0:T(8,128)(2,1)S(1)} %copy-done.69), kind=kOutput, calls=%fused_computation.1 | convolution fusion | flops 5728665600 | bytes 13164544 | tf_op jit(solution)/shard_map/dot_general | solution.py:84
  377.6 2.1 constant_dynamic-slice_fusion.10
  381.6 6.3 collective-permute-done.8
  387.8 4.8 add_convert_fusion
  392.7 74.5 %ffn_back.1 = (bf16[4,208,2240]{2,1,0:T(8,128)(2,1)}, f32[208,1536]{1,0:T(8,128)}, bf16[4,208,1536]{2,1,0:T(8,128)(2,1)}, bf16[4,208,384]{2,1,0:T(8,128)(2,1)}, f32[3,8,1536]{2,1,0:T(8,128)}) custom-call(bf16[4,208,1536]{2,1,0:T(8,128)(2,1)} %get-tuple-element.72.refs_0_, bf16[2,2240,768]{2,1,0:T(8,128)(2,1)} %bitcast.312, ...), custom_call_target="tpu_custom_call" | custom-call | flops 82800001024 | bytes 259200000 | tf_op jit(solution)/shard_map/ffn_back/pallas_call | solution.py:344
  467.3 11.4 %bitcast_convert_fusion = bf16[1536,2240]{0,1:T(8,128)(2,1)} fusion(bf16[4,208,1536]{2,1,0:T(8,128)(2,1)S(1)} %copy-done.68, bf16[4,208,2240]{2,1,0:T(8,128)(2,1)} %get-tuple-element.105), kind=kOutput, calls=%fused_computation | convolution fusion | flops 5728665600 | bytes 13164544 | tf_op jit(solution)/shard_map/dot_general | solution.py:84
  478.6 10.4 %copy.95 = bf16[1536,2240]{1,0:T(8,128)(2,1)} copy(bf16[1536,2240]{0,1:T(8,128)(2,1)} %bitcast_convert_fusion) | data formatting | bytes 13762560 | tf_op jit(solution)/shard_map/convert_element_type | solution.py:534
  489.1 4.1 dynamic-slice_bitcast_fusion
  497.0 2.8 collective-permute-done.10
  499.8 3.9 fusion.2
  503.7 2.0 copy.96
  505.8 105.8 %cross_back.1 = (bf16[4,208,384]{2,1,0:T(8,128)(2,1)}, bf16[4,512,768]{2,1,0:T(8,128)(2,1)}, f32[8,384]{1,0:T(8,128)}, f32[208,1536]{1,0:T(8,128)}, bf16[4,208,1...) custom-call(f32[4,208,384]{2,1,0:T(8,128)} %get-tuple-element.66.refs_0_, ...), custom_call_target="tpu_custom_call" | custom-call | flops 92000002048 | bytes 288000000 | tf_op jit(solution)/shard_map/cross_back/pallas_call | solution.py:344
  614.7 2.4 slice.385
  622.6 2.2 pad_maximum_fusion
  625.0 142.1 %self_back.1 = (bf16[4,208,1152]{2,1,0:T(8,128)(2,1)}, f32[2,8,384]{2,1,0:T(8,128)}, f32[208,1536]{1,0:T(8,128)}, f32[2,8,1536]{2,1,0:T(8,128)}, f32[96,8960]{1,0:T(8,128)}, /*index=5*/f32[560,1536]{1,0:T(8,128)}) custom-call(bf16[4,208,1152]{2,1,0:T(8,128)(2,1)} %get-tuple-element.65.refs_0_, bf16[4,208,384]{2,1,0:T(8,128)(2,1)} %get-tuple-element.82.refs_1_, ...), custom_call_target="tpu_custom_call" | custom-call | flops 138000007168 | bytes 432000000 | tf_op jit(solution)/shard_map/self_back/pallas_call | solution.py:344
  768.8 2.4 slice.386
  779.4 2.9 convert_reduce_fusion
  786.0 4.5 fusion
  792.0 2.3 copy-done.66
  798.1 3.0 bitcast_convert_fusion.2
  804.8 2.4 fusion.12
  822.1 2.4 collective-permute-done.17
  824.5 8.3 collective-permute-done.18
  837.6 48.8 %small_sums.1 = (f32[32,1536]{1,0:T(8,128)}, f32[32,1536]{1,0:T(8,128)}) custom-call(f32[32,1536]{1,0:T(8,128)} %pad.28.refs_0_), custom_call_target="tpu_custom_call" | custom-call | flops 28750000128 | bytes 90000000 | tf_op jit(solution)/shard_map/small_sums/pallas_call | solution.py:344
  899.0 2.1 reduce-scatter.14.cloned.1.call-done
  903.8 2.8 collective-permute-done.21
  906.9 3.4 collective-permute-done.25
  911.8 8.1 collective-permute-done.22
  923.5 2.6 reshape.719
  929.9 2.6 reshape.720
  932.6 4.1 copy.146
  (376 shorter events, 119.6 us)
Async XLA Ops:
  7.2 48.0 %copy-start = (f32[4,1536]{1,0:T(4,128)S(1)}, f32[4,1536]{1,0:T(4,128)}, u32[]{:S(2)}) copy-start(f32[4,1536]{1,0:T(4,128)} %param.33) | copy-start | bytes 73732
  7.2 63.2 %all-gather.8.cloned.1.call-start = ((), (), s32[]{:S(2)}) async-start(), calls=%async_computation.6 | async-start | bytes 1966080 | tf_op jit(solution)/shard_map/all_gather | solution.py:581
  7.9 84.0 %all-gather.6.cloned.1.call-start = ((), (), s32[]{:S(2)}) async-start(), calls=%async_computation.5 | async-start | bytes 3981312 | tf_op jit(solution)/shard_map/all_gather | solution.py:501
  11.7 8.5 collective-permute-start
  21.0 172.1 %all-gather.10.cloned.1.call-start = ((), (), s32[]{:S(2)}) async-start(), calls=%async_computation.7 | async-start | bytes 5308416 | tf_op jit(solution)/shard_map/all_gather | solution.py:524
  21.8 4.4 collective-permute-start.2
  24.0 11.9 %copy-start.19 = (bf16[96,8960]{1,0:T(8,128)(2,1)S(1)}, bf16[96,8960]{1,0:T(8,128)(2,1)}, u32[]{:S(2)}) copy-start(bf16[96,8960]{1,0:T(8,128)(2,1)} %param.30) | copy-start | bytes 5160964
  24.0 8.2 collective-permute-start.1
  34.2 270.1 %all-gather.12.cloned.1.call-start = ((), (), s32[]{:S(2)}) async-start(), calls=%async_computation.8 | async-start | bytes 9289728 | tf_op jit(solution)/shard_map/all_gather | solution.py:528
  35.9 5.7 collective-permute-start.7
  39.8 12.6 %collective-permute-start.6 = (bf16[96,2240]{1,0:T(8,128)(2,1)S(1)}, bf16[96,2240]{1,0:T(8,128)(2,1)S(1)}, u32[]{:S(2)}, u32[]{:S(2)}) collective-permute-start(bf16[96,2240]{1,0:T(8,128)(2,1)S(1)} %bitcast.290), channel_id=1, source_target_pairs={{0,8},{8,0},{1,9},{9,1},{2,10},{10,2},{3,11},{11,3},{4,12},{12,4},... | collective-permute-start | bytes 1290248 | tf_op jit(solution)/shard_map/ppermute | solution.py:452
  53.9 338.8 %all-gather.14.cloned.1.call-start = ((), (), s32[]{:S(2)}) async-start(), calls=%async_computation.9 | async-start | bytes 7741440 | tf_op jit(solution)/shard_map/all_gather | solution.py:511
  55.2 13.8 %collective-permute-start.9 = (bf16[560,768]{1,0:T(8,128)(2,1)}, bf16[560,768]{1,0:T(8,128)(2,1)}, u32[]{:S(2)}, u32[]{:S(2)}) collective-permute-start(bf16[560,768]{1,0:T(8,128)(2,1)} %constant_dynamic-slice_fusion.9), channel_id=1, source_target_pairs={{0,4},{4,0},{1,5},{5,1},{2,6},{6,2},{3,7},{7,3},{8,12},{12,8},{9,1... | collective-permute-start | bytes 2580488 | tf_op jit(solution)/shard_map/ppermute | solution.py:461
  70.1 435.7 %reduce-scatter.6.cloned.1.call-start = ((), (), s32[]{:S(2)}) async-start(), calls=%async_computation.10 | async-start | bytes 4300800 | tf_op jit(solution)/shard_map/reduce_scatter | solution.py:548
  197.5 96.1 %copy-start.2 = (bf16[2,768,384]{2,1,0:T(8,128)(2,1)}, bf16[2,768,384]{2,1,0:T(8,128)(2,1)S(1)}, u32[]{:S(2)}) copy-start(bf16[2,768,384]{2,1,0:T(8,128)(2,1)S(1)} %get-tuple-element.182) | copy-start | bytes 3538948
  203.4 96.7 %collective-permute-start.5 = (f32[4,512]{1,0:T(4,128)S(1)}, f32[4,512]{1,0:T(4,128)S(1)}, u32[]{:S(2)}, u32[]{:S(2)}) collective-permute-start(f32[4,512]{1,0:T(4,128)S(1)} %get-tuple-element.265), channel_id=1, source_target_pairs={{0,24},{8,16},{16,8},{24,0},{1,25},{9,17},{17,9},{25,1},{2,26},{10... | collective-permute-start | bytes 24584 | tf_op jit(solution)/shard_map/ppermute | solution.py:458
  205.1 95.0 %collective-permute-start.4 = (f32[4,512]{1,0:T(4,128)S(1)}, f32[4,512]{1,0:T(4,128)S(1)}, u32[]{:S(2)}, u32[]{:S(2)}) collective-permute-start(f32[4,512]{1,0:T(4,128)S(1)} %get-tuple-element.265), channel_id=1, source_target_pairs={{0,16},{16,0},{1,17},{17,1},{2,18},{18,2},{3,19},{19,3},{4,20},{20... | collective-permute-start | bytes 24584 | tf_op jit(solution)/shard_map/ppermute | solution.py:455
  206.4 93.7 %collective-permute-start.3 = (f32[4,512]{1,0:T(4,128)S(1)}, f32[4,512]{1,0:T(4,128)S(1)}, u32[]{:S(2)}, u32[]{:S(2)}) collective-permute-start(f32[4,512]{1,0:T(4,128)S(1)} %get-tuple-element.265), channel_id=1, source_target_pairs={{0,8},{8,0},{1,9},{9,1},{2,10},{10,2},{3,11},{11,3},{4,12},{12,4},... | collective-permute-start | bytes 24584 | tf_op jit(solution)/shard_map/ppermute | solution.py:452
  207.5 86.1 %copy-start.60 = (f32[384]{0:T(512)S(1)}, f32[384]{0:T(512)}, u32[]{:S(2)}) copy-start(f32[384]{0:T(512)} %get-tuple-element.172) | copy-start | bytes 4612
  307.9 59.4 %copy-start.69 = (bf16[4,208,1536]{2,1,0:T(8,128)(2,1)S(1)}, bf16[4,208,1536]{2,1,0:T(8,128)(2,1)}, u32[]{:S(2)}) copy-start(bf16[4,208,1536]{2,1,0:T(8,128)(2,1)} %get-tuple-element.72.refs_0_) | copy-start | bytes 7667716
  381.6 6.3 collective-permute-start.8
  392.6 224.5 %reduce-scatter.8.cloned.1.call-start = ((), (), s32[]{:S(2)}) async-start(), calls=%async_computation.11 | async-start | bytes 4423680 | tf_op jit(solution)/shard_map/reduce_scatter | solution.py:548
  392.7 74.5 %copy-start.68 = (bf16[4,208,1536]{2,1,0:T(8,128)(2,1)S(1)}, bf16[4,208,1536]{2,1,0:T(8,128)(2,1)}, u32[]{:S(2)}) copy-start(bf16[4,208,1536]{2,1,0:T(8,128)(2,1)} %get-tuple-element.76) | copy-start | bytes 7667716
  493.2 6.6 collective-permute-start.10
  505.8 265.4 %reduce-scatter.10.cloned.1.call-start = ((), (), s32[]{:S(2)}) async-start(), calls=%async_computation.12 | async-start | bytes 5406720 | tf_op jit(solution)/shard_map/reduce_scatter | solution.py:976
  505.8 111.3 %copy-start.26 = (bf16[4,208,384]{2,1,0:T(8,128)(2,1)S(1)}, bf16[4,208,384]{2,1,0:T(8,128)(2,1)}, u32[]{:S(2)}) copy-start(bf16[4,208,384]{2,1,0:T(8,128)(2,1)} %get-tuple-element.91) | copy-start | bytes 1916932
  618.6 3.0 collective-permute-start.11
  620.4 2.1 collective-permute-start.12
  624.9 272.3 %reduce-scatter.12.cloned.1.call-start = ((), (), s32[]{:S(2)}) async-start(), calls=%async_computation.13 | async-start | bytes 2211840 | tf_op jit(solution)/shard_map/reduce_scatter | solution.py:548
  773.8 22.7 %collective-permute-start.15 = (f32[4,128]{1,0:T(4,128)S(1)}, f32[4,128]{1,0:T(4,128)S(1)}, u32[]{:S(2)}, u32[]{:S(2)}) collective-permute-start(f32[4,128]{1,0:T(4,128)S(1)} %get-tuple-element.165), channel_id=1, source_target_pairs={{0,24},{8,16},{16,8},{24,0},{1,25},{9,17},{17,9},{25,1},{2,26},{10... | collective-permute-start | bytes 6152 | tf_op jit(solution)/shard_map/ppermute | solution.py:458
  775.4 21.2 %collective-permute-start.14 = (f32[4,128]{1,0:T(4,128)S(1)}, f32[4,128]{1,0:T(4,128)S(1)}, u32[]{:S(2)}, u32[]{:S(2)}) collective-permute-start(f32[4,128]{1,0:T(4,128)S(1)} %get-tuple-element.165), channel_id=1, source_target_pairs={{0,16},{16,0},{1,17},{17,1},{2,18},{18,2},{3,19},{19,3},{4,20},{20... | collective-permute-start | bytes 6152 | tf_op jit(solution)/shard_map/ppermute | solution.py:455
  775.7 20.9 %collective-permute-start.13 = (f32[4,128]{1,0:T(4,128)S(1)}, f32[4,128]{1,0:T(4,128)S(1)}, u32[]{:S(2)}, u32[]{:S(2)}) collective-permute-start(f32[4,128]{1,0:T(4,128)S(1)} %get-tuple-element.165), channel_id=1, source_target_pairs={{0,8},{8,0},{1,9},{9,1},{2,10},{10,2},{3,11},{11,3},{4,12},{12,4},... | collective-permute-start | bytes 6152 | tf_op jit(solution)/shard_map/ppermute | solution.py:452
  784.0 31.2 %collective-permute-start.23 = (bf16[96,768]{1,0:T(8,128)(2,1)}, bf16[96,768]{1,0:T(8,128)(2,1)S(1)}, u32[]{:S(2)}, u32[]{:S(2)}) collective-permute-start(bf16[96,768]{1,0:T(8,128)(2,1)} %get-tuple-element.195), channel_id=1, source_target_pairs={{0,16},{16,0},{1,17},{17,1},{2,18},{18,2},{3,19},{19,3},{4,20},{20... | collective-permute-start | bytes 442376 | tf_op jit(solution)/shard_map/ppermute | solution.py:455
  785.4 31.3 %collective-permute-start.27 = (bf16[96,768]{1,0:T(8,128)(2,1)}, bf16[96,768]{1,0:T(8,128)(2,1)S(1)}, u32[]{:S(2)}, u32[]{:S(2)}) collective-permute-start(bf16[96,768]{1,0:T(8,128)(2,1)} %get-tuple-element.194), channel_id=1, source_target_pairs={{0,16},{16,0},{1,17},{17,1},{2,18},{18,2},{3,19},{19,3},{4,20},{20... | collective-permute-start | bytes 442376 | tf_op jit(solution)/shard_map/ppermute | solution.py:455
  796.5 8.3 collective-permute-start.20
  803.0 31.2 %collective-permute-start.19 = (bf16[2,4,96,1152]{3,2,1,0:T(8,128)(2,1)}, bf16[2,4,96,1152]{3,2,1,0:T(8,128)(2,1)}, u32[]{:S(2)}, u32[]{:S(2)}) collective-permute-start(bf16[2,4,96,1152]{3,2,1,0:T(8,128)(2,1)} %fusion.14), channel_id=1, source_target_pairs={{0,4},{4,0},{1,5},{5,1},{2,6},{6,2},{3,7},{7,3},{8,12},{12,8},{9,1... | collective-permute-start | bytes 5308424 | tf_op jit(solution)/shard_map/ppermute | solution.py:461
  808.6 92.5 %reduce-scatter.14.cloned.1.call-start = ((), (), s32[]{:S(2)}) async-start(), calls=%async_computation.14 | async-start | bytes 2211840 | tf_op jit(solution)/shard_map/reduce_scatter | solution.py:548
  811.0 11.1 %collective-permute-start.16 = (bf16[128,1536]{1,0:T(8,128)(2,1)S(1)}, bf16[128,1536]{1,0:T(8,128)(2,1)S(1)}, u32[]{:S(2)}, u32[]{:S(2)}) collective-permute-start(bf16[128,1536]{1,0:T(8,128)(2,1)S(1)} %fusion.8), channel_id=1, source_target_pairs={{0,8},{8,0},{1,9},{9,1},{2,10},{10,2},{3,11},{11,3},{4,12},{12,4},... | collective-permute-start | bytes 1179656 | tf_op jit(solution)/shard_map/ppermute | solution.py:452
  812.4 12.1 %collective-permute-start.17 = (bf16[128,1536]{1,0:T(8,128)(2,1)S(1)}, bf16[128,1536]{1,0:T(8,128)(2,1)S(1)}, u32[]{:S(2)}, u32[]{:S(2)}) collective-permute-start(bf16[128,1536]{1,0:T(8,128)(2,1)S(1)} %fusion.9), channel_id=1, source_target_pairs={{0,16},{16,0},{1,17},{17,1},{2,18},{18,2},{3,19},{19,3},{4,20},{20... | collective-permute-start | bytes 1179656 | tf_op jit(solution)/shard_map/ppermute | solution.py:455
  815.2 17.6 %collective-permute-start.18 = (bf16[128,1536]{1,0:T(8,128)(2,1)S(1)}, bf16[128,1536]{1,0:T(8,128)(2,1)S(1)}, u32[]{:S(2)}, u32[]{:S(2)}) collective-permute-start(bf16[128,1536]{1,0:T(8,128)(2,1)S(1)} %fusion.10), channel_id=1, source_target_pairs={{0,24},{8,16},{16,8},{24,0},{1,25},{9,17},{17,9},{25,1},{2,26},{10... | collective-permute-start | bytes 1179656 | tf_op jit(solution)/shard_map/ppermute | solution.py:458
  817.8 1.4 collective-permute-start.28
  819.2 1.4 collective-permute-start.24
  820.6 13.7 %copy-start.7 = (bf16[1536,768]{1,0:T(8,128)(2,1)S(1)}, bf16[1536,768]{1,0:T(8,128)(2,1)}, u32[]{:S(2)}) copy-start(bf16[1536,768]{1,0:T(8,128)(2,1)} %copy-done.6) | copy-start | bytes 7077892
  820.6 13.7 %copy-start.11 = (bf16[1536,384]{1,0:T(8,128)(2,1)S(1)}, bf16[1536,384]{1,0:T(8,128)(2,1)}, u32[]{:S(2)}) copy-start(bf16[1536,384]{1,0:T(8,128)(2,1)} %copy-done.10) | copy-start | bytes 3538948
  898.3 8.4 collective-permute-start.21
  902.2 8.1 collective-permute-start.25
  906.7 13.2 %collective-permute-start.22 = (bf16[2,96,1152]{2,1,0:T(8,128)(2,1)S(1)}, bf16[2,96,1152]{2,1,0:T(8,128)(2,1)}, u32[]{:S(2)}, u32[]{:S(2)}) collective-permute-start(bf16[2,96,1152]{2,1,0:T(8,128)(2,1)S(1)} %maximum_select_fusion.7), channel_id=1, source_target_pairs={{0,16},{16,0},{1,17},{17,1},{2,18},{18,2},{3,19},{19,3},{4,20},{20... | collective-permute-start | bytes 1327112 | tf_op jit(solution)/shard_map/ppermute | solution.py:455
  910.3 16.0 %collective-permute-start.26 = (bf16[2,96,1152]{2,1,0:T(8,128)(2,1)S(1)}, bf16[2,96,1152]{2,1,0:T(8,128)(2,1)}, u32[]{:S(2)}, u32[]{:S(2)}) collective-permute-start(bf16[2,96,1152]{2,1,0:T(8,128)(2,1)S(1)} %maximum_select_fusion.8), channel_id=1, source_target_pairs={{0,16},{16,0},{1,17},{17,1},{2,18},{18,2},{3,19},{19,3},{4,20},{20... | collective-permute-start | bytes 1327112 | tf_op jit(solution)/shard_map/ppermute | solution.py:455
  (62 other events, 275.8 us)
Sparse Core Ops, SparseCore 0:
  9.6 39.7 all-gather.7
  51.5 40.3 all-gather.5
  94.1 85.9 all-gather.9
  181.6 92.7 all-gather.11
  275.8 68.0 all-gather.13
  392.8 74.1 reduce-scatter.5
  505.9 76.2 reduce-scatter.7
  625.0 117.6 reduce-scatter.9
  808.8 50.0 reduce-scatter.11
  861.6 39.4 reduce-scatter.13

commit v5 on v4

--- a/solution.py
+++ b/solution.py
@@ -89,14 +89,14 @@
 
 
 class Links:
-    def __init__(self, named, stats, line, pair):
+    def __init__(self, named, stats, line, pair, near):
         self.named = named
         self.used = 0
         self.started = []
         self.x, self.y, self.z = [lax.axis_index(n) for n in ("x", "y", "z")]
         self.seqs = lax.axis_size("z")
         barrier = pltpu.get_barrier_semaphore()
-        peers = [{"x": 1 - self.x}, {"y": 1 - self.y}]
+        peers = [{"x": 1 - self.x}, {"y": 1 - self.y}] if near else []
         if stats:
             peers.append({"x": 1 - self.x, "y": 1 - self.y})
         if pair:
@@ -320,7 +320,7 @@
     return jnp.sum(jnp.where(same, row, 0.0), 1, keepdims=True)
 
 
-def run_kernel(name, cid, inputs, outputs, body, scratch, cost, stats=False, line=0, pair=False):
+def run_kernel(name, cid, inputs, outputs, body, scratch, cost, stats=False, line=0, pair=False, near=True):
     names_in, names_out = list(inputs), list(outputs)
     spaces = dict(sems=pltpu.SemaphoreType.DMA((2, 24)))
     if line:
@@ -336,7 +336,7 @@
 
     def kernel(*refs):
         named = SimpleNamespace(**dict(zip(names_in + names_out + list(spaces), refs)))
-        links = Links(named, stats, line, pair)
+        links = Links(named, stats, line, pair, near)
         body(links, named)
         links.finish()
 
@@ -432,6 +432,73 @@
 
 def head_at(h, base=0):
     return pl.ds(base + h * HD, HD)
+
+
+def column_terms(a, b, c, seqs, at, store):
+    tall, quarter = a.shape[0] * a.shape[1], a.shape[2] // 4
+    rows = quarter // seqs
+    for part in range(2):
+        lanes = pl.ds(pl.multiple_of((part * 2 + c) * quarter, HD), quarter)
+        left = a[:, :, lanes].reshape(tall, quarter)
+        for column, size in column_chunks(b.shape[2], 640):
+            value = mm_l(left, b[:, :, pl.ds(column, size)].reshape(tall, size))
+            for z in range(seqs):
+                store(
+                    (z, part, slice(None), pl.ds(at + column, size)),
+                    value[z * rows : (z + 1) * rows],
+                )
+
+
+def row_terms(a, b, c, store):
+    tall, half = a.shape[0] * a.shape[1], b.shape[2] // 2
+    right = b[:, :, pl.ds(pl.multiple_of(c * half, HD), half)].reshape(tall, half)
+    for row, size in column_chunks(a.shape[2], 640):
+        value = mm_l(a[:, :, pl.ds(row, size)].reshape(tall, size), right)
+        store((pl.ds(row, size), slice(None)), value)
+
+
+def weight_sums(name, cid, shapes, jobs, seqs, cost):
+    inputs, outputs, scratch = {}, {}, {}
+    for index, (out, left, right, column) in enumerate(jobs):
+        inputs[f"a{index}"], inputs[f"b{index}"] = left, right
+    for index, shape in enumerate(shapes):
+        outputs[f"out{index}"] = (shape, BF16)
+        scratch[f"mine{index}"] = scratch[f"theirs{index}"] = (shape, BF16)
+
+    def body(links, refs):
+        core = lax.axis_index("core")
+
+        def terms(c, out, store):
+            for index, (into, _, _, column) in enumerate(jobs):
+                if into != out:
+                    continue
+                a, b = getattr(refs, f"a{index}"), getattr(refs, f"b{index}")
+                if column is None:
+                    row_terms(a, b, c, store)
+                else:
+                    column_terms(a, b, c, seqs, column, store)
+
+        copies = []
+        for out in range(len(shapes)):
+            mine, theirs = getattr(refs, f"mine{out}"), getattr(refs, f"theirs{out}")
+
+            def store_mine(at, value):
+                mine[at] = value.astype(BF16)
+
+            terms(1 - core, out, store_mine)
+            copies.append(links.send(("core",), mine, theirs))
+        for out in range(len(shapes)):
+            result, theirs = getattr(refs, f"out{out}"), getattr(refs, f"theirs{out}")
+
+            def store_result(at, value):
+                result[at] = value.astype(BF16)
+
+            terms(core, out, store_result)
+            copies[out].wait_recv()
+            result[...] = (result[...].astype(F32) + theirs[...].astype(F32)).astype(BF16)
+
+    done = run_kernel(name, cid, inputs, outputs, body, scratch, cost=cost, pair=True, near=False)
+    return [getattr(done, f"out{index}") for index in range(len(shapes))]
 
 
 def on_device(
@@ -529,20 +596,6 @@
 
     def over_reps(a):
         return lax.psum(a, "rep") if reps > 1 else a
-
-    def column_core(g):
-        g = g.astype(BF16).reshape(2, 2, seqs, -1, g.shape[1])
-        keep = lax.dynamic_index_in_dim(g, core, 1, False)
-        recv = from_core(lax.dynamic_index_in_dim(g, 1 - core, 1, False))
-        both = (keep.astype(F32) + recv.astype(F32)).astype(BF16)
-        return both.transpose(1, 0, 2, 3).reshape(-1, g.shape[4])
-
-    def row_core(g):
-        half = g.shape[1] // 2
-        g = g.astype(BF16)
-        keep = lax.dynamic_slice_in_dim(g, core * half, half, 1)
-        recv = from_core(lax.dynamic_slice_in_dim(g, (1 - core) * half, half, 1))
-        return (keep.astype(F32) + recv.astype(F32)).astype(BF16)
 
     def scatter_z(a):
         return over_reps(lax.psum_scatter(a, "z", scatter_dimension=0, tiled=True))
@@ -814,7 +867,9 @@
     )
     cross_mix, after_cross, x_ffn, hidden = third.mix, third.joined, third.held, third.hidden
 
-    down_core = row_core(outer(hidden, g_ffn))
+    (down_core,) = weight_sums(
+        "down_sums", 9, [(hidden_width, dim // 2)], [(0, hidden, g_ffn, None)], seqs, cost=14
+    )
     down_part = scatter_z(down_core)
     inner_partial = turned_partial("d_hpre", "w_up")
 
@@ -861,8 +916,11 @@
     )
     d_hpre, d_cross, g_cross, d_cmix = fourth.d_hpre, fourth.d_cross, fourth.held, fourth.d_mix
     sums4 = jnp.sum(fourth.sums, 1)
-    up_core = column_core(outer(x_ffn, d_hpre))
-    up_part = scatter_z(up_core)
+    spread_rows = (seqs, 2, dim // (4 * seqs))
+    (up_core,) = weight_sums(
+        "up_sums", 10, [spread_rows + (hidden_width,)], [(0, x_ffn, d_hpre, 0)], seqs, cost=14
+    )
+    up_part = scatter_z(up_core.reshape(-1, hidden_width))
 
     def rms_back(grad, unit, inverse, mean):
         return inverse * (grad - unit * mean)
@@ -967,8 +1025,10 @@
     cq_gain = jnp.sum(fifth.gains, 0)
     sums5 = jnp.sum(fifth.sums, 1)
     d_kv, mixed, cross_mix = after((fifth.d_kv, mixed, cross_mix), up_part)
-    outproj_core = row_core(outer(mixed, g_self))
-    crossout_core = row_core(outer(cross_mix, g_cross))
+    outproj_core, crossout_core = weight_sums(
+        "output_sums", 11, [(width, dim // 2)] * 2,
+        [(0, mixed, g_self, None), (1, cross_mix, g_cross, None)], seqs, cost=8,
+    )
     d_kv = d_kv.reshape(4, seqs, -1, 2 * width).transpose(1, 0, 2, 3)
     parts = [d_kv.reshape(seqs, -1, 2 * width)]
     parts += [v.reshape(seqs, -1, 2 * width) for v in (outproj_core, crossout_core)]
@@ -1116,8 +1176,6 @@
     q_gain, k_gain = jnp.sum(sixth.gains, 1)
     states_grad = sixth.out[:own_tokens]
     sums6 = jnp.sum(sixth.sums, 1)
-    qkv_core = column_core(outer(x_self, d_qkv))
-    qkv_part = scatter_z(qkv_core)
 
     d_ckn = d_ckv[..., :width].astype(F32)
     d_cv = d_ckv[..., width:]
@@ -1132,14 +1190,18 @@
     ck_gain = jnp.sum(d_ckn * ck_unit, (0, 1))
     d_text = jnp.concatenate([d_ck, d_cv], -1)
     text_grad = reduce4(lambda k: mm_t(d_ck[k], cross_wk) + mm_t(d_cv[k], cross_wv))
-    cross_core = column_core(jnp.concatenate([outer(x_cross, d_cq), outer(x_text, d_text)], 1))
-    cross_part = scatter_z(cross_core)
+    (last_core,) = weight_sums(
+        "last_sums", 12, [spread_rows + (2 * blocks3,)],
+        [(0, x_self, d_qkv, 0), (0, x_cross, d_cq, blocks3), (0, x_text, d_text, blocks3 + width)],
+        seqs, cost=16,
+    )
+    last_part = scatter_z(last_core.reshape(-1, 2 * blocks3))
 
     block_out = fifth.block_out[:own_tokens]
     up_grad, down_grad = sixth.up_grad, sixth.down_grad
-    qkv_grad = column_done(qkv_part, 3)
+    both_grad = column_done(last_part, 6)
+    qkv_grad, cross_grad = both_grad[:, :3], both_grad[:, 3:]
     outproj_grad = row_done(outproj_part)
-    cross_grad = column_done(cross_part, 3)
     crossout_grad = row_done(crossout_part)
 
     def column_sum(v):
@@ -1196,7 +1258,7 @@
 
     shape = ((rows, dim), F32)
     summed = run_kernel(
-        "small_sums", 8, dict(small=after(small, cross_core)), dict(clip=shape, all=shape),
+        "small_sums", 8, dict(small=after(small, last_core)), dict(clip=shape, all=shape),
         body, dict(stages=((6, rows, dim), F32), others=((5, rows, dim), F32)),
         line=1, pair=True, cost=25,
     )

time: 956 us -> 937 us (0.980)
  Pallas kernels: 617 us -> 684 us
  matrix products: 51.1 us -> 20 us
  local copies, waits for them, and re-layouts: 103 us -> 81.9 us
  other arithmetic: 51.2 us -> 34.2 us
  waiting for transfers between devices: 82.8 us -> 68 us
    pallas_call x7 -> x11, Pallas kernels: 617 us -> 684 us  [run_kernel(): pl.pallas_call(kernel, name=name, out_shape=[jax.ShapeDtypeStruct(*output...]
    dot_general x7 -> x0, matrix products: 33.7 us -> none  [outer(): lax.dot_general(a, b, ((lead, lead), ((), ())), preferred_element_type=F32)]
    ppermute x11 -> x5, waiting for transfers between devices: 11 us -> 0.33 us  [from_core(): return lax.ppermute(a, 'core', SWAP)]
    convert_element_type x1 -> x0, local copies, waits for them, and re-layouts: 10.4 us -> none  [column_core(): g = g.astype(BF16).reshape(2, 2, seqs, -1, g.shape[1])]
    ppermute x8 -> x7, waiting for transfers between devices: 28.3 us -> 33.8 us  [from_y(): return lax.ppermute(a, 'y', SWAP)]
  transfers between devices with their start and end apart: 39 -> 30, of which waited for: 17 -> 8; matrix products, arithmetic and copies ran while one was open for 19% -> 11% of each run, Pallas kernels for 65% -> 71%
where the time goes in v5:
time: 937 us; the launch traced here: 927 us
  Pallas kernels  684 us (73%)
  local copies, waits for them, and re-layouts  81.9 us (9%)
  waiting for transfers between devices  68 us (7%)
  other arithmetic  34.2 us (4%)
  starting transfers between devices  23 us (2%)
  matrix products  20 us (2%)
  between operations  15.5 us (2%)
    pallas_call x11, Pallas kernels, run_kernel(): pl.pallas_call(kernel, name=name, out_shape=[jax.ShapeDtypeStruct(*output...  684 us
    ppermute x7, waiting for transfers between devices, from_y(): return lax.ppermute(a, 'y', SWAP)  33.8 us
    all_gather x1, waiting for transfers between devices, column_block(): full = lax.all_gather(column_own(w), ('core', 'z'), axis=1, tiled=True)  21.3 us
  transfers between devices with their start and end apart: 30, of which 8 were waited for; matrix products, arithmetic and copies ran while one was open for 11% of the time, Pallas kernels for 71%

profile of v5, /device:TPU:0, one launch (start us, length us, event | category | flops | bytes accessed | tf_op | source)
XLA Modules:
  0.0 927.0 jit_solution(14228708074681523616)
XLA Ops:
  8.0 2.4 reshape.604
  11.7 3.1 collective-permute-start
  15.3 4.9 collective-permute-done
  24.0 1.7 collective-permute-start.1
  26.3 5.8 collective-permute-done.1
  35.0 2.0 reshape_broadcast_in_dim.3
  37.0 1.8 constant_dynamic-slice_fusion.10
  38.9 1.8 collective-permute-start.6
  40.8 10.7 %collective-permute-done.6 = bf16[96,2240]{1,0:T(8,128)(2,1)S(1)} collective-permute-done((bf16[96,2240]{1,0:T(8,128)(2,1)S(1)}, bf16[96,2240]{1,0:T(8,128)(2,1)S(1)}, u32[]{:S(2)}, u32[]{:S(2)}) %collective-permute-start.6) | collective-permute-done | bytes 430112 | tf_op jit(solution)/shard_map/ppermute | solution.py:519
  56.1 2.5 pad.23.refs_0_.refs_2_.refs_7_
  70.6 21.3 %all-gather.6.cloned.1.call-done = bf16[2,768,1152]{2,1,0:T(8,128)(2,1)} async-done(((bf16[2,96,1152]{2,1,0:T(8,128)(2,1)}), bf16[2,768,1152]{2,1,0:T(8,128)(2,1)}) %all-gather.6.cloned.1.call-update) | async-done | bytes 3538960 | tf_op jit(solution)/shard_map/all_gather | solution.py:568
  92.5 100.6 %self_in.1 = (bf16[4,208,1536]{2,1,0:T(8,128)(2,1)}, f32[4,208,768]{2,1,0:T(8,128)}, f32[4,8,256]{2,1,0:T(8,128)}, bf16[4,208,1152]{2,1,0:T(8,128)(2,1)}, bf16[4...) custom-call(f32[208,1536]{1,0:T(8,128)} %pad.23.refs_0_.refs_2_.refs_7_, f32[8,1536]{1,0:T(8,128)} %get-tuple-element.230.refs_1_, ...), custom_call_target="tpu_custom_call" | custom-call | flops 80499998720 | bytes 252000000 | tf_op jit(solution)/shard_map/self_in/pallas_call | solution.py:344
  193.1 2.7 constant_dynamic-slice_fusion.5.refs_4_
  195.8 4.4 fusion.34
  200.6 5.1 multiply_reduce_fusion
  205.8 1.8 collective-permute-start.5
  209.9 85.6 %self_attend.1 = (bf16[4,208,384]{2,1,0:T(8,128)(2,1)}, f32[208,1536]{1,0:T(8,128)}, f32[208,1536]{1,0:T(8,128)}, bf16[4,208,1536]{2,1,0:T(8,128)(2,1)}, bf16[4,...) custom-call(bf16[4,208,1152]{2,1,0:T(8,128)(2,1)} %get-tuple-element.67.refs_0_, ...), custom_call_target="tpu_custom_call" | custom-call | flops 92000002048 | bytes 288000000 | tf_op jit(solution)/shard_map/self_attend/pallas_call | solution.py:344
  295.5 6.4 add_convert_fusion
  302.7 2.2 multiply_convert_fusion
  304.9 1.9 pad_maximum_fusion.1.refs_2_.refs_3_
  306.8 3.0 slice.472.refs_3_.refs_7_
  310.4 58.9 %cross_attend.1 = (bf16[4,208,384]{2,1,0:T(8,128)(2,1)}, f32[208,1536]{1,0:T(8,128)}, bf16[4,208,1536]{2,1,0:T(8,128)(2,1)}, bf16[4,208,2240]{2,1,0:T(8,128)(2,1)}, f32[4,208,2240]{2,1,0:T(8,128)}) custom-call(f32[4,208,384]{2,1,0:T(8,128)} %get-tuple-element.68.refs_0_, f32[8,384]{1,0:T(8,128)} %pad.24.refs_4_.refs_1_.refs_2_, ...), custom_call_target="tpu_custom_call" | custom-call | flops 69000003584 | bytes 216000000 | tf_op jit(solution)/shard_map/cross_attend/pallas_call | solution.py:344
  369.3 16.1 %down_sums.1 = bf16[2240,768]{1,0:T(8,128)(2,1)} custom-call(bf16[4,208,2240]{2,1,0:T(8,128)(2,1)} %get-tuple-element.73.refs_0_.refs_11_, bf16[4,208,1536]{2,1,0:T(8,128)(2,1)} %get-tuple-element.74.refs_1_.refs_0_), custom_call_target="tpu_custom_call" | custom-call | flops 16099999744 | bytes 50400000 | tf_op jit(solution)/shard_map/down_sums/pallas_call | solution.py:344
  385.6 73.9 %ffn_back.1 = (bf16[4,208,2240]{2,1,0:T(8,128)(2,1)}, f32[208,1536]{1,0:T(8,128)}, bf16[4,208,1536]{2,1,0:T(8,128)(2,1)}, bf16[4,208,384]{2,1,0:T(8,128)(2,1)}, f32[3,8,1536]{2,1,0:T(8,128)}) custom-call(bf16[4,208,1536]{2,1,0:T(8,128)(2,1)} %get-tuple-element.74.refs_1_.refs_0_, bf16[2,2240,768]{2,1,0:T(8,128)(2,1)} %bitcast.228, ...), custom_call_target="tpu_custom_call" | custom-call | flops 82800001024 | bytes 259200000 | tf_op jit(solution)/shard_map/ffn_back/pallas_call | solution.py:344
  461.1 16.6 %up_sums.1 = bf16[4,2,96,2240]{3,2,1,0:T(8,128)(2,1)} custom-call(bf16[4,208,1536]{2,1,0:T(8,128)(2,1)} %get-tuple-element.78.refs_0_, bf16[4,208,2240]{2,1,0:T(8,128)(2,1)} %get-tuple-element.109.refs_1_), custom_call_target="tpu_custom_call" | custom-call | flops 16099999744 | bytes 50400000 | tf_op jit(solution)/shard_map/up_sums/pallas_call | solution.py:344
  478.1 101.3 %cross_back.1 = (bf16[4,208,384]{2,1,0:T(8,128)(2,1)}, bf16[4,512,768]{2,1,0:T(8,128)(2,1)}, f32[8,384]{1,0:T(8,128)}, f32[208,1536]{1,0:T(8,128)}, bf16[4,208,1...) custom-call(f32[4,208,384]{2,1,0:T(8,128)} %get-tuple-element.68.refs_0_, ...), custom_call_target="tpu_custom_call" | custom-call | flops 92000002048 | bytes 288000000 | tf_op jit(solution)/shard_map/cross_back/pallas_call | solution.py:344
  579.5 2.4 slice.391
  581.9 2.2 copy.79
  584.1 8.7 output_sums.1
  592.8 4.1 pad_maximum_fusion
  597.0 142.3 %self_back.1 = (bf16[4,208,1152]{2,1,0:T(8,128)(2,1)}, f32[2,8,384]{2,1,0:T(8,128)}, f32[208,1536]{1,0:T(8,128)}, f32[2,8,1536]{2,1,0:T(8,128)}, f32[96,8960]{1,0:T(8,128)}, /*index=5*/f32[560,1536]{1,0:T(8,128)}) custom-call(bf16[4,208,1152]{2,1,0:T(8,128)(2,1)} %get-tuple-element.67.refs_0_, bf16[4,208,384]{2,1,0:T(8,128)(2,1)} %get-tuple-element.84.refs_1_, ...), custom_call_target="tpu_custom_call" | custom-call | flops 138000007168 | bytes 432000000 | tf_op jit(solution)/shard_map/self_back/pallas_call | solution.py:344
  739.3 2.5 slice.392
  748.2 2.7 convert_reduce_fusion
  755.2 16.8 %last_sums.1 = bf16[4,2,96,2304]{3,2,1,0:T(8,128)(2,1)} custom-call(bf16[4,208,1536]{2,1,0:T(8,128)(2,1)} %get-tuple-element.110.refs_0_, bf16[4,208,1152]{2,1,0:T(8,128)(2,1)} %tied.1.refs_1_, bf16[4,208,1536]{2,1,0:T(8,128)(2,1)} %get-tuple-element.111.refs_2_, bf16[4,208,384]{2,1,0:T(8,128)(2,1)} %get-tuple-element.105.refs_3_, ...), custom_call_target="tpu_custom_call" | custom-call | flops 18400000000 | bytes 57600000 | tf_op jit(solution)/shard_map/last_sums/pallas_call | solution.py:344
  778.8 63.5 %small_sums.1 = (f32[32,1536]{1,0:T(8,128)}, f32[32,1536]{1,0:T(8,128)}) custom-call(f32[32,1536]{1,0:T(8,128)} %pad.28.refs_0_), custom_call_target="tpu_custom_call" | custom-call | flops 28750000128 | bytes 90000000 | tf_op jit(solution)/shard_map/small_sums/pallas_call | solution.py:344
  851.7 1.9 collective-permute-start.14
  855.3 1.7 collective-permute-start.13
  864.0 2.0 collective-permute-start.12
  867.2 9.1 collective-permute-done.15
  879.9 3.2 collective-permute-done.12
  883.2 2.6 convert_add_fusion
  888.2 11.6 %collective-permute-done.16 = bf16[2,96,2304]{2,1,0:T(8,128)(2,1)} collective-permute-done((bf16[2,96,2304]{2,1,0:T(8,128)(2,1)}, bf16[2,96,2304]{2,1,0:T(8,128)(2,1)}, u32[]{:S(2)}, u32[]{:S(2)}) %collective-permute-start.16) | collective-permute-done | bytes 884768 | tf_op jit(solution)/shard_map/ppermute | solution.py:522
  899.8 2.0 stack_reshape.11
  902.8 4.5 copy.82
  907.3 4.5 reshape.629
  911.8 2.0 fusion.35
  915.1 1.8 copy.121
  918.3 1.8 copy.122
  (290 shorter events, 79.1 us)
Async XLA Ops:
  7.2 48.3 %copy-start = (f32[4,1536]{1,0:T(4,128)S(1)}, f32[4,1536]{1,0:T(4,128)}, u32[]{:S(2)}) copy-start(f32[4,1536]{1,0:T(4,128)} %param.33) | copy-start | bytes 73732
  7.2 63.4 %all-gather.8.cloned.1.call-start = ((), (), s32[]{:S(2)}) async-start(), calls=%async_computation.5 | async-start | bytes 1966080 | tf_op jit(solution)/shard_map/all_gather | solution.py:634
  7.9 84.0 %all-gather.6.cloned.1.call-start = ((), (), s32[]{:S(2)}) async-start(), calls=%async_computation.4 | async-start | bytes 3981312 | tf_op jit(solution)/shard_map/all_gather | solution.py:568
  11.3 9.8 %copy-start.18 = (bf16[96,1536]{1,0:T(8,128)(2,1)S(1)}, bf16[96,1536]{1,0:T(8,128)(2,1)}, u32[]{:S(2)}) copy-start(bf16[96,1536]{1,0:T(8,128)(2,1)} %param.27) | copy-start | bytes 884740
  11.6 10.1 %copy-start.16 = (bf16[96,3,1536]{2,0,1:T(8,128)(2,1)S(1)}, bf16[96,3,1536]{2,0,1:T(8,128)(2,1)}, u32[]{:S(2)}) copy-start(bf16[96,3,1536]{2,0,1:T(8,128)(2,1)} %param.28) | copy-start | bytes 2654212
  11.7 8.5 collective-permute-start
  21.0 174.7 %all-gather.10.cloned.1.call-start = ((), (), s32[]{:S(2)}) async-start(), calls=%async_computation.6 | async-start | bytes 5308416 | tf_op jit(solution)/shard_map/all_gather | solution.py:591
  21.8 4.5 collective-permute-start.2
  24.0 8.2 collective-permute-start.1
  26.0 8.3 copy-start.20
  26.2 8.8 copy-start.13
  34.2 272.5 %all-gather.12.cloned.1.call-start = ((), (), s32[]{:S(2)}) async-start(), calls=%async_computation.7 | async-start | bytes 9289728 | tf_op jit(solution)/shard_map/all_gather | solution.py:595
  35.0 5.7 collective-permute-start.7
  38.9 12.6 %collective-permute-start.6 = (bf16[96,2240]{1,0:T(8,128)(2,1)S(1)}, bf16[96,2240]{1,0:T(8,128)(2,1)S(1)}, u32[]{:S(2)}, u32[]{:S(2)}) collective-permute-start(bf16[96,2240]{1,0:T(8,128)(2,1)S(1)} %bitcast.206), channel_id=1, source_target_pairs={{0,8},{8,0},{1,9},{9,1},{2,10},{10,2},{3,11},{11,3},{4,12},{12,4},... | collective-permute-start | bytes 1290248 | tf_op jit(solution)/shard_map/ppermute | solution.py:519
  52.8 332.7 %all-gather.14.cloned.1.call-start = ((), (), s32[]{:S(2)}) async-start(), calls=%async_computation.8 | async-start | bytes 7741440 | tf_op jit(solution)/shard_map/all_gather | solution.py:578
  54.5 14.5 %collective-permute-start.8 = (bf16[560,768]{1,0:T(8,128)(2,1)}, bf16[560,768]{1,0:T(8,128)(2,1)}, u32[]{:S(2)}, u32[]{:S(2)}) collective-permute-start(bf16[560,768]{1,0:T(8,128)(2,1)} %constant_dynamic-slice_fusion.7), channel_id=1, source_target_pairs={{0,4},{4,0},{1,5},{5,1},{2,6},{6,2},{3,7},{7,3},{8,12},{12,8},{9,1... | collective-permute-start | bytes 2580488 | tf_op jit(solution)/shard_map/ppermute | solution.py:528
  59.6 7.4 copy-start.45
  59.6 7.4 copy-start.46
  59.6 7.4 copy-start.47
  59.6 7.4 copy-start.48
  70.1 408.1 %reduce-scatter.5.cloned.1.call-start = ((), (), s32[]{:S(2)}) async-start(), calls=%async_computation.9 | async-start | bytes 4300800 | tf_op jit(solution)/shard_map/reduce_scatter | solution.py:601
  200.1 5.7 copy-start.4
  200.1 95.4 %copy-start.2 = (bf16[2,768,384]{2,1,0:T(8,128)(2,1)}, bf16[2,768,384]{2,1,0:T(8,128)(2,1)S(1)}, u32[]{:S(2)}) copy-start(bf16[2,768,384]{2,1,0:T(8,128)(2,1)S(1)} %get-tuple-element.186) | copy-start | bytes 3538948
  205.8 96.2 %collective-permute-start.5 = (f32[4,512]{1,0:T(4,128)S(1)}, f32[4,512]{1,0:T(4,128)S(1)}, u32[]{:S(2)}, u32[]{:S(2)}) collective-permute-start(f32[4,512]{1,0:T(4,128)S(1)} %get-tuple-element.269), channel_id=1, source_target_pairs={{0,24},{8,16},{16,8},{24,0},{1,25},{9,17},{17,9},{25,1},{2,26},{10... | collective-permute-start | bytes 24584 | tf_op jit(solution)/shard_map/ppermute | solution.py:525
  207.6 94.4 %collective-permute-start.4 = (f32[4,512]{1,0:T(4,128)S(1)}, f32[4,512]{1,0:T(4,128)S(1)}, u32[]{:S(2)}, u32[]{:S(2)}) collective-permute-start(f32[4,512]{1,0:T(4,128)S(1)} %get-tuple-element.269), channel_id=1, source_target_pairs={{0,16},{16,0},{1,17},{17,1},{2,18},{18,2},{3,19},{19,3},{4,20},{20... | collective-permute-start | bytes 24584 | tf_op jit(solution)/shard_map/ppermute | solution.py:522
  208.8 93.3 %collective-permute-start.3 = (f32[4,512]{1,0:T(4,128)S(1)}, f32[4,512]{1,0:T(4,128)S(1)}, u32[]{:S(2)}, u32[]{:S(2)}) collective-permute-start(f32[4,512]{1,0:T(4,128)S(1)} %get-tuple-element.269), channel_id=1, source_target_pairs={{0,8},{8,0},{1,9},{9,1},{2,10},{10,2},{3,11},{11,3},{4,12},{12,4},... | collective-permute-start | bytes 24584 | tf_op jit(solution)/shard_map/ppermute | solution.py:519
  209.9 85.6 %copy-start.44 = (f32[384]{0:T(512)S(1)}, f32[384]{0:T(512)}, u32[]{:S(2)}) copy-start(f32[384]{0:T(512)} %get-tuple-element.176) | copy-start | bytes 4612
  295.5 7.2 copy-start.9
  295.5 7.2 copy-start.32
  385.5 196.4 %reduce-scatter.7.cloned.1.call-start = ((), (), s32[]{:S(2)}) async-start(), calls=%async_computation.10 | async-start | bytes 4423680 | tf_op jit(solution)/shard_map/reduce_scatter | solution.py:601
  460.4 17.2 %copy-start.26 = (f32[3,1536]{1,0:T(4,128)}, f32[3,1536]{1,0:T(4,128)S(1)}, u32[]{:S(2)}) copy-start(f32[3,1536]{1,0:T(4,128)S(1)} %reduce_sum.128) | copy-start | bytes 55300
  477.7 264.4 %reduce-scatter.9.cloned.1.call-start = ((), (), s32[]{:S(2)}) async-start(), calls=%async_computation.11 | async-start | bytes 5406720 | tf_op jit(solution)/shard_map/reduce_scatter | solution.py:1036
  596.9 265.1 %reduce-scatter.11.cloned.1.call-start = ((), (), s32[]{:S(2)}) async-start(), calls=%async_computation.12 | async-start | bytes 4423680 | tf_op jit(solution)/shard_map/reduce_scatter | solution.py:601
  744.6 8.1 collective-permute-start.11
  746.2 6.6 collective-permute-start.10
  746.7 6.2 collective-permute-start.9
  774.0 90.0 %collective-permute-start.19 = (bf16[96,768]{1,0:T(8,128)(2,1)}, bf16[96,768]{1,0:T(8,128)(2,1)}, u32[]{:S(2)}, u32[]{:S(2)}) collective-permute-start(bf16[96,768]{1,0:T(8,128)(2,1)} %get-tuple-element.200), channel_id=1, source_target_pairs={{0,16},{16,0},{1,17},{17,1},{2,18},{18,2},{3,19},{19,3},{4,20},{20... | collective-permute-start | bytes 442376 | tf_op jit(solution)/shard_map/ppermute | solution.py:522
  775.6 90.4 %collective-permute-start.17 = (bf16[96,768]{1,0:T(8,128)(2,1)}, bf16[96,768]{1,0:T(8,128)(2,1)}, u32[]{:S(2)}, u32[]{:S(2)}) collective-permute-start(bf16[96,768]{1,0:T(8,128)(2,1)} %get-tuple-element.201), channel_id=1, source_target_pairs={{0,16},{16,0},{1,17},{17,1},{2,18},{18,2},{3,19},{19,3},{4,20},{20... | collective-permute-start | bytes 442376 | tf_op jit(solution)/shard_map/ppermute | solution.py:522
  778.8 71.1 %copy-start.5 = (bf16[2,768,384]{2,1,0:T(8,128)(2,1)S(1)}, bf16[2,768,384]{2,1,0:T(8,128)(2,1)}, u32[]{:S(2)}) copy-start(bf16[2,768,384]{2,1,0:T(8,128)(2,1)} %copy-done.4) | copy-start | bytes 3538948
  842.4 8.1 copy-start.3
  851.7 28.2 %collective-permute-start.14 = (bf16[128,1536]{1,0:T(8,128)(2,1)}, bf16[128,1536]{1,0:T(8,128)(2,1)}, u32[]{:S(2)}, u32[]{:S(2)}) collective-permute-start(bf16[128,1536]{1,0:T(8,128)(2,1)} %fusion.2), channel_id=1, source_target_pairs={{0,24},{8,16},{16,8},{24,0},{1,25},{9,17},{17,9},{25,1},{2,26},{10... | collective-permute-start | bytes 1179656 | tf_op jit(solution)/shard_map/ppermute | solution.py:525
  855.3 24.6 %collective-permute-start.13 = (bf16[128,1536]{1,0:T(8,128)(2,1)}, bf16[128,1536]{1,0:T(8,128)(2,1)}, u32[]{:S(2)}, u32[]{:S(2)}) collective-permute-start(bf16[128,1536]{1,0:T(8,128)(2,1)} %fusion.1), channel_id=1, source_target_pairs={{0,16},{16,0},{1,17},{17,1},{2,18},{18,2},{3,19},{19,3},{4,20},{20... | collective-permute-start | bytes 1179656 | tf_op jit(solution)/shard_map/ppermute | solution.py:522
  863.3 13.1 %collective-permute-start.15 = (bf16[96,2304]{1,0:T(8,128)(2,1)S(1)}, bf16[96,2304]{1,0:T(8,128)(2,1)S(1)}, u32[]{:S(2)}, u32[]{:S(2)}) collective-permute-start(bf16[96,2304]{1,0:T(8,128)(2,1)S(1)} %get-tuple-element.203), channel_id=1, source_target_pairs={{0,8},{8,0},{1,9},{9,1},{2,10},{10,2},{3,11},{11,3},{4,12},{12,4},... | collective-permute-start | bytes 1327112 | tf_op jit(solution)/shard_map/ppermute | solution.py:519
  864.0 19.2 %collective-permute-start.12 = (bf16[128,1536]{1,0:T(8,128)(2,1)S(1)}, bf16[128,1536]{1,0:T(8,128)(2,1)S(1)}, u32[]{:S(2)}, u32[]{:S(2)}) collective-permute-start(bf16[128,1536]{1,0:T(8,128)(2,1)S(1)} %fusion), channel_id=1, source_target_pairs={{0,8},{8,0},{1,9},{9,1},{2,10},{10,2},{3,11},{11,3},{4,12},{12,4},... | collective-permute-start | bytes 1179656 | tf_op jit(solution)/shard_map/ppermute | solution.py:519
  867.2 11.8 %collective-permute-start.20 = (bf16[96,768]{1,0:T(8,128)(2,1)S(1)}, bf16[96,768]{1,0:T(8,128)(2,1)S(1)}, u32[]{:S(2)}, u32[]{:S(2)}) collective-permute-start(bf16[96,768]{1,0:T(8,128)(2,1)S(1)} %get-tuple-element.194), channel_id=1, source_target_pairs={{0,4},{4,0},{1,5},{5,1},{2,6},{6,2},{3,7},{7,3},{8,12},{12,8},{9,1... | collective-permute-start | bytes 442376 | tf_op jit(solution)/shard_map/ppermute | solution.py:528
  876.4 1.4 collective-permute-start.18
  876.4 6.8 copy-start.10
  877.7 22.1 %collective-permute-start.16 = (bf16[2,96,2304]{2,1,0:T(8,128)(2,1)}, bf16[2,96,2304]{2,1,0:T(8,128)(2,1)}, u32[]{:S(2)}, u32[]{:S(2)}) collective-permute-start(bf16[2,96,2304]{2,1,0:T(8,128)(2,1)} %maximum_select_fusion.3), channel_id=1, source_target_pairs={{0,16},{16,0},{1,17},{17,1},{2,18},{18,2},{3,19},{19,3},{4,20},{20... | collective-permute-start | bytes 2654216 | tf_op jit(solution)/shard_map/ppermute | solution.py:522
  (32 other events, 101.9 us)
Sparse Core Ops, SparseCore 0:
  9.6 39.7 all-gather.7
  51.5 40.3 all-gather.5
  94.1 85.9 all-gather.9
  181.6 92.7 all-gather.11
  275.8 67.9 all-gather.13
  385.6 70.0 reduce-scatter.4
  477.8 72.2 reduce-scatter.6
  597.0 117.4 reduce-scatter.8
  772.2 85.0 reduce-scatter.10
